TPU v7x, 512 devices: a whole 4x4x16 slice. The times are simulated.
512 devices in a mesh: rows: 16 (over z), cols: 8 (over y, core), layers: 4 (over x).
Axes of the slice: x: 4, y: 4, z: 16, core: 2. Of those that a mesh axis runs over, the one named last changes fastest.
Arguments:
- bottom_known_vector: float32 [768, 128, 256], P(('rows', 'layers')), may hold values from -6 to 6
- bottom_pivot_reciprocal: float32 [768, 128, 128], P(('rows', 'layers'), 'cols'), as said below
- leaf_blocks: float32 [768, 8, 128, 128], P(('rows', 'layers'), 'cols'), may hold values from -0.02734375 to 0.02734375
- leaf_target: int32 [768, 8], P(('rows', 'layers'), 'cols'), may hold values from 0 to 15, as said below
- top_rhs: float32 [16, 128, 256], P('rows'), may hold values from -6 to 6
- top_inv: float32 [16, 128, 128], P('rows'), as said below
- top_sub: float32 [16, 128, 128], P('rows'), may hold values from -0.4375 to 0.4375
Outputs:
- leaf_solution: float32 [768, 128, 256], P(('rows', 'layers'), 'cols')
- top_solution: float32 [16, 128, 256], P('rows')
Inputs may be any that keep to these rules, and one draw needn't show every extreme that they name: `leaf_target`: each leaf names 8 different top supernodes. `bottom_pivot_reciprocal`: each block is its diagonal times a factor of 0.7 to 1.3 plus a full-rank off-diagonal part. `top_inv`: each block is its diagonal times a factor of 0.7 to 1.3 plus a full-rank off-diagonal part.
All inputs are finite; a program needn't handle non-finite values.
Results may differ from a plain program's by a relative error of at most 0.00028.
Values sent between devices are 32-bit elements; how exact they have to be, the bound alone decides.
No kernel may reach another device: no remote copies, remote signals or barrier semaphores. Data moves between devices by JAX's collectives and lax.ppermute only.
A program may use at most 64 MiB of HBM per device.

v0:
```python
import jax
import jax.numpy as jnp
from jax import lax
from jax.sharding import PartitionSpec as P


def from_behind(x, axis, by):
    peers = lax.axis_size(axis)
    pairs = [(i, i + by) for i in range(peers) if 0 <= i + by < peers]
    return lax.ppermute(x, axis, pairs)


def on_device(
    bottom_known_vector,
    bottom_pivot_reciprocal,
    leaf_blocks,
    leaf_target,
    top_rhs,
    top_inv,
    top_sub,
):
    exact_arithmetic_mode = lax.Precision.HIGHEST
    row_count = lax.axis_size("rows")
    distribute_equations = bottom_pivot_reciprocal.shape[1]
    forward_portion = jnp.einsum(
        "bxr,brl->bxl",
        bottom_pivot_reciprocal,
        bottom_known_vector,
        precision=exact_arithmetic_mode,
    )
    leaf_forward = lax.all_gather(forward_portion, "cols", axis=1, tiled=True)
    inverse_full = lax.all_gather(bottom_pivot_reciprocal, "cols", axis=1, tiled=True)
    blocks = leaf_blocks[:, 0]
    targets = leaf_target[:, 0]
    contrib = jnp.einsum("lab,lbr->lar", blocks, leaf_forward, precision=exact_arithmetic_mode)
    top_ids = jnp.arange(row_count, dtype=jnp.int32)
    picker = (targets[:, None] == top_ids[None, :]).astype(jnp.float32)
    top_rows = jnp.arange(1 * lax.axis_size("rows"), dtype=jnp.int32)
    selector = (targets[:, None] == top_rows[None, :]).astype(jnp.float32)
    own_sums = lax.psum_scatter(
        jnp.einsum("lt,lar->tar", selector, contrib, precision=exact_arithmetic_mode),
        "rows",
        scatter_dimension=0,
        tiled=True,
    )
    carried = lax.psum(own_sums, ("cols", "layers"))
    diag_inv = top_inv[0]
    coupling = top_sub[0]
    local_term = jnp.dot(diag_inv, top_rhs[0] - carried[0], precision=exact_arithmetic_mode)
    forward_map = -jnp.dot(diag_inv, coupling, precision=exact_arithmetic_mode)

    def forward_turn(turn_index, current):
        previous = from_behind(current, "rows", 1)
        return local_term + jnp.dot(forward_map, previous, precision=exact_arithmetic_mode)

    top_forward = lax.fori_loop(0, row_count - 1, forward_turn, local_term)
    coupling_next = from_behind(coupling, "rows", -1)
    back_term = jnp.dot(diag_inv.T, top_forward, precision=exact_arithmetic_mode)
    back_map = -jnp.dot(diag_inv.T, coupling_next.T, precision=exact_arithmetic_mode)

    def upward_sweep_pass(turn_index, current):
        following = from_behind(current, "rows", -1)
        return back_term + jnp.dot(back_map, following, precision=exact_arithmetic_mode)

    top_own = lax.fori_loop(0, row_count - 1, upward_sweep_pass, back_term)
    top_part = top_own[None]
    top_all = lax.all_gather(top_part, "rows", axis=0, tiled=True)
    gathered = jnp.einsum("lt,tar->lar", picker, top_all, precision=exact_arithmetic_mode)
    back_part = jnp.einsum("lab,lar->lbr", blocks, gathered, precision=exact_arithmetic_mode)
    back_sum = lax.psum(back_part, "cols")
    leftover_rows = leaf_forward - back_sum
    column_list = lax.dynamic_slice_in_dim(
        inverse_full, lax.axis_index("cols") * distribute_equations, distribute_equations, 2
    )
    leaf_portion = jnp.einsum(
        "edv,edg->evg", column_list, leftover_rows, precision=exact_arithmetic_mode
    )
    return (leaf_portion, top_part)


def solution(mesh):
    in_specs = (
        P(("rows", "layers"), None, None),
        P(("rows", "layers"), "cols", None),
        P(("rows", "layers"), "cols", None, None),
        P(("rows", "layers"), "cols"),
        P("rows", None, None),
        P("rows", None, None),
        P("rows", None, None),
    )
    out_specs = (P(("rows", "layers"), "cols", None), P("rows", None, None))
    return jax.shard_map(
        on_device, mesh=mesh, in_specs=in_specs, out_specs=out_specs, check_vma=False
    )
```

profile of v0, /device:TPU:1, one launch (start us, length us, event | category | flops | bytes accessed | tf_op | source)
XLA Modules:
  0.0 689.4 jit_solution(13225634676516913542)
XLA Ops:
  11.1 37.9 %all-gather.4.cloned.1.call-done = f32[12,128,256]{2,1,0:T(8,128)} async-done(((f32[12,16,256]{2,1,0:T(8,128)}), f32[12,128,256]{2,1,0:T(8,128)}) %all-gather.4.cloned.1.call-update) | async-done | bytes 1572880 | tf_op jit(solution)/shard_map/all_gather | solution.py:31
  62.9 60.6 %reduce-scatter.2.cloned.1.call-done = f32[1,128,256]{2,1,0:T(8,128)} async-done(((f32[16,128,256]{2,1,0:T(8,128)}), f32[1,128,256]{2,1,0:T(8,128)}) %reduce-scatter.2.cloned.1.call-update) | async-done | bytes 131088 | tf_op jit(solution)/shard_map/reduce_scatter | solution.py:40
  123.9 141.6 %all-reduce.3.cloned.1.call-done = f32[1,128,256]{2,1,0:T(8,128)} async-done(((f32[1,128,256]{2,1,0:T(8,128)}), f32[1,128,256]{2,1,0:T(8,128)}) %all-reduce.3.cloned.1.call-update) | async-done | bytes 131088 | tf_op jit(solution)/shard_map/psum | solution.py:46
  266.7 105.0 %while.20 = (s32[]{:T(128)}, f32[128,256]{1,0:T(8,128)S(1)}, f32[128,128]{1,0:T(8,128)S(1)}, f32[128,256]{1,0:T(8,128)S(1)}, s32[]{:T(128)}) while((s32[]{:T(128)}, f32[128,256]{1,0:T(8,128)S(1)}, f32[128,128]{1,0:T(8,128)S(1)}, f32[128,256]{1,0:T(8,128)S(1)}, s32[]{:T(128)}) %tuple.37), condition=%wide.region_3.0_spmd, body=%wide.region_2.0_spmd.sunk | while | flops 50364416 | bytes 983141 | solution.py:56
  320.3 5.4 collective-permute-start
  342.0 5.3 collective-permute-start
  372.2 113.7 %while.21 = (s32[]{:T(128)}, f32[128,256]{1,0:T(8,128)S(1)}, f32[128,128]{1,0:T(8,128)S(1)}, f32[128,256]{1,0:T(8,128)S(1)}, s32[]{:T(128)}) while((s32[]{:T(128)}, f32[128,256]{1,0:T(8,128)S(1)}, f32[128,128]{1,0:T(8,128)S(1)}, f32[128,256]{1,0:T(8,128)S(1)}, s32[]{:T(128)}) %tuple.40), condition=%wide.region_5.0_spmd, body=%wide.region_4.0_spmd.sunk | while | flops 50364416 | bytes 983141 | solution.py:65
  373.6 6.3 collective-permute-done.1
  381.5 6.7 collective-permute-done.1
  389.8 6.1 collective-permute-done.1
  397.4 6.4 collective-permute-done.1
  405.4 5.6 collective-permute-done.1
  412.6 5.6 collective-permute-done.1
  419.8 5.6 collective-permute-done.1
  427.0 6.6 collective-permute-done.1
  435.2 7.5 %collective-permute-done.1 = f32[128,256]{1,0:T(8,128)S(1)} collective-permute-done((f32[128,256]{1,0:T(8,128)S(1)}, f32[128,256]{1,0:T(8,128)S(1)}, u32[]{:S(2)}, u32[]{:S(2)}) %collective-permute-start.1) | collective-permute-done | bytes 131104 | tf_op jit(solution)/shard_map/while/body/eval_jaxpr/ppermute | solution.py:10
  444.3 6.5 collective-permute-done.1
  458.7 5.3 collective-permute-done.1
  465.6 5.6 collective-permute-done.1
  472.8 5.6 collective-permute-done.1
  480.0 5.6 collective-permute-done.1
  486.8 100.5 %all-gather.6.cloned.1.call-done = f32[2048,256]{1,0:T(8,128)} async-done(((f32[128,256]{1,0:T(8,128)}), f32[2048,256]{1,0:T(8,128)}) %all-gather.6.cloned.1.call-update) | async-done | bytes 2097168 | tf_op jit(solution)/shard_map/all_gather | solution.py:67
  594.9 24.5 %all_gather.9 = f32[12,128,128]{2,1,0:T(8,128)} all-gather(f32[12,16,128]{2,1,0:T(8,128)S(1)} %copy-done.5), channel_id=1, replica_groups=mesh['rows'=16,'cols'=8,'layers'=4] {'cols'}, dimensions={1}, use_global_device_ids=true | all-gather | bytes 884736 | tf_op jit(solution)/shard_map/all_gather | solution.py:32
  619.5 59.4 %all-reduce.5.cloned.1.call-done = f32[12,128,256]{2,1,0:T(8,128)} async-done(((f32[12,128,256]{2,1,0:T(8,128)}), f32[12,128,256]{2,1,0:T(8,128)}) %all-reduce.5.cloned.1.call-update) | async-done | bytes 1572880 | tf_op jit(solution)/shard_map/psum | solution.py:70
  (119 shorter events, 154.2 us)
Async XLA Ops:
  7.2 41.8 %all-gather.4.cloned.1.call-start = ((), (), s32[]{:S(2)}) async-start(), calls=%async_computation.1 | async-start | bytes 1769472 | tf_op jit(solution)/shard_map/all_gather | solution.py:31
  11.0 112.5 %reduce-scatter.2.cloned.1.call-start = ((), (), s32[]{:S(2)}) async-start(), calls=%async_computation.2 | async-start | bytes 2228224 | tf_op jit(solution)/shard_map/reduce_scatter | solution.py:40
  60.6 204.9 %all-reduce.3.cloned.1.call-start = ((), (), s32[]{:S(2)}) async-start(), calls=%async_computation.3 | async-start | bytes 262144 | tf_op jit(solution)/shard_map/psum | solution.py:46
  61.4 62.2 %collective-permute-start.2 = (f32[128,128]{1,0:T(8,128)S(1)}, f32[128,128]{1,0:T(8,128)S(1)}, u32[]{:S(2)}, u32[]{:S(2)}) collective-permute-start(f32[128,128]{1,0:T(8,128)S(1)} %bitcast.55), channel_id=1, source_target_pairs={{32,0},{64,32},{96,64},{128,96},{160,128},{192,160},{224,192},{256... | collective-permute-start | bytes 196616 | tf_op jit(solution)/shard_map/ppermute | solution.py:10
  123.6 463.7 %all-gather.6.cloned.1.call-start = ((), (), s32[]{:S(2)}) async-start(), calls=%async_computation.5 | async-start | bytes 2228224 | tf_op jit(solution)/shard_map/all_gather | solution.py:67
  297.1 6.9 %collective-permute-start = (f32[128,256]{1,0:T(8,128)S(1)}, f32[128,256]{1,0:T(8,128)S(1)}, u32[]{:S(2)}, u32[]{:S(2)}) collective-permute-start(f32[128,256]{1,0:T(8,128)S(1)} %get-tuple-element.128), channel_id=1, source_target_pairs={{0,32},{32,64},{64,96},{96,128},{128,160},{160,192},{192,224},{224... | collective-permute-start | bytes 393224 | tf_op jit(solution)/shard_map/while/body/eval_jaxpr/ppermute | solution.py:10
  304.4 7.0 %collective-permute-start = (f32[128,256]{1,0:T(8,128)S(1)}, f32[128,256]{1,0:T(8,128)S(1)}, u32[]{:S(2)}, u32[]{:S(2)}) collective-permute-start(f32[128,256]{1,0:T(8,128)S(1)} %get-tuple-element.128), channel_id=1, source_target_pairs={{0,32},{32,64},{64,96},{96,128},{128,160},{160,192},{192,224},{224... | collective-permute-start | bytes 393224 | tf_op jit(solution)/shard_map/while/body/eval_jaxpr/ppermute | solution.py:10
  311.6 8.4 %collective-permute-start = (f32[128,256]{1,0:T(8,128)S(1)}, f32[128,256]{1,0:T(8,128)S(1)}, u32[]{:S(2)}, u32[]{:S(2)}) collective-permute-start(f32[128,256]{1,0:T(8,128)S(1)} %get-tuple-element.128), channel_id=1, source_target_pairs={{0,32},{32,64},{64,96},{96,128},{128,160},{160,192},{192,224},{224... | collective-permute-start | bytes 393224 | tf_op jit(solution)/shard_map/while/body/eval_jaxpr/ppermute | solution.py:10
  320.3 7.7 %collective-permute-start = (f32[128,256]{1,0:T(8,128)S(1)}, f32[128,256]{1,0:T(8,128)S(1)}, u32[]{:S(2)}, u32[]{:S(2)}) collective-permute-start(f32[128,256]{1,0:T(8,128)S(1)} %get-tuple-element.128), channel_id=1, source_target_pairs={{0,32},{32,64},{64,96},{96,128},{128,160},{160,192},{192,224},{224... | collective-permute-start | bytes 393224 | tf_op jit(solution)/shard_map/while/body/eval_jaxpr/ppermute | solution.py:10
  342.0 7.3 %collective-permute-start = (f32[128,256]{1,0:T(8,128)S(1)}, f32[128,256]{1,0:T(8,128)S(1)}, u32[]{:S(2)}, u32[]{:S(2)}) collective-permute-start(f32[128,256]{1,0:T(8,128)S(1)} %get-tuple-element.128), channel_id=1, source_target_pairs={{0,32},{32,64},{64,96},{96,128},{128,160},{160,192},{192,224},{224... | collective-permute-start | bytes 393224 | tf_op jit(solution)/shard_map/while/body/eval_jaxpr/ppermute | solution.py:10
  356.7 6.9 %collective-permute-start = (f32[128,256]{1,0:T(8,128)S(1)}, f32[128,256]{1,0:T(8,128)S(1)}, u32[]{:S(2)}, u32[]{:S(2)}) collective-permute-start(f32[128,256]{1,0:T(8,128)S(1)} %get-tuple-element.128), channel_id=1, source_target_pairs={{0,32},{32,64},{64,96},{96,128},{128,160},{160,192},{192,224},{224... | collective-permute-start | bytes 393224 | tf_op jit(solution)/shard_map/while/body/eval_jaxpr/ppermute | solution.py:10
  363.9 7.5 %collective-permute-start = (f32[128,256]{1,0:T(8,128)S(1)}, f32[128,256]{1,0:T(8,128)S(1)}, u32[]{:S(2)}, u32[]{:S(2)}) collective-permute-start(f32[128,256]{1,0:T(8,128)S(1)} %get-tuple-element.128), channel_id=1, source_target_pairs={{0,32},{32,64},{64,96},{96,128},{128,160},{160,192},{192,224},{224... | collective-permute-start | bytes 393224 | tf_op jit(solution)/shard_map/while/body/eval_jaxpr/ppermute | solution.py:10
  372.3 7.6 %collective-permute-start.1 = (f32[128,256]{1,0:T(8,128)S(1)}, f32[128,256]{1,0:T(8,128)S(1)}, u32[]{:S(2)}, u32[]{:S(2)}) collective-permute-start(f32[128,256]{1,0:T(8,128)S(1)} %get-tuple-element.143), channel_id=1, source_target_pairs={{32,0},{64,32},{96,64},{128,96},{160,128},{192,160},{224,192},{256... | collective-permute-start | bytes 393224 | tf_op jit(solution)/shard_map/while/body/eval_jaxpr/ppermute | solution.py:10
  380.2 8.0 %collective-permute-start.1 = (f32[128,256]{1,0:T(8,128)S(1)}, f32[128,256]{1,0:T(8,128)S(1)}, u32[]{:S(2)}, u32[]{:S(2)}) collective-permute-start(f32[128,256]{1,0:T(8,128)S(1)} %get-tuple-element.143), channel_id=1, source_target_pairs={{32,0},{64,32},{96,64},{128,96},{160,128},{192,160},{224,192},{256... | collective-permute-start | bytes 393224 | tf_op jit(solution)/shard_map/while/body/eval_jaxpr/ppermute | solution.py:10
  388.5 7.4 %collective-permute-start.1 = (f32[128,256]{1,0:T(8,128)S(1)}, f32[128,256]{1,0:T(8,128)S(1)}, u32[]{:S(2)}, u32[]{:S(2)}) collective-permute-start(f32[128,256]{1,0:T(8,128)S(1)} %get-tuple-element.143), channel_id=1, source_target_pairs={{32,0},{64,32},{96,64},{128,96},{160,128},{192,160},{224,192},{256... | collective-permute-start | bytes 393224 | tf_op jit(solution)/shard_map/while/body/eval_jaxpr/ppermute | solution.py:10
  396.1 7.7 %collective-permute-start.1 = (f32[128,256]{1,0:T(8,128)S(1)}, f32[128,256]{1,0:T(8,128)S(1)}, u32[]{:S(2)}, u32[]{:S(2)}) collective-permute-start(f32[128,256]{1,0:T(8,128)S(1)} %get-tuple-element.143), channel_id=1, source_target_pairs={{32,0},{64,32},{96,64},{128,96},{160,128},{192,160},{224,192},{256... | collective-permute-start | bytes 393224 | tf_op jit(solution)/shard_map/while/body/eval_jaxpr/ppermute | solution.py:10
  411.3 6.9 %collective-permute-start.1 = (f32[128,256]{1,0:T(8,128)S(1)}, f32[128,256]{1,0:T(8,128)S(1)}, u32[]{:S(2)}, u32[]{:S(2)}) collective-permute-start(f32[128,256]{1,0:T(8,128)S(1)} %get-tuple-element.143), channel_id=1, source_target_pairs={{32,0},{64,32},{96,64},{128,96},{160,128},{192,160},{224,192},{256... | collective-permute-start | bytes 393224 | tf_op jit(solution)/shard_map/while/body/eval_jaxpr/ppermute | solution.py:10
  425.7 7.9 %collective-permute-start.1 = (f32[128,256]{1,0:T(8,128)S(1)}, f32[128,256]{1,0:T(8,128)S(1)}, u32[]{:S(2)}, u32[]{:S(2)}) collective-permute-start(f32[128,256]{1,0:T(8,128)S(1)} %get-tuple-element.143), channel_id=1, source_target_pairs={{32,0},{64,32},{96,64},{128,96},{160,128},{192,160},{224,192},{256... | collective-permute-start | bytes 393224 | tf_op jit(solution)/shard_map/while/body/eval_jaxpr/ppermute | solution.py:10
  433.9 8.8 %collective-permute-start.1 = (f32[128,256]{1,0:T(8,128)S(1)}, f32[128,256]{1,0:T(8,128)S(1)}, u32[]{:S(2)}, u32[]{:S(2)}) collective-permute-start(f32[128,256]{1,0:T(8,128)S(1)} %get-tuple-element.143), channel_id=1, source_target_pairs={{32,0},{64,32},{96,64},{128,96},{160,128},{192,160},{224,192},{256... | collective-permute-start | bytes 393224 | tf_op jit(solution)/shard_map/while/body/eval_jaxpr/ppermute | solution.py:10
  443.0 7.8 %collective-permute-start.1 = (f32[128,256]{1,0:T(8,128)S(1)}, f32[128,256]{1,0:T(8,128)S(1)}, u32[]{:S(2)}, u32[]{:S(2)}) collective-permute-start(f32[128,256]{1,0:T(8,128)S(1)} %get-tuple-element.143), channel_id=1, source_target_pairs={{32,0},{64,32},{96,64},{128,96},{160,128},{192,160},{224,192},{256... | collective-permute-start | bytes 393224 | tf_op jit(solution)/shard_map/while/body/eval_jaxpr/ppermute | solution.py:10
  464.3 6.9 %collective-permute-start.1 = (f32[128,256]{1,0:T(8,128)S(1)}, f32[128,256]{1,0:T(8,128)S(1)}, u32[]{:S(2)}, u32[]{:S(2)}) collective-permute-start(f32[128,256]{1,0:T(8,128)S(1)} %get-tuple-element.143), channel_id=1, source_target_pairs={{32,0},{64,32},{96,64},{128,96},{160,128},{192,160},{224,192},{256... | collective-permute-start | bytes 393224 | tf_op jit(solution)/shard_map/while/body/eval_jaxpr/ppermute | solution.py:10
  471.5 6.9 %collective-permute-start.1 = (f32[128,256]{1,0:T(8,128)S(1)}, f32[128,256]{1,0:T(8,128)S(1)}, u32[]{:S(2)}, u32[]{:S(2)}) collective-permute-start(f32[128,256]{1,0:T(8,128)S(1)} %get-tuple-element.143), channel_id=1, source_target_pairs={{32,0},{64,32},{96,64},{128,96},{160,128},{192,160},{224,192},{256... | collective-permute-start | bytes 393224 | tf_op jit(solution)/shard_map/while/body/eval_jaxpr/ppermute | solution.py:10
  478.7 6.9 %collective-permute-start.1 = (f32[128,256]{1,0:T(8,128)S(1)}, f32[128,256]{1,0:T(8,128)S(1)}, u32[]{:S(2)}, u32[]{:S(2)}) collective-permute-start(f32[128,256]{1,0:T(8,128)S(1)} %get-tuple-element.143), channel_id=1, source_target_pairs={{32,0},{64,32},{96,64},{128,96},{160,128},{192,160},{224,192},{256... | collective-permute-start | bytes 393224 | tf_op jit(solution)/shard_map/while/body/eval_jaxpr/ppermute | solution.py:10
  486.6 192.3 %all-reduce.5.cloned.1.call-start = ((), (), s32[]{:S(2)}) async-start(), calls=%async_computation.4 | async-start | bytes 3145728 | tf_op jit(solution)/shard_map/psum | solution.py:70
  (21 other events, 379.1 us)
Sparse Core Ops, SparseCore 0:
  11.2 37.7 all-gather.3
  60.7 62.7 reduce-scatter.1
  126.8 138.7 all-reduce.2
  486.7 100.5 all-gather.5
  595.1 83.7 all-reduce.4
where the time goes:
time: 691 us; the launch traced here: 689 us
  waiting for transfers between devices  521 us (75%)
  starting transfers between devices  90.6 us (13%)
  matrix products  31.1 us (5%)
  blocking collectives  24.5 us (4%)
  between operations  13.9 us (2%)
  local copies, waits for them, and re-layouts  7.36 us (1%)
    psum x1, waiting for transfers between devices, on_device(): carried = lax.psum(own_sums, ('cols', 'layers'))  142 us
    ppermute x31, waiting for transfers between devices, from_behind(): return lax.ppermute(x, axis, pairs)  121 us
    all_gather x1, waiting for transfers between devices, on_device(): top_all = lax.all_gather(top_part, 'rows', axis=0, tiled=True)  100 us
    ppermute x31, starting transfers between devices, from_behind(): return lax.ppermute(x, axis, pairs)  90.3 us
    reduce_scatter x1, waiting for transfers between devices, on_device(): lax.psum_scatter(jnp.einsum('lt,lar->tar', selector, contrib, precision=e...  60.6 us
    psum x1, waiting for transfers between devices, on_device(): back_sum = lax.psum(back_part, 'cols')  59.4 us
    all_gather x1, waiting for transfers between devices, on_device(): leaf_forward = lax.all_gather(forward_portion, 'cols', axis=1, tiled=True)  37.9 us
    all_gather x1, blocking collectives, on_device(): lax.all_gather(bottom_pivot_reciprocal, 'cols', axis=1, tiled=True)  24.5 us
  transfers between devices with their start and end apart: 36, of which 35 were waited for; matrix products, arithmetic and copies ran while one was open for 0% of the time, Pallas kernels for 0%

commit v1 on v0

v1 whole, which is shorter than its diff:
```python
import jax
import jax.numpy as jnp
from jax import lax
from jax.experimental import pallas as pl
from jax.experimental.pallas import tpu as pltpu
from jax.sharding import Mesh, PartitionSpec as P

F32 = jnp.float32
BF16 = jnp.bfloat16
ROWS = ("rhi", "rlo")
EXACT = lax.Precision.HIGHEST


def dot(a, b, ca=1, cb=0):
    return lax.dot_general(
        a, b, (((ca,), (cb,)), ((), ())), precision=EXACT, preferred_element_type=F32
    )


def split(x):
    high = x.astype(BF16)
    low = (x - high.astype(F32)).astype(BF16)
    return high, low


def split_dot(x, pair):
    n = x.shape[0]
    m = pair.shape[1] // 2
    rows = jnp.concatenate(split(x), axis=0)
    r = lax.dot_general(rows, pair, (((1,), (0,)), ((), ())), preferred_element_type=F32)
    return (r[:n, :m] + (r[n:, :m] + r[:n, m:])) + r[n:, m:]


def whole(shape):
    return pl.BlockSpec(shape, lambda *_: (0,) * len(shape))


def leaf_forward_kernel(leaves, targets_ref, col_ref, inv_ref, blocks_ref, known_ref, sums_ref, own_ref):
    leaf = pl.program_id(0)

    @pl.when(leaf == 0)
    def _():
        sums_ref[...] = jnp.zeros_like(sums_ref)

    forward = dot(known_ref[0].T, inv_ref[0], 1, 1)
    update = dot(forward, blocks_ref[0], 1, 1)
    t = targets_ref[leaf]
    for q in range(sums_ref.shape[0]):
        sums_ref[q, t] += update[8 * q : 8 * q + 8]
    own = own_ref.shape[1]
    parts = forward.shape[0] // own
    col = col_ref[0]
    picked = forward[:own]
    for c in range(1, parts):
        picked = jnp.where(col == c, forward[c * own : (c + 1) * own], picked)
    own_ref[0] = picked


def leaf_forward(targets, col, inv, blocks, known, tops, n_cols):
    leaves, b, r = known.shape
    return pl.pallas_call(
        lambda *refs: leaf_forward_kernel(leaves, *refs),
        grid_spec=pltpu.PrefetchScalarGridSpec(
            num_scalar_prefetch=2,
            grid=(leaves,),
            in_specs=[
                pl.BlockSpec((1, b, b), lambda i, *_: (i, 0, 0)),
                pl.BlockSpec((1, b, b), lambda i, *_: (i, 0, 0)),
                pl.BlockSpec((1, b, r), lambda i, *_: (i, 0, 0)),
            ],
            out_specs=[
                whole((r // 8, tops, 8, b)),
                pl.BlockSpec((1, r // n_cols, b), lambda i, *_: (i, 0, 0)),
            ],
        ),
        out_shape=[
            jax.ShapeDtypeStruct((r // 8, tops, 8, b), F32),
            jax.ShapeDtypeStruct((leaves, r // n_cols, b), F32),
        ],
        name="leaf_forward",
    )(targets, col, inv, blocks, known)


def top_maps_kernel(inv_ref, sub_ref, next_ref, fwd_ref, bwd_ref, inv_t_ref, inv_pair_ref):
    def store(ref, x):
        high, low = split(x)
        m = x.shape[1]
        ref[0, :, :m] = high
        ref[0, :, m:] = low

    a = inv_ref[0]
    store(fwd_ref, -dot(a, sub_ref[0]).T)
    store(bwd_ref, -dot(next_ref[0], a))
    store(inv_t_ref, a.T)
    store(inv_pair_ref, a)


def top_maps(both):
    tops, _, b, _ = both.shape
    pair = jax.ShapeDtypeStruct((tops, b, 2 * b), BF16)
    out = pl.BlockSpec((1, b, 2 * b), lambda i: (i, 0, 0))
    return pl.pallas_call(
        top_maps_kernel,
        grid=(tops,),
        in_specs=[
            pl.BlockSpec((1, None, b, b), lambda i: (i, 0, 0, 0)),
            pl.BlockSpec((1, None, b, b), lambda i: (i, 1, 0, 0)),
            pl.BlockSpec((1, None, b, b), lambda i: (jnp.minimum(i + 1, tops - 1), 1, 0, 0)),
        ],
        out_specs=[out] * 4,
        out_shape=[pair] * 4,
        name="top_maps",
    )(both, both, both)


def top_chain_kernel(rhs_ref, fwd_ref, bwd_ref, inv_t_ref, inv_ref, out_ref):
    tops = rhs_ref.shape[0]
    scaled = []
    current = split_dot(rhs_ref[0], inv_t_ref[0])
    scaled.append(split_dot(current, inv_ref[0]))
    for t in range(1, tops):
        current = split_dot(rhs_ref[t], inv_t_ref[t]) + split_dot(current, fwd_ref[t])
        scaled.append(split_dot(current, inv_ref[t]))
    current = scaled[tops - 1]
    out_ref[tops - 1] = current
    for t in range(tops - 2, -1, -1):
        current = scaled[t] + split_dot(current, bwd_ref[t])
        out_ref[t] = current


def top_chain(rhs, maps):
    return pl.pallas_call(
        top_chain_kernel,
        out_shape=jax.ShapeDtypeStruct(rhs.shape, F32),
        name="top_chain",
    )(rhs, *maps)


def leaf_backward_kernel(targets_ref, tops_ref, blocks_ref, own_ref, inv_ref, out_ref, stage):
    leaf = pl.program_id(0)
    n_cols = blocks_ref.shape[0]
    own = own_ref.shape[1]
    b = own_ref.shape[2]
    left = own_ref[0]
    for p in range(n_cols):
        t = targets_ref[p, leaf]
        left = left - dot(tops_ref[:, t].reshape(own, b), blocks_ref[p, 0])
    group = b // own
    place = leaf % group
    stage[pl.ds(pl.multiple_of(place * own, own), own), :] = dot(left, inv_ref[0])

    @pl.when(place == group - 1)
    def _():
        turned = stage[...].T
        rows = b // n_cols
        for c in range(n_cols):
            out_ref[c, 0] = turned[c * rows : (c + 1) * rows]


def leaf_backward(targets, tops, blocks, own, inv):
    n_cols, leaves, b, _ = blocks.shape
    mine = own.shape[1]
    group = b // mine
    rows = b // n_cols
    return pl.pallas_call(
        leaf_backward_kernel,
        grid_spec=pltpu.PrefetchScalarGridSpec(
            num_scalar_prefetch=1,
            grid=(leaves,),
            in_specs=[
                pl.BlockSpec(tops.shape, lambda i, *_: (0, 0, 0, 0)),
                pl.BlockSpec((n_cols, 1, b, b), lambda i, *_: (0, i, 0, 0)),
                pl.BlockSpec((1, mine, b), lambda i, *_: (i, 0, 0)),
                pl.BlockSpec((1, b, b), lambda i, *_: (i, 0, 0)),
            ],
            out_specs=pl.BlockSpec((n_cols, 1, rows, b), lambda i, *_: (0, i // group, 0, 0)),
            scratch_shapes=[pltpu.VMEM((b, b), F32)],
        ),
        out_shape=jax.ShapeDtypeStruct((n_cols, leaves // group, rows, b), F32),
        name="leaf_backward",
    )(targets, tops, blocks, own, inv)


def arrange_kernel(got_ref, out_ref):
    n_cols, groups, _, lanes = got_ref.shape
    own = out_ref.shape[2] // n_cols
    group = lanes // own
    for g in range(groups):
        for i in range(group):
            for h in range(n_cols // group):
                out_ref[g * group + i, :, h * lanes : (h + 1) * lanes] = jnp.concatenate(
                    [got_ref[h * group + q, g, :, i * own : (i + 1) * own] for q in range(group)],
                    axis=1,
                )


def arrange(got, leaves, r):
    return pl.pallas_call(
        arrange_kernel,
        out_shape=jax.ShapeDtypeStruct((leaves, got.shape[2], r), F32),
        name="arrange",
    )(got)


def on_device(known, pivot, leaf_blocks, leaf_target, top_rhs, top_inv, top_sub):
    leaves, b, r = known.shape
    n_cols = lax.axis_size("cols")
    n_layers = lax.axis_size("layers")
    tops = lax.axis_size(ROWS)
    col = lax.axis_index("cols")
    row = lax.axis_index(ROWS)
    part = col * n_layers + lax.axis_index("layers")
    blocks = leaf_blocks[:, 0]
    slab = pivot.shape[1]

    both = lax.all_gather(jnp.stack([top_inv[0], top_sub[0]]), ROWS, axis=0, tiled=False)
    all_blocks = lax.all_gather(blocks, "cols", axis=0, tiled=False)

    named = jnp.zeros((1, slab, b), F32).at[0, 0, :leaves].set(leaf_target[:, 0].astype(F32))
    gathered = lax.all_gather(jnp.concatenate([pivot, named]), "cols", axis=1, tiled=True)
    all_targets = gathered[leaves].reshape(n_cols, slab, b)[:, 0, :leaves].astype(jnp.int32)

    sums, own = leaf_forward(
        leaf_target[:, 0], col[None], gathered, blocks, known, tops, n_cols
    )
    arrived = lax.all_to_all(sums, ("cols", "layers"), 0, 0, tiled=True)
    rhs_t = lax.dynamic_slice_in_dim(top_rhs[0], part * 8, 8, 1).T
    mine = (jnp.arange(tops) == row)[:, None, None]
    partial = jnp.where(mine, rhs_t[None], 0.0) - arrived.sum(0)

    quarter = lax.all_to_all(partial, "rlo", 0, 0, tiled=True)
    quarter = quarter.reshape((lax.axis_size("rlo"), -1) + quarter.shape[1:]).sum(0)
    quarter = lax.all_gather(quarter, "rhi", axis=0, tiled=False).sum(0)
    rhs = lax.all_gather(quarter, "rlo", axis=0, tiled=True)

    solved = top_chain(rhs, top_maps(both))
    own_tops = lax.all_gather(solved, "layers", axis=0, tiled=False)

    top_cols = lax.dynamic_index_in_dim(own_tops, row, 1, keepdims=False).reshape(1, -1, b)
    top_cols = jnp.broadcast_to(top_cols, (n_cols,) + top_cols.shape[1:])
    top_all = lax.all_to_all(top_cols, "cols", 0, 0, tiled=True)
    top_part = top_all.reshape(r, b).T[None]

    turned = leaf_backward(all_targets, own_tops, all_blocks, own, gathered)
    got = lax.all_to_all(turned, "cols", 0, 0, tiled=True)
    return arrange(got, leaves, r), top_part


def solution(mesh):
    rows = mesh.shape["rows"]
    low = 4 if rows % 4 == 0 else 1
    fine = Mesh(
        mesh.devices.reshape(rows // low, low, mesh.shape["cols"], mesh.shape["layers"]),
        ROWS + ("cols", "layers"),
    )
    held = ROWS + ("layers",)
    in_specs = (
        P(held, None, None),
        P(held, "cols", None),
        P(held, "cols", None, None),
        P(held, "cols"),
        P(ROWS, None, None),
        P(ROWS, None, None),
        P(ROWS, None, None),
    )
    out_specs = (P(held, "cols", None), P(ROWS, None, None))
    return jax.shard_map(
        on_device, mesh=fine, in_specs=in_specs, out_specs=out_specs, check_vma=False
    )
```

time: 691 us -> 196 us (0.28)
  waiting for transfers between devices: 521 us -> 37.2 us
  starting transfers between devices: 90.6 us -> 26.1 us
  Pallas kernels: 0 us -> 47.6 us
  blocking collectives: 24.5 us -> 62.9 us
  matrix products: 31.1 us -> 0 us
    psum x2 -> x0, waiting for transfers between devices: 201 us -> none  [the longest x1 142 us: on_device(): carried = lax.psum(own_sums, ('cols', 'layers'))]
    all_gather x2, waiting for transfers between devices: 138 us -> 0.01 us  [the longest x1 0.01 us: on_device(): lax.all_gather(jnp.stack([top_inv[0], top_sub[0]]), ROWS, axis=0, tiled=F...]
    ppermute x31 -> x0, waiting for transfers between devices: 121 us -> none  [from_behind(): return lax.ppermute(x, axis, pairs)]
    ppermute x31 -> x0, starting transfers between devices: 90.3 us -> none  [from_behind(): return lax.ppermute(x, axis, pairs)]
    reduce_scatter x1 -> x0, waiting for transfers between devices: 60.6 us -> none  [on_device(): lax.psum_scatter(jnp.einsum('lt,lar->tar', selector, contrib, precision=e...]
    pallas_call x0 -> x5, Pallas kernels: none -> 47.6 us  [the longest x1 13.8 us: leaf_backward(): pl.pallas_call(leaf_backward_kernel, grid_spec=pltpu.PrefetchScalarGridSp...]
    all_gather x1 -> x4, blocking collectives: 24.5 us -> 62.9 us  [the longest x1 21.3 us: on_device(): lax.all_gather(jnp.concatenate([pivot, named]), 'cols', axis=1, tiled=True)]
    all_to_all x0 -> x4, waiting for transfers between devices: none -> 36.4 us  [the longest x1 26.7 us: on_device(): arrived = lax.all_to_all(sums, ('cols', 'layers'), 0, 0, tiled=True)]
  transfers between devices with their start and end apart: 36 -> 6, of which waited for: 35 -> 3; matrix products, arithmetic and copies ran while one was open for 0% -> 2% of each run, Pallas kernels for 0% -> 23%
where the time goes in v1:
time: 196 us; the launch traced here: 195 us
  blocking collectives  62.9 us (32%)
  Pallas kernels  47.6 us (24%)
  waiting for transfers between devices  37.2 us (19%)
  starting transfers between devices  26.1 us (13%)
  between operations  14.1 us (7%)
  other arithmetic  4.57 us (2%)
  local copies, waits for them, and re-layouts  2.31 us (1%)
    all_to_all x1, waiting for transfers between devices, on_device(): arrived = lax.all_to_all(sums, ('cols', 'layers'), 0, 0, tiled=True)  26.7 us
    all_gather x1, blocking collectives, on_device(): lax.all_gather(jnp.concatenate([pivot, named]), 'cols', axis=1, tiled=True)  21.3 us
    all_gather x1, blocking collectives, on_device(): quarter = lax.all_gather(quarter, 'rhi', axis=0, tiled=False).sum(0)  20.5 us
    all_to_all x1, starting transfers between devices, on_device(): top_all = lax.all_to_all(top_cols, 'cols', 0, 0, tiled=True)  14 us
    pallas_call x1, Pallas kernels, leaf_backward(): pl.pallas_call(leaf_backward_kernel, grid_spec=pltpu.PrefetchScalarGridSp...  13.8 us
    pallas_call x1, Pallas kernels, leaf_forward(): pl.pallas_call(lambda *refs: leaf_forward_kernel(leaves, *refs), grid_spe...  13.1 us
    pallas_call x1, Pallas kernels, top_maps(): pl.pallas_call(top_maps_kernel, grid=(tops,), in_specs=[pl.BlockSpec((1,...  11.7 us
    all_gather x1, blocking collectives, on_device(): rhs = lax.all_gather(quarter, 'rlo', axis=0, tiled=True)  11.2 us
  transfers between devices with their start and end apart: 6, of which 3 were waited for; matrix products, arithmetic and copies ran while one was open for 2% of the time, Pallas kernels for 23%

profile of v1, /device:TPU:1, one launch (start us, length us, event | category | flops | bytes accessed | tf_op | source)
XLA Modules:
  0.0 194.7 jit_solution(6270447774475620698)
XLA Ops:
  7.2 1.6 pad_maximum_fusion
  8.9 0.7 all-gather.9.cloned.1.call-update
  9.6 0.7 convert_bitcast_fusion.1
  10.2 0.9 select_maximum_fusion
  11.1 21.3 %all_gather.27.refs_2_.inv_ref = f32[13,128,128]{2,1,0:T(8,128)} all-gather(f32[13,16,128]{2,1,0:T(8,128)S(1)} %select_maximum_fusion), channel_id=1, replica_groups=mesh['rhi'=4,'rlo'=4,'cols'=8,'layers'=4] {'cols'}, dimensions={1}, use_global_device_ids=true | all-gather | bytes 958464 | tf_op jit(solution)/shard_map/all_gather | solution.py:220
  32.4 13.1 %leaf_forward.1 = (f32[32,16,8,128]{3,2,1,0:T(8,128)}, f32[12,32,128]{2,1,0:T(8,128)}) custom-call(s32[12]{0:T(128)} %bitcast.37, s32[1]{0:T(128)} %bitcast.6.refs_1_, f32[13,128,128]{2,1,0:T(8,128)} %all_gather.27.refs_2_.inv_ref, f32[12,128,128]{2,1,0:T(8,128)} %bitcast.29, f32[12,128,256]{2,1,0:T(8,128)} %refs_4_.1), custom_call_target="tpu_custom_call" | custom-call | tf_op jit(solution)/shard_map/leaf_forward/pallas_call | solution.py:61
  45.5 3.9 %all-to-all-start = ((f32[32,16,8,128]{3,2,1,0:T(8,128)}), f32[32,16,8,128]{3,2,1,0:T(8,128)S(1)}, u32[]{:S(2)}, u32[]{:S(2)}) async-start(f32[32,16,8,128]{3,2,1,0:T(8,128)} %get-tuple-element.20), calls=%async_computation | async-start | bytes 4194304 | tf_op jit(solution)/shard_map/all_to_all | solution.py:226
  49.6 26.7 %all-to-all-done = f32[32,16,8,128]{3,2,1,0:T(8,128)S(1)} async-done(((f32[32,16,8,128]{3,2,1,0:T(8,128)}), f32[32,16,8,128]{3,2,1,0:T(8,128)S(1)}, u32[]{:S(2)}, u32[]{:S(2)}) %all-to-all-start) | async-done | bytes 2097184 | tf_op jit(solution)/shard_map/all_to_all | solution.py:226
  76.4 0.7 select_subtract_fusion
  77.1 3.4 %all-to-all-start.1 = ((f32[16,8,128]{2,1,0:T(8,128)}), f32[16,8,128]{2,1,0:T(8,128)S(1)}, u32[]{:S(2)}, u32[]{:S(2)}) async-start(f32[16,8,128]{2,1,0:T(8,128)} %select_subtract_fusion), calls=%async_computation.1 | async-start | bytes 131072 | tf_op jit(solution)/shard_map/all_to_all | solution.py:231
  80.5 4.6 %all-to-all-done.1 = f32[16,8,128]{2,1,0:T(8,128)S(1)} async-done(((f32[16,8,128]{2,1,0:T(8,128)}), f32[16,8,128]{2,1,0:T(8,128)S(1)}, u32[]{:S(2)}, u32[]{:S(2)}) %all-to-all-start.1) | async-done | bytes 65568 | tf_op jit(solution)/shard_map/all_to_all | solution.py:231
  85.1 20.5 %all-gather = f32[16,8,128]{2,1,0:T(8,128)S(1)} all-gather(f32[4,8,128]{2,1,0:T(8,128)S(1)} %reduce_sum.28), channel_id=2, replica_groups=mesh['rhi'=4,'rlo'=4,'cols'=8,'layers'=4] {'rhi'}, dimensions={0}, use_global_device_ids=true | all-gather | bytes 81920 | tf_op jit(solution)/shard_map/all_gather | solution.py:233
  105.6 11.2 %all_gather.30.rhs_ref = f32[16,8,128]{2,1,0:T(8,128)} all-gather(f32[4,8,128]{2,1,0:T(8,128)S(1)} %reduce_sum.29), channel_id=1, replica_groups=mesh['rhi'=4,'rlo'=4,'cols'=8,'layers'=4] {'rlo'}, dimensions={0}, use_global_device_ids=true | all-gather | bytes 81920 | tf_op jit(solution)/shard_map/all_gather | solution.py:234
  116.8 11.7 %top_maps.1 = (bf16[16,128,256]{2,1,0:T(8,128)(2,1)}, bf16[16,128,256]{2,1,0:T(8,128)(2,1)}, bf16[16,128,256]{2,1,0:T(8,128)(2,1)}, bf16[16,128,256]{2,1,0:T(8,128)(2,1)}) custom-call(f32[16,2,128,128]{3,2,1,0:T(8,128)} %bitcast.24, f32[16,2,128,128]{3,2,1,0:T(8,128)} %bitcast.25, f32[16,2,128,128]{3,2,1,0:T(8,128)} %bitcast.26), custom_call_target="tpu_custom_call" | custom-call | tf_op jit(solution)/shard_map/top_maps/pallas_call | solution.py:102
  128.5 7.1 %top_chain.1 = f32[16,8,128]{2,1,0:T(8,128)} custom-call(f32[16,8,128]{2,1,0:T(8,128)} %all_gather.30.rhs_ref, bf16[16,128,256]{2,1,0:T(8,128)(2,1)} %get-tuple-element.21.fwd_ref, bf16[16,128,256]{2,1,0:T(8,128)(2,1)} %get-tuple-element.22.bwd_ref, bf16[16,128,256]{2,1,0:T(8,128)(2,1)} %get-tuple-element.23.inv_t_ref, ...), custom_call_target="tpu_custom_call" | custom-call | tf_op jit(solution)/shard_map/top_chain/pallas_call | solution.py:132
  135.6 9.9 %all-gather.2 = f32[64,8,128]{2,1,0:T(8,128)S(1)} all-gather(f32[16,8,128]{2,1,0:T(8,128)} %top_chain.1), channel_id=4, replica_groups=mesh['rhi'=4,'rlo'=4,'cols'=8,'layers'=4] {'layers'}, dimensions={0}, use_global_device_ids=true | all-gather | bytes 327680 | tf_op jit(solution)/shard_map/all_gather | solution.py:237
  145.6 0.7 broadcast_in_dim.41
  146.3 14.0 %all-to-all-start.3 = ((f32[8,32,128]{2,1,0:T(8,128)}), f32[8,32,128]{2,1,0:T(8,128)S(1)}, u32[]{:S(2)}, u32[]{:S(2)}) async-start(f32[8,32,128]{2,1,0:T(8,128)} %broadcast_in_dim.41), calls=%async_computation.3 | async-start | bytes 262144 | tf_op jit(solution)/shard_map/all_to_all | solution.py:241
  160.9 13.8 %leaf_backward.1 = f32[8,3,16,128]{3,2,1,0:T(8,128)} custom-call(s32[8,12]{1,0:T(8,128)} %convert_bitcast_fusion.targets_ref, f32[4,16,8,128]{3,2,1,0:T(8,128)} %bitcast.31, f32[8,12,128,128]{3,2,1,0:T(8,128)} %bitcast.28, f32[12,32,128]{2,1,0:T(8,128)} %get-tuple-element.25.own_ref, f32[13,128,128]{2,1,0:T(8,128)} %all_gather.27.refs_2_.inv_ref), custom_call_target="tpu_custom_call" | custom-call | tf_op jit(solution)/shard_map/leaf_backward/pallas_call | solution.py:165
  174.7 4.8 %all-to-all-start.2 = ((f32[8,3,16,128]{3,2,1,0:T(8,128)}), f32[8,3,16,128]{3,2,1,0:T(8,128)S(1)}, u32[]{:S(2)}, u32[]{:S(2)}) async-start(f32[8,3,16,128]{3,2,1,0:T(8,128)} %leaf_backward.1), calls=%async_computation.2 | async-start | bytes 393216 | tf_op jit(solution)/shard_map/all_to_all | solution.py:245
  179.5 0.8 copy.18
  180.2 5.1 %all-to-all-done.2.got_ref = f32[8,3,16,128]{3,2,1,0:T(8,128)S(1)} async-done(((f32[8,3,16,128]{3,2,1,0:T(8,128)}), f32[8,3,16,128]{3,2,1,0:T(8,128)S(1)}, u32[]{:S(2)}, u32[]{:S(2)}) %all-to-all-start.2) | async-done | bytes 196640 | tf_op jit(solution)/shard_map/all_to_all | solution.py:245
  185.3 0.7 copy-done.2
  186.0 1.8 arrange.1
  (22 shorter events, 1.0 us)
Async XLA Ops:
  7.2 42.2 %copy-start = (f32[1,128,256]{2,1,0:T(8,128)S(1)}, f32[1,128,256]{2,1,0:T(8,128)}, u32[]{:S(2)}) copy-start(f32[1,128,256]{2,1,0:T(8,128)} %param.13) | copy-start | bytes 393220
  7.2 109.6 %all-gather.7.cloned.1.call-start = ((), (), s32[]{:S(2)}) async-start(), calls=%async_computation.4 | async-start | bytes 2228224 | tf_op jit(solution)/shard_map/all_gather | solution.py:216
  8.8 152.1 %all-gather.9.cloned.1.call-start = ((), (), s32[]{:S(2)}) async-start(), calls=%async_computation.5 | async-start | bytes 7077888 | tf_op jit(solution)/shard_map/all_gather | solution.py:217
  45.5 30.8 %all-to-all-start = ((f32[32,16,8,128]{3,2,1,0:T(8,128)}), f32[32,16,8,128]{3,2,1,0:T(8,128)S(1)}, u32[]{:S(2)}, u32[]{:S(2)}) async-start(f32[32,16,8,128]{3,2,1,0:T(8,128)} %get-tuple-element.20), calls=%async_computation | async-start | bytes 4194304 | tf_op jit(solution)/shard_map/all_to_all | solution.py:226
  49.4 31.1 %slice-start = ((f32[13,128,128]{2,1,0:T(8,128)}), f32[1,128,128]{2,1,0:T(8,128)S(1)}, s32[]{:S(2)}) async-start(f32[13,128,128]{2,1,0:T(8,128)} %all_gather.27.refs_2_.inv_ref), calls=%async_computation.6 | async-start | bytes 131072 | tf_op jit(solution)/shard_map/slice | solution.py:221
  77.1 8.0 %all-to-all-start.1 = ((f32[16,8,128]{2,1,0:T(8,128)}), f32[16,8,128]{2,1,0:T(8,128)S(1)}, u32[]{:S(2)}, u32[]{:S(2)}) async-start(f32[16,8,128]{2,1,0:T(8,128)} %select_subtract_fusion), calls=%async_computation.1 | async-start | bytes 131072 | tf_op jit(solution)/shard_map/all_to_all | solution.py:231
  145.5 15.3 %copy-start.1 = (f32[64,8,128]{2,1,0:T(8,128)}, f32[64,8,128]{2,1,0:T(8,128)S(1)}, u32[]{:S(2)}) copy-start(f32[64,8,128]{2,1,0:T(8,128)S(1)} %all-gather.2) | copy-start | bytes 786436
  146.3 28.4 %all-to-all-start.3 = ((f32[8,32,128]{2,1,0:T(8,128)}), f32[8,32,128]{2,1,0:T(8,128)S(1)}, u32[]{:S(2)}, u32[]{:S(2)}) async-start(f32[8,32,128]{2,1,0:T(8,128)} %broadcast_in_dim.41), calls=%async_computation.3 | async-start | bytes 262144 | tf_op jit(solution)/shard_map/all_to_all | solution.py:241
  174.7 10.7 %all-to-all-start.2 = ((f32[8,3,16,128]{3,2,1,0:T(8,128)}), f32[8,3,16,128]{3,2,1,0:T(8,128)S(1)}, u32[]{:S(2)}, u32[]{:S(2)}) async-start(f32[8,3,16,128]{3,2,1,0:T(8,128)} %leaf_backward.1), calls=%async_computation.2 | async-start | bytes 393216 | tf_op jit(solution)/shard_map/all_to_all | solution.py:245
  185.3 0.7 copy-start.2
Sparse Core Ops, SparseCore 0:
  10.7 69.9 all-gather.6
  82.8 54.2 all-gather.8

commit v2 on v1

v2 whole, which is shorter than its diff:
```python
import jax
import jax.numpy as jnp
from jax import lax
from jax.experimental import pallas as pl
from jax.experimental.pallas import tpu as pltpu
from jax.sharding import Mesh, PartitionSpec as P

F32 = jnp.float32
BF16 = jnp.bfloat16
ROWS = ("rhi", "rlo")
COLS = ("y", "core")


def dot(a, b, cb=0):
    return lax.dot_general(a, b, (((1,), (cb,)), ((), ())), preferred_element_type=F32)


def split(x):
    high = x.astype(BF16)
    low = (x - high.astype(F32)).astype(BF16)
    return high, low


def dot3(a, b, cb=0):
    ah, al = split(a)
    bh, bl = split(b)
    both = dot(
        jnp.concatenate([ah, al], axis=1), jnp.concatenate([bh, bh], axis=cb), cb
    )
    return both + dot(ah, bl, cb)


def row_dot(x, matrix, cb=0):
    n = x.shape[0]
    m = matrix.shape[1 - cb]
    rows = jnp.concatenate(split(x), axis=0)
    r = dot(rows, jnp.concatenate(split(matrix), axis=1 - cb), cb)
    return (r[:n, :m] + (r[n:, :m] + r[:n, m:])) + r[n:, m:]


def whole(shape):
    return pl.BlockSpec(shape, lambda *_: (0,) * len(shape))


def leaf_forward_kernel(place_ref, targets_ref, inv_ref, mine_ref, pair_ref, known_ref, sums_ref, own_ref, stage):
    leaf = pl.program_id(0)

    @pl.when(leaf == 0)
    def _():
        sums_ref[...] = jnp.zeros_like(sums_ref)

    b = inv_ref.shape[1]
    forward = dot3(known_ref[0].T, inv_ref[0], 1)
    update = dot3(forward, jnp.concatenate([mine_ref[0], pair_ref[0]], axis=0), 1)
    for k in range(2):
        t = targets_ref[k, leaf]
        for q in range(sums_ref.shape[0]):
            sums_ref[q, t] += update[8 * q : 8 * q + 8, k * b : (k + 1) * b]
    own = own_ref.shape[1]
    stage[...] = forward
    own_ref[0] = stage[pl.ds(pl.multiple_of(place_ref[1] * own, own), own), :]


def leaf_forward(place, targets, inv, mine, pair, known, tops, n_cols):
    leaves, b, r = known.shape
    half = r // 2
    own = r // n_cols
    block = pl.BlockSpec((1, b, b), lambda i, *_: (i, 0, 0))
    return pl.pallas_call(
        leaf_forward_kernel,
        grid_spec=pltpu.PrefetchScalarGridSpec(
            num_scalar_prefetch=2,
            grid=(leaves,),
            in_specs=[
                block,
                block,
                block,
                pl.BlockSpec((1, b, half), lambda i, place, _: (i, 0, place[0])),
            ],
            out_specs=[
                whole((half // 8, tops, 8, b)),
                pl.BlockSpec((1, own, b), lambda i, *_: (i, 0, 0)),
            ],
            scratch_shapes=[pltpu.VMEM((half, b), F32)],
        ),
        out_shape=[
            jax.ShapeDtypeStruct((half // 8, tops, 8, b), F32),
            jax.ShapeDtypeStruct((leaves, own, b), F32),
        ],
        name="leaf_forward",
    )(place, targets, inv, mine, pair, known)


def top_map_kernel(inv_ref, sub_ref, out_ref):
    out_ref[0] = inv_ref[0]
    out_ref[1] = -lax.dot_general(
        inv_ref[0],
        sub_ref[0],
        (((1,), (0,)), ((), ())),
        precision=lax.Precision.HIGHEST,
        preferred_element_type=F32,
    )


def top_map(inv, sub):
    return pl.pallas_call(
        top_map_kernel,
        out_shape=jax.ShapeDtypeStruct((2,) + inv.shape[1:], F32),
        name="top_map",
    )(inv, sub)


def top_chain_kernel(rhs_ref, maps_ref, out_ref):
    tops = rhs_ref.shape[0]
    solved = []
    current = row_dot(rhs_ref[0], maps_ref[0, 0], 1)
    solved.append(current)
    for t in range(1, tops):
        current = row_dot(rhs_ref[t], maps_ref[t, 0], 1) + row_dot(current, maps_ref[t, 1], 1)
        solved.append(current)
    rest = solved[tops - 1]
    out_ref[tops - 1] = row_dot(rest, maps_ref[tops - 1, 0])
    for t in range(tops - 2, -1, -1):
        rest = solved[t] + row_dot(rest, maps_ref[t + 1, 1])
        out_ref[t] = row_dot(rest, maps_ref[t, 0])


def top_chain(rhs, maps):
    return pl.pallas_call(
        top_chain_kernel,
        out_shape=jax.ShapeDtypeStruct(rhs.shape, F32),
        name="top_chain",
    )(rhs, maps)


def leaf_backward_kernel(targets_ref, tops_ref, *refs):
    *block_refs, own_ref, inv_ref, out_ref, stage, parts = refs
    leaf = pl.program_id(0)
    n_cols = len(block_refs)
    own = own_ref.shape[1]
    b = own_ref.shape[2]

    @pl.when(leaf == 0)
    def _():
        for t in range(parts.shape[0]):
            high, low = split(tops_ref[:, t].reshape(own, b))
            parts[t, :own] = high
            parts[t, own:] = low

    both = jnp.concatenate([parts[targets_ref[p, leaf]] for p in range(n_cols)], axis=1)
    high, low = split(jnp.concatenate([ref[0] for ref in block_refs], axis=0))
    r = dot(both, high)
    left = own_ref[0] - ((r[:own] + r[own:]) + dot(both[:own], low))
    group = b // own
    place = leaf % group
    stage[pl.ds(pl.multiple_of(place * own, own), own), :] = dot3(left, inv_ref[0])

    @pl.when(place == group - 1)
    def _():
        turned = stage[...].T
        rows = b // n_cols
        for c in range(n_cols):
            out_ref[c, 0] = turned[c * rows : (c + 1) * rows]


def leaf_backward(targets, tops, blocks, own, inv):
    n_cols = len(blocks)
    leaves, b, _ = blocks[0].shape
    mine = own.shape[1]
    group = b // mine
    rows = b // n_cols
    block = pl.BlockSpec((1, b, b), lambda i, *_: (i, 0, 0))
    return pl.pallas_call(
        leaf_backward_kernel,
        grid_spec=pltpu.PrefetchScalarGridSpec(
            num_scalar_prefetch=1,
            grid=(leaves,),
            in_specs=[pl.BlockSpec(tops.shape, lambda i, *_: (0, 0, 0, 0))]
            + [block] * n_cols
            + [pl.BlockSpec((1, mine, b), lambda i, *_: (i, 0, 0)), block],
            out_specs=pl.BlockSpec((n_cols, 1, rows, b), lambda i, *_: (0, i // group, 0, 0)),
            scratch_shapes=[
                pltpu.VMEM((b, b), F32),
                pltpu.VMEM((tops.shape[1], 2 * mine, b), BF16),
            ],
        ),
        out_shape=jax.ShapeDtypeStruct((n_cols, leaves // group, rows, b), F32),
        name="leaf_backward",
    )(targets, tops, *blocks, own, inv)


def arrange_kernel(got_ref, out_ref):
    n_cols, groups, _, lanes = got_ref.shape
    own = out_ref.shape[2] // n_cols
    group = lanes // own
    for g in range(groups):
        for i in range(group):
            for h in range(n_cols // group):
                out_ref[g * group + i, :, h * lanes : (h + 1) * lanes] = jnp.concatenate(
                    [got_ref[2 * q + h, g, :, i * own : (i + 1) * own] for q in range(group)],
                    axis=1,
                )


def arrange(got, leaves, r):
    return pl.pallas_call(
        arrange_kernel,
        out_shape=jax.ShapeDtypeStruct((leaves, got.shape[2], r), F32),
        name="arrange",
    )(got)


def spread(x, axis):
    return lax.all_to_all(jnp.broadcast_to(x, (lax.axis_size(axis),) + x.shape), axis, 0, 0, tiled=True)


def from_core(x):
    return lax.ppermute(x, "core", [(0, 1), (1, 0)])


def from_y(x, step):
    n = lax.axis_size("y")
    return lax.ppermute(x, "y", [(i, (i - step) % n) for i in range(n)])


def on_device(known, pivot, leaf_blocks, leaf_target, top_rhs, top_inv, top_sub):
    leaves, b, r = known.shape
    n_y = lax.axis_size("y")
    n_cols = 2 * n_y
    n_layers = lax.axis_size("layers")
    tops = lax.axis_size(ROWS)
    y = lax.axis_index("y")
    core = lax.axis_index("core")
    row = lax.axis_index(ROWS)
    blocks = leaf_blocks[:, 0]
    slab = pivot.shape[1]
    own = r // n_cols

    maps = lax.all_gather(top_map(top_inv, top_sub), ROWS, axis=0, tiled=False)

    paired = from_core(blocks)
    named = jnp.zeros((1, slab, b), F32).at[0, 0, :leaves].set(leaf_target[:, 0].astype(F32))
    inv = lax.all_gather(jnp.concatenate([pivot, named]), COLS, axis=1, tiled=True)
    targets = inv[leaves].reshape(n_y, 2, slab, b)[:, :, 0, :leaves].astype(jnp.int32)
    targets = jnp.roll(targets, -y, axis=0)
    targets = jnp.where(core == 0, targets, targets[:, ::-1]).reshape(n_cols, leaves)

    sums, own_forward = leaf_forward(
        jnp.stack([core, y]), targets, inv, blocks, paired, known, tops, n_cols
    )
    arrived = lax.all_to_all(sums, ("y", "layers"), 0, 0, tiled=True)
    start = core * (r // 2) + y * own + lax.axis_index("layers") * 8
    rhs_t = lax.dynamic_slice_in_dim(top_rhs[0], start, 8, 1).T
    mine = (jnp.arange(tops) == row)[:, None, None]
    partial = jnp.where(mine, rhs_t[None], 0.0) - arrived.sum(0)

    held, partial = lax.optimization_barrier((blocks, partial))
    far = [from_y(held, step) for step in range(1, n_y)]

    quarter = lax.all_to_all(partial, "rlo", 0, 0, tiled=True)
    quarter = quarter.reshape((lax.axis_size("rlo"), -1) + quarter.shape[1:]).sum(0)
    quarter = spread(quarter, "rhi").reshape((-1,) + quarter.shape).sum(0)
    rhs = spread(quarter, "rlo").reshape(tops, 8, b)

    solved = top_chain(rhs, maps)
    solved, far = lax.optimization_barrier((solved, far))
    all_blocks = [blocks, paired]
    for block in far:
        all_blocks += [block, from_core(block)]
    own_tops = spread(solved, "layers").reshape(n_layers, tops, 8, b)

    top_cols = lax.dynamic_index_in_dim(own_tops, row, 1, keepdims=False).reshape(own, b)
    top_all = spread(top_cols, COLS).reshape(n_y, 2, own, b)
    top_part = top_all.transpose(1, 0, 2, 3).reshape(r, b).T[None]

    turned = leaf_backward(targets, own_tops, all_blocks, own_forward, inv)
    got = lax.all_to_all(turned, COLS, 0, 0, tiled=True)
    return arrange(got, leaves, r), top_part


def solution(mesh):
    rows = mesh.shape["rows"]
    low = 4
    fine = Mesh(
        mesh.devices.reshape(
            rows // low, low, mesh.shape["cols"] // 2, 2, mesh.shape["layers"]
        ),
        ROWS + COLS + ("layers",),
    )
    held = ROWS + ("layers",)
    in_specs = (
        P(held, None, None),
        P(held, COLS, None),
        P(held, COLS, None, None),
        P(held, COLS),
        P(ROWS, None, None),
        P(ROWS, None, None),
        P(ROWS, None, None),
    )
    out_specs = (P(held, COLS, None), P(ROWS, None, None))
    return jax.shard_map(
        on_device, mesh=fine, in_specs=in_specs, out_specs=out_specs, check_vma=False
    )
```

time: 196 us -> 184 us (0.939)
  starting transfers between devices: 26.1 us -> 47.2 us
  Pallas kernels: 47.6 us -> 31.6 us
  blocking collectives: 62.9 us -> 51 us
  waiting for transfers between devices: 37.2 us -> 30.2 us
  local copies, waits for them, and re-layouts: 2.31 us -> 4.83 us
    all_gather x4 -> x1, blocking collectives: 62.9 us -> 13.5 us  [on_device(): lax.all_gather(jnp.concatenate([pivot, named]), COLS, axis=1, tiled=True)]
    all_to_all x0 -> x3, blocking collectives: none -> 37.5 us  [the longest x2 30.2 us: spread(): lax.all_to_all(jnp.broadcast_to(x, (lax.axis_size(axis),) + x.shape), axi...]
    ppermute x0 -> x7, starting transfers between devices: none -> 29.2 us  [the longest x4 21.8 us: from_core(): return lax.ppermute(x, 'core', [(0, 1), (1, 0)])]
    pallas_call x2, Pallas kernels: 24.8 us -> 12.6 us  [the longest x1 10.8 us: leaf_forward(): pl.pallas_call(leaf_forward_kernel, grid_spec=pltpu.PrefetchScalarGridSpe...]
    all_to_all x4, starting transfers between devices: 26 us -> 17.9 us  [the longest x2 9.34 us: spread(): lax.all_to_all(jnp.broadcast_to(x, (lax.axis_size(axis),) + x.shape), axi...]
    all_to_all x4, waiting for transfers between devices: 36.4 us -> 30.1 us  [the longest x1 18.2 us: on_device(): arrived = lax.all_to_all(sums, ('y', 'layers'), 0, 0, tiled=True)]
    pallas_call x1, Pallas kernels: 13.8 us -> 10.9 us  [leaf_backward(): pl.pallas_call(leaf_backward_kernel, grid_spec=pltpu.PrefetchScalarGridSp...]
  transfers between devices with their start and end apart: 6 -> 12, of which waited for: 3 -> 3; matrix products, arithmetic and copies ran while one was open for 2% -> 3% of each run, Pallas kernels for 23% -> 15%
where the time goes in v2:
time: 184 us; the launch traced here: 182 us
  blocking collectives  51 us (28%)
  starting transfers between devices  47.2 us (26%)
  Pallas kernels  31.6 us (17%)
  waiting for transfers between devices  30.2 us (16%)
  between operations  14.3 us (8%)
  local copies, waits for them, and re-layouts  4.83 us (3%)
  other arithmetic  3.12 us (2%)
    all_to_all x2, blocking collectives, spread(): lax.all_to_all(jnp.broadcast_to(x, (lax.axis_size(axis),) + x.shape), axi...  30.2 us
    ppermute x4, starting transfers between devices, from_core(): return lax.ppermute(x, 'core', [(0, 1), (1, 0)])  21.8 us
    all_to_all x1, waiting for transfers between devices, on_device(): arrived = lax.all_to_all(sums, ('y', 'layers'), 0, 0, tiled=True)  18.2 us
    all_gather x1, blocking collectives, on_device(): lax.all_gather(jnp.concatenate([pivot, named]), COLS, axis=1, tiled=True)  13.5 us
    pallas_call x1, Pallas kernels, leaf_backward(): pl.pallas_call(leaf_backward_kernel, grid_spec=pltpu.PrefetchScalarGridSp...  10.9 us
    pallas_call x1, Pallas kernels, leaf_forward(): pl.pallas_call(leaf_forward_kernel, grid_spec=pltpu.PrefetchScalarGridSpe...  10.8 us
    all_to_all x2, starting transfers between devices, spread(): lax.all_to_all(jnp.broadcast_to(x, (lax.axis_size(axis),) + x.shape), axi...  9.34 us
    ppermute x3, starting transfers between devices, from_y(): return lax.ppermute(x, 'y', [(i, (i - step) % n) for i in range(n)])  7.43 us
  transfers between devices with their start and end apart: 12, of which 3 were waited for; matrix products, arithmetic and copies ran while one was open for 3% of the time, Pallas kernels for 15%

profile of v2, /device:TPU:1, one launch (start us, length us, event | category | flops | bytes accessed | tf_op | source)
XLA Modules:
  0.0 182.2 jit_solution(6021235046790953320)
XLA Ops:
  7.2 1.8 top_map.1
  9.0 8.8 %collective-permute-start = (f32[12,128,128]{2,1,0:T(8,128)}, f32[12,128,128]{2,1,0:T(8,128)S(1)}, u32[]{:S(2)}, u32[]{:S(2)}) collective-permute-start(f32[12,128,128]{2,1,0:T(8,128)} %bitcast.26), channel_id=1, source_target_pairs={{0,4},{4,0},{1,5},{5,1},{2,6},{6,2},{3,7},{7,3},{8,12},{12,8},{9,1... | collective-permute-start | bytes 2359304 | tf_op jit(solution)/shard_map/ppermute | solution.py:218
  19.4 13.5 %all_gather.9.inv_ref.refs_9_ = f32[13,128,128]{2,1,0:T(8,128)S(1)} all-gather(f32[13,16,128]{2,1,0:T(8,128)S(1)} %select_maximum_fusion), channel_id=1, replica_groups=mesh['rhi'=4,'rlo'=4,'y'=4,'core'=2,'layers'=4] {'y','core'}, dimensions={1}, use_global_device_ids=true | all-gather | bytes 958464 | tf_op jit(solution)/shard_map/all_gather | solution.py:243
  35.2 10.8 %leaf_forward.1 = (f32[16,16,8,128]{3,2,1,0:T(8,128)}, f32[12,32,128]{2,1,0:T(8,128)}) custom-call(s32[2]{0:T(128)} %pad_add_fusion.place_ref, s32[8,12]{1,0:T(8,128)} %bitcast.38, f32[13,128,128]{2,1,0:T(8,128)} %copy-done.1, f32[12,128,128]{2,1,0:T(8,128)} %bitcast.27, f32[12,128,128]{2,1,0:T(8,128)} %copy-done.3, f32[12,128,256]{2,1,0:T(8,128)} %known_ref.1), custom_call_target="tpu_custom_call" | custom-call | tf_op jit(solution)/shard_map/leaf_forward/pallas_call | solution.py:69
  46.1 3.8 %all-to-all-start = ((f32[16,16,8,128]{3,2,1,0:T(8,128)}), f32[16,16,8,128]{3,2,1,0:T(8,128)S(1)}, u32[]{:S(2)}, u32[]{:S(2)}) async-start(f32[16,16,8,128]{3,2,1,0:T(8,128)} %get-tuple-element.22), calls=%async_computation | async-start | bytes 2097152 | tf_op jit(solution)/shard_map/all_to_all | solution.py:251
  50.0 18.2 %all-to-all-done = f32[16,16,8,128]{3,2,1,0:T(8,128)S(1)} async-done(((f32[16,16,8,128]{3,2,1,0:T(8,128)}), f32[16,16,8,128]{3,2,1,0:T(8,128)S(1)}, u32[]{:S(2)}, u32[]{:S(2)}) %all-to-all-start) | async-done | bytes 1048608 | tf_op jit(solution)/shard_map/all_to_all | solution.py:251
  68.4 3.0 %collective-permute-start.1 = (f32[12,128,128]{2,1,0:T(8,128)S(1)}, f32[12,128,128]{2,1,0:T(8,128)S(1)}, u32[]{:S(2)}, u32[]{:S(2)}) collective-permute-start(f32[12,128,128]{2,1,0:T(8,128)S(1)} %bitcast.29), channel_id=1, source_target_pairs={{0,24},{8,0},{16,8},{24,16},{1,25},{9,1},{17,9},{25,17},{2,26},{10... | collective-permute-start | bytes 2359304 | tf_op jit(solution)/shard_map/ppermute | solution.py:223
  71.4 2.5 %collective-permute-start.2 = (f32[12,128,128]{2,1,0:T(8,128)S(1)}, f32[12,128,128]{2,1,0:T(8,128)S(1)}, u32[]{:S(2)}, u32[]{:S(2)}) collective-permute-start(f32[12,128,128]{2,1,0:T(8,128)S(1)} %bitcast.30), channel_id=1, source_target_pairs={{0,16},{8,24},{16,0},{24,8},{1,17},{9,25},{17,1},{25,9},{2,18},{10... | collective-permute-start | bytes 2359304 | tf_op jit(solution)/shard_map/ppermute | solution.py:223
  73.9 1.9 %collective-permute-start.3 = (f32[12,128,128]{2,1,0:T(8,128)S(1)}, f32[12,128,128]{2,1,0:T(8,128)S(1)}, u32[]{:S(2)}, u32[]{:S(2)}) collective-permute-start(f32[12,128,128]{2,1,0:T(8,128)S(1)} %bitcast.31), channel_id=1, source_target_pairs={{0,8},{8,16},{16,24},{24,0},{1,9},{9,17},{17,25},{25,1},{2,10},{10... | collective-permute-start | bytes 2359304 | tf_op jit(solution)/shard_map/ppermute | solution.py:223
  75.9 7.3 %all_to_all.35 = f32[16,8,128]{2,1,0:T(8,128)S(1)} all-to-all(f32[16,8,128]{2,1,0:T(8,128)S(1)} %select_subtract_fusion), channel_id=1, replica_groups=mesh['rhi'=4,'rlo'=4,'y'=4,'core'=2,'layers'=4] {'rlo'}, dimensions={0} | all-to-all | bytes 131072 | tf_op jit(solution)/shard_map/all_to_all | solution.py:260
  83.2 22.6 %all_to_all.36 = f32[4,4,8,128]{3,2,1,0:T(8,128)S(1)} all-to-all(f32[4,4,8,128]{3,2,1,0:T(8,128)S(1)} %broadcast_in_dim.41), channel_id=1, replica_groups=mesh['rhi'=4,'rlo'=4,'y'=4,'core'=2,'layers'=4] {'rhi'}, dimensions={0} | all-to-all | bytes 131072 | tf_op jit(solution)/shard_map/all_to_all | solution.py:214
  105.8 7.6 %all_to_all.37 = f32[4,4,8,128]{3,2,1,0:T(8,128)} all-to-all(f32[4,4,8,128]{3,2,1,0:T(8,128)S(1)} %broadcast_in_dim.42), channel_id=1, replica_groups=mesh['rhi'=4,'rlo'=4,'y'=4,'core'=2,'layers'=4] {'rlo'}, dimensions={0} | all-to-all | bytes 131072 | tf_op jit(solution)/shard_map/all_to_all | solution.py:214
  113.4 6.3 %top_chain.1 = f32[16,8,128]{2,1,0:T(8,128)} custom-call(f32[16,8,128]{2,1,0:T(8,128)} %bitcast.35, f32[16,2,128,128]{3,2,1,0:T(8,128)} %bitcast.32), custom_call_target="tpu_custom_call" | custom-call | tf_op jit(solution)/shard_map/top_chain/pallas_call | solution.py:129
  119.7 8.7 %collective-permute-start.4 = (f32[12,128,128]{2,1,0:T(8,128)S(1)}, f32[12,128,128]{2,1,0:T(8,128)}, u32[]{:S(2)}, u32[]{:S(2)}) collective-permute-start(f32[12,128,128]{2,1,0:T(8,128)S(1)} %collective-permute-done.1.refs_2_), channel_id=1, source_target_pairs={{0,4},{4,0},{1,5},{5,1},{2,6},{6,2},{3,7},{7,3},{8,12},{12,8},{9,1... | collective-permute-start | bytes 2359304 | tf_op jit(solution)/shard_map/ppermute | solution.py:218
  128.4 1.9 %collective-permute-start.5 = (f32[12,128,128]{2,1,0:T(8,128)S(1)}, f32[12,128,128]{2,1,0:T(8,128)}, u32[]{:S(2)}, u32[]{:S(2)}) collective-permute-start(f32[12,128,128]{2,1,0:T(8,128)S(1)} %collective-permute-done.2.refs_4_), channel_id=1, source_target_pairs={{0,4},{4,0},{1,5},{5,1},{2,6},{6,2},{3,7},{7,3},{8,12},{12,8},{9,1... | collective-permute-start | bytes 2359304 | tf_op jit(solution)/shard_map/ppermute | solution.py:218
  130.4 2.4 %collective-permute-start.6 = (f32[12,128,128]{2,1,0:T(8,128)S(1)}, f32[12,128,128]{2,1,0:T(8,128)}, u32[]{:S(2)}, u32[]{:S(2)}) collective-permute-start(f32[12,128,128]{2,1,0:T(8,128)S(1)} %collective-permute-done.3.refs_6_), channel_id=1, source_target_pairs={{0,4},{4,0},{1,5},{5,1},{2,6},{6,2},{3,7},{7,3},{8,12},{12,8},{9,1... | collective-permute-start | bytes 2359304 | tf_op jit(solution)/shard_map/ppermute | solution.py:218
  132.8 1.6 broadcast_in_dim.43
  134.3 3.4 %all-to-all-start.4 = ((f32[4,16,8,128]{3,2,1,0:T(8,128)}), f32[4,16,8,128]{3,2,1,0:T(8,128)S(1)}, u32[]{:S(2)}, u32[]{:S(2)}) async-start(f32[4,16,8,128]{3,2,1,0:T(8,128)} %broadcast_in_dim.43), calls=%async_computation.4 | async-start | bytes 524288 | tf_op jit(solution)/shard_map/all_to_all | solution.py:214
  137.8 6.8 %all-to-all-done.4.tops_ref = f32[4,16,8,128]{3,2,1,0:T(8,128)S(1)} async-done(((f32[4,16,8,128]{3,2,1,0:T(8,128)}), f32[4,16,8,128]{3,2,1,0:T(8,128)S(1)}, u32[]{:S(2)}, u32[]{:S(2)}) %all-to-all-start.4) | async-done | bytes 262176 | tf_op jit(solution)/shard_map/all_to_all | solution.py:214
  145.3 5.9 %all-to-all-start.6 = ((f32[8,32,128]{2,1,0:T(8,128)}), f32[8,32,128]{2,1,0:T(8,128)S(1)}, u32[]{:S(2)}, u32[]{:S(2)}) async-start(f32[8,32,128]{2,1,0:T(8,128)} %broadcast_in_dim.44), calls=%async_computation.6 | async-start | bytes 262144 | tf_op jit(solution)/shard_map/all_to_all | solution.py:214
  151.3 10.9 %leaf_backward.1 = f32[8,3,16,128]{3,2,1,0:T(8,128)} custom-call(s32[8,12]{1,0:T(8,128)} %bitcast.39, f32[4,16,8,128]{3,2,1,0:T(8,128)} %copy-done.4, f32[12,128,128]{2,1,0:T(8,128)} %bitcast.28, f32[12,128,128]{2,1,0:T(8,128)} %copy-done.3, f32[12,128,128]{2,1,0:T(8,128)} %copy-done.5, f32[12,128,128]{2,1,0:T(8,128)} %collective-permute-done.4.refs_3_, ...), custom_call_target="tpu_custom_call" | custom-call | tf_op jit(solution)/shard_map/leaf_backward/pallas_call | solution.py:173
  162.2 4.8 %all-to-all-start.5 = ((f32[8,3,16,128]{3,2,1,0:T(8,128)}), f32[8,3,16,128]{3,2,1,0:T(8,128)S(1)}, u32[]{:S(2)}, u32[]{:S(2)}) async-start(f32[8,3,16,128]{3,2,1,0:T(8,128)} %leaf_backward.1), calls=%async_computation.5 | async-start | bytes 393216 | tf_op jit(solution)/shard_map/all_to_all | solution.py:277
  167.8 5.1 %all-to-all-done.5.got_ref = f32[8,3,16,128]{3,2,1,0:T(8,128)S(1)} async-done(((f32[8,3,16,128]{3,2,1,0:T(8,128)}), f32[8,3,16,128]{3,2,1,0:T(8,128)S(1)}, u32[]{:S(2)}, u32[]{:S(2)}) %all-to-all-start.5) | async-done | bytes 196640 | tf_op jit(solution)/shard_map/all_to_all | solution.py:277
  173.6 1.8 arrange.1
  (51 shorter events, 6.5 us)
Async XLA Ops:
  7.2 42.7 %copy-start = (f32[1,128,256]{2,1,0:T(8,128)S(1)}, f32[1,128,256]{2,1,0:T(8,128)}, u32[]{:S(2)}) copy-start(f32[1,128,256]{2,1,0:T(8,128)} %param.13) | copy-start | bytes 393220
  7.2 106.2 %all-gather.3.cloned.1.call-start = ((), (), s32[]{:S(2)}) async-start(), calls=%async_computation.7 | async-start | bytes 2228224 | tf_op jit(solution)/shard_map/all_gather | solution.py:239
  9.0 25.3 %collective-permute-start = (f32[12,128,128]{2,1,0:T(8,128)}, f32[12,128,128]{2,1,0:T(8,128)S(1)}, u32[]{:S(2)}, u32[]{:S(2)}) collective-permute-start(f32[12,128,128]{2,1,0:T(8,128)} %bitcast.26), channel_id=1, source_target_pairs={{0,4},{4,0},{1,5},{5,1},{2,6},{6,2},{3,7},{7,3},{8,12},{12,8},{9,1... | collective-permute-start | bytes 2359304 | tf_op jit(solution)/shard_map/ppermute | solution.py:218
  32.8 1.5 copy-start.1
  34.3 0.9 copy-start.3
  46.1 22.4 %copy-start.2 = (f32[12,1,128,128]{3,2,1,0:T(8,128)S(1)}, f32[12,1,128,128]{3,2,1,0:T(8,128)}, u32[]{:S(2)}) copy-start(f32[12,1,128,128]{3,2,1,0:T(8,128)} %param.11) | copy-start | bytes 2359300
  46.1 22.2 %all-to-all-start = ((f32[16,16,8,128]{3,2,1,0:T(8,128)}), f32[16,16,8,128]{3,2,1,0:T(8,128)S(1)}, u32[]{:S(2)}, u32[]{:S(2)}) async-start(f32[16,16,8,128]{3,2,1,0:T(8,128)} %get-tuple-element.22), calls=%async_computation | async-start | bytes 2097152 | tf_op jit(solution)/shard_map/all_to_all | solution.py:251
  68.4 51.3 %collective-permute-start.1 = (f32[12,128,128]{2,1,0:T(8,128)S(1)}, f32[12,128,128]{2,1,0:T(8,128)S(1)}, u32[]{:S(2)}, u32[]{:S(2)}) collective-permute-start(f32[12,128,128]{2,1,0:T(8,128)S(1)} %bitcast.29), channel_id=1, source_target_pairs={{0,24},{8,0},{16,8},{24,16},{1,25},{9,1},{17,9},{25,17},{2,26},{10... | collective-permute-start | bytes 2359304 | tf_op jit(solution)/shard_map/ppermute | solution.py:223
  71.4 48.3 %collective-permute-start.2 = (f32[12,128,128]{2,1,0:T(8,128)S(1)}, f32[12,128,128]{2,1,0:T(8,128)S(1)}, u32[]{:S(2)}, u32[]{:S(2)}) collective-permute-start(f32[12,128,128]{2,1,0:T(8,128)S(1)} %bitcast.30), channel_id=1, source_target_pairs={{0,16},{8,24},{16,0},{24,8},{1,17},{9,25},{17,1},{25,9},{2,18},{10... | collective-permute-start | bytes 2359304 | tf_op jit(solution)/shard_map/ppermute | solution.py:223
  73.9 45.8 %collective-permute-start.3 = (f32[12,128,128]{2,1,0:T(8,128)S(1)}, f32[12,128,128]{2,1,0:T(8,128)S(1)}, u32[]{:S(2)}, u32[]{:S(2)}) collective-permute-start(f32[12,128,128]{2,1,0:T(8,128)S(1)} %bitcast.31), channel_id=1, source_target_pairs={{0,8},{8,16},{16,24},{24,0},{1,9},{9,17},{17,25},{25,1},{2,10},{10... | collective-permute-start | bytes 2359304 | tf_op jit(solution)/shard_map/ppermute | solution.py:223
  119.7 31.5 %copy-start.5 = (f32[12,128,128]{2,1,0:T(8,128)}, f32[12,128,128]{2,1,0:T(8,128)S(1)}, u32[]{:S(2)}) copy-start(f32[12,128,128]{2,1,0:T(8,128)S(1)} %collective-permute-done.1.refs_2_) | copy-start | bytes 2359300
  119.7 31.5 %copy-start.6 = (f32[12,128,128]{2,1,0:T(8,128)}, f32[12,128,128]{2,1,0:T(8,128)S(1)}, u32[]{:S(2)}) copy-start(f32[12,128,128]{2,1,0:T(8,128)S(1)} %collective-permute-done.2.refs_4_) | copy-start | bytes 2359300
  119.7 31.5 %copy-start.7 = (f32[12,128,128]{2,1,0:T(8,128)}, f32[12,128,128]{2,1,0:T(8,128)S(1)}, u32[]{:S(2)}) copy-start(f32[12,128,128]{2,1,0:T(8,128)S(1)} %collective-permute-done.3.refs_6_) | copy-start | bytes 2359300
  119.7 31.5 %collective-permute-start.4 = (f32[12,128,128]{2,1,0:T(8,128)S(1)}, f32[12,128,128]{2,1,0:T(8,128)}, u32[]{:S(2)}, u32[]{:S(2)}) collective-permute-start(f32[12,128,128]{2,1,0:T(8,128)S(1)} %collective-permute-done.1.refs_2_), channel_id=1, source_target_pairs={{0,4},{4,0},{1,5},{5,1},{2,6},{6,2},{3,7},{7,3},{8,12},{12,8},{9,1... | collective-permute-start | bytes 2359304 | tf_op jit(solution)/shard_map/ppermute | solution.py:218
  128.4 22.8 %collective-permute-start.5 = (f32[12,128,128]{2,1,0:T(8,128)S(1)}, f32[12,128,128]{2,1,0:T(8,128)}, u32[]{:S(2)}, u32[]{:S(2)}) collective-permute-start(f32[12,128,128]{2,1,0:T(8,128)S(1)} %collective-permute-done.2.refs_4_), channel_id=1, source_target_pairs={{0,4},{4,0},{1,5},{5,1},{2,6},{6,2},{3,7},{7,3},{8,12},{12,8},{9,1... | collective-permute-start | bytes 2359304 | tf_op jit(solution)/shard_map/ppermute | solution.py:218
  130.4 20.9 %collective-permute-start.6 = (f32[12,128,128]{2,1,0:T(8,128)S(1)}, f32[12,128,128]{2,1,0:T(8,128)}, u32[]{:S(2)}, u32[]{:S(2)}) collective-permute-start(f32[12,128,128]{2,1,0:T(8,128)S(1)} %collective-permute-done.3.refs_6_), channel_id=1, source_target_pairs={{0,4},{4,0},{1,5},{5,1},{2,6},{6,2},{3,7},{7,3},{8,12},{12,8},{9,1... | collective-permute-start | bytes 2359304 | tf_op jit(solution)/shard_map/ppermute | solution.py:218
  134.3 10.2 %all-to-all-start.4 = ((f32[4,16,8,128]{3,2,1,0:T(8,128)}), f32[4,16,8,128]{3,2,1,0:T(8,128)S(1)}, u32[]{:S(2)}, u32[]{:S(2)}) async-start(f32[4,16,8,128]{3,2,1,0:T(8,128)} %broadcast_in_dim.43), calls=%async_computation.4 | async-start | bytes 524288 | tf_op jit(solution)/shard_map/all_to_all | solution.py:214
  144.5 6.7 %copy-start.4 = (f32[4,16,8,128]{3,2,1,0:T(8,128)}, f32[4,16,8,128]{3,2,1,0:T(8,128)S(1)}, u32[]{:S(2)}) copy-start(f32[4,16,8,128]{3,2,1,0:T(8,128)S(1)} %all-to-all-done.4.tops_ref) | copy-start | bytes 786436
  145.3 16.9 %all-to-all-start.6 = ((f32[8,32,128]{2,1,0:T(8,128)}), f32[8,32,128]{2,1,0:T(8,128)S(1)}, u32[]{:S(2)}, u32[]{:S(2)}) async-start(f32[8,32,128]{2,1,0:T(8,128)} %broadcast_in_dim.44), calls=%async_computation.6 | async-start | bytes 262144 | tf_op jit(solution)/shard_map/all_to_all | solution.py:214
  162.2 10.7 %all-to-all-start.5 = ((f32[8,3,16,128]{3,2,1,0:T(8,128)}), f32[8,3,16,128]{3,2,1,0:T(8,128)S(1)}, u32[]{:S(2)}, u32[]{:S(2)}) async-start(f32[8,3,16,128]{3,2,1,0:T(8,128)} %leaf_backward.1), calls=%async_computation.5 | async-start | bytes 393216 | tf_op jit(solution)/shard_map/all_to_all | solution.py:277
  172.9 0.7 copy-start.8
Sparse Core Ops, SparseCore 0:
  10.7 69.5 all-gather.2

commit v3 on v2

v3 whole, which is shorter than its diff:
```python
import jax
import jax.numpy as jnp
from jax import lax
from jax.experimental import pallas as pl
from jax.experimental.pallas import tpu as pltpu
from jax.sharding import Mesh, PartitionSpec as P

F32 = jnp.float32
BF16 = jnp.bfloat16
ROWS = ("rhi", "rlo")
COLS = ("y", "core")
STEP = 4


def dot(a, b, cb=0):
    return lax.dot_general(a, b, (((1,), (cb,)), ((), ())), preferred_element_type=F32)


def split(x):
    high = x.astype(BF16)
    low = (x - high.astype(F32)).astype(BF16)
    return high, low


def dot3(a, b, cb=0):
    ah, al = split(a)
    bh, bl = split(b)
    both = dot(
        jnp.concatenate([ah, al], axis=1), jnp.concatenate([bh, bh], axis=cb), cb
    )
    return both + dot(ah, bl, cb)


def row_dot(x, matrix, cb=0):
    n = x.shape[0]
    m = matrix.shape[1 - cb]
    rows = jnp.concatenate(split(x), axis=0)
    r = dot(rows, jnp.concatenate(split(matrix), axis=1 - cb), cb)
    return (r[:n, :m] + (r[n:, :m] + r[:n, m:])) + r[n:, m:]


def whole(shape):
    return pl.BlockSpec(shape, lambda *_: (0,) * len(shape))


def leaf_forward_kernel(place_ref, targets_ref, inv_ref, mine_ref, pair_ref, known_ref, sums_ref, own_ref, stage):
    step = pl.program_id(0)
    count, b = mine_ref.shape[:2]
    own = own_ref.shape[1]

    @pl.when(step == 0)
    def _():
        sums_ref[...] = jnp.zeros_like(sums_ref)

    for i in range(count):
        inv = inv_ref[:, i].reshape(b, b)
        forward = dot3(known_ref[i].T, inv, 1)
        update = dot3(forward, jnp.concatenate([mine_ref[i], pair_ref[i]], axis=0), 1)
        for k in range(2):
            t = targets_ref[k, step * count + i]
            for q in range(sums_ref.shape[0]):
                sums_ref[q, t] += update[8 * q : 8 * q + 8, k * b : (k + 1) * b]
        stage[i] = forward
        own_ref[i] = stage[i, pl.ds(pl.multiple_of(place_ref[1] * own, own), own), :]


def leaf_forward(place, targets, inv, mine, pair, known, tops):
    leaves, b, r = known.shape
    n_cols, _, slab, _ = inv.shape
    half = r // 2
    own = r // n_cols
    block = pl.BlockSpec((STEP, b, b), lambda i, *_: (i, 0, 0))
    return pl.pallas_call(
        leaf_forward_kernel,
        grid_spec=pltpu.PrefetchScalarGridSpec(
            num_scalar_prefetch=2,
            grid=(leaves // STEP,),
            in_specs=[
                pl.BlockSpec((n_cols, STEP, slab, b), lambda i, *_: (0, i, 0, 0)),
                block,
                block,
                pl.BlockSpec((STEP, b, half), lambda i, place, _: (i, 0, place[0])),
            ],
            out_specs=[
                whole((half // 8, tops, 8, b)),
                pl.BlockSpec((STEP, own, b), lambda i, *_: (i, 0, 0)),
            ],
            scratch_shapes=[pltpu.VMEM((STEP, half, b), F32)],
        ),
        out_shape=[
            jax.ShapeDtypeStruct((half // 8, tops, 8, b), F32),
            jax.ShapeDtypeStruct((leaves, own, b), F32),
        ],
        name="leaf_forward",
    )(place, targets, inv, mine, pair, known)


def top_map_kernel(inv_ref, sub_ref, out_ref):
    out_ref[0] = inv_ref[0]
    out_ref[1] = -lax.dot_general(
        inv_ref[0],
        sub_ref[0],
        (((1,), (0,)), ((), ())),
        precision=lax.Precision.HIGHEST,
        preferred_element_type=F32,
    )


def top_map(inv, sub):
    return pl.pallas_call(
        top_map_kernel,
        out_shape=jax.ShapeDtypeStruct((2,) + inv.shape[1:], F32),
        name="top_map",
    )(inv, sub)


def top_chain_kernel(rhs_ref, maps_ref, out_ref):
    low, layers, high, n, b = rhs_ref.shape
    tops = low * high

    def rhs(t):
        return rhs_ref[t // high, :, t % high].reshape(layers * n, b)

    def maps(t, kind):
        return maps_ref[t % low, t // low, kind]

    solved = []
    current = row_dot(rhs(0), maps(0, 0), 1)
    solved.append(current)
    for t in range(1, tops):
        current = row_dot(rhs(t), maps(t, 0), 1) + row_dot(current, maps(t, 1), 1)
        solved.append(current)
    rest = solved[tops - 1]
    out_ref[tops - 1] = row_dot(rest, maps(tops - 1, 0))
    for t in range(tops - 2, -1, -1):
        rest = solved[t] + row_dot(rest, maps(t + 1, 1))
        out_ref[t] = row_dot(rest, maps(t, 0))


def top_chain(rhs, maps):
    low, layers, high, n, b = rhs.shape
    return pl.pallas_call(
        top_chain_kernel,
        out_shape=jax.ShapeDtypeStruct((low * high, layers * n, b), F32),
        name="top_chain",
    )(rhs, maps)


def leaf_backward_kernel(row_ref, targets_ref, tops_ref, blocks_ref, own_ref, inv_ref, out_ref, parts):
    step = pl.program_id(0)
    n_cols, count, b, _ = blocks_ref.shape
    own = own_ref.shape[1]
    slab = b // n_cols
    leaf_rows = out_ref.shape[1] - own

    @pl.when(step == 0)
    def _():
        for t in range(parts.shape[0]):
            high, low = split(tops_ref[t])
            parts[t, :own] = high
            parts[t, own:] = low
        for c in range(n_cols):
            out_ref[c, leaf_rows:] = tops_ref[row_ref[0]]

    results = []
    for i in range(count):
        leaf = step * count + i
        both = jnp.concatenate([parts[targets_ref[p, leaf]] for p in range(n_cols)], axis=1)
        high, low = split(blocks_ref[:, i].reshape(n_cols * b, b))
        r = dot(both, high)
        left = own_ref[i] - ((r[:own] + r[own:]) + dot(both[:own], low))
        results.append(dot3(left, inv_ref[:, i].reshape(b, b)))
    turned = jnp.concatenate(results, axis=0).T
    for c in range(n_cols):
        out_ref[c, pl.ds(pl.multiple_of(step * slab, slab), slab)] = turned[
            c * slab : (c + 1) * slab
        ]


def leaf_backward(row, targets, tops, blocks, own, inv):
    n_cols, leaves, b, _ = blocks.shape
    mine = own.shape[1]
    slab = b // n_cols
    step = b // mine
    out = (n_cols, leaves // step * slab + mine, b)
    return pl.pallas_call(
        leaf_backward_kernel,
        grid_spec=pltpu.PrefetchScalarGridSpec(
            num_scalar_prefetch=2,
            grid=(leaves // step,),
            in_specs=[
                whole(tops.shape),
                pl.BlockSpec((n_cols, step, b, b), lambda i, *_: (0, i, 0, 0)),
                pl.BlockSpec((step, mine, b), lambda i, *_: (i, 0, 0)),
                pl.BlockSpec((n_cols, step, slab, b), lambda i, *_: (0, i, 0, 0)),
            ],
            out_specs=whole(out),
            scratch_shapes=[pltpu.VMEM((tops.shape[0], 2 * mine, b), BF16)],
        ),
        out_shape=jax.ShapeDtypeStruct(out, F32),
        name="leaf_backward",
    )(row, targets, tops, blocks, own, inv)


def arrange_kernel(got_ref, leaf_ref, top_ref):
    n_cols, _, b = got_ref.shape
    leaves, slab, r = leaf_ref.shape
    own = r // n_cols
    step = b // own
    groups = leaves // step
    for h in range(2):
        for g in range(groups):
            for i in range(step):
                leaf_ref[g * step + i, :, h * b : (h + 1) * b] = jnp.concatenate(
                    [
                        got_ref[2 * q + h, g * slab : (g + 1) * slab, i * own : (i + 1) * own]
                        for q in range(step)
                    ],
                    axis=1,
                )
        top_ref[0, :, h * b : (h + 1) * b] = jnp.concatenate(
            [got_ref[2 * q + h, groups * slab :] for q in range(step)], axis=0
        ).T


def arrange(got, leaves, r):
    n_cols, _, b = got.shape
    return pl.pallas_call(
        arrange_kernel,
        out_shape=[
            jax.ShapeDtypeStruct((leaves, b // n_cols, r), F32),
            jax.ShapeDtypeStruct((1, b, r), F32),
        ],
        name="arrange",
    )(got)


def spread(x, axis):
    n = lax.axis_size(axis)
    return lax.all_to_all(jnp.broadcast_to(x, (n,) + x.shape), axis, 0, 0, tiled=True)


def from_core(x):
    return lax.ppermute(x, "core", [(0, 1), (1, 0)])


def on_device(known, pivot, leaf_blocks, leaf_target, top_rhs, top_inv, top_sub):
    leaves, b, r = known.shape
    n_y = lax.axis_size("y")
    n_cols = 2 * n_y
    tops = lax.axis_size(ROWS)
    y = lax.axis_index("y")
    core = lax.axis_index("core")
    row = lax.axis_index(ROWS)
    blocks = leaf_blocks[:, 0]
    slab = pivot.shape[1]
    own = r // n_cols

    all_blocks = lax.all_gather(blocks, COLS, axis=0, tiled=False)
    paired = from_core(blocks)
    named = jnp.zeros((1, slab, b), F32).at[0, 0, :leaves].set(leaf_target[:, 0].astype(F32))
    inv = spread(jnp.concatenate([pivot, named]), COLS)
    targets = inv[:, leaves, 0, :leaves].astype(jnp.int32)
    two = jnp.stack([leaf_target[:, 0], lax.dynamic_index_in_dim(targets, 2 * y + 1 - core, 0, False)])

    sums, own_forward = leaf_forward(jnp.stack([core, y]), two, inv, blocks, paired, known, tops)
    arrived = lax.all_to_all(sums, ("y", "layers"), 0, 0, tiled=True)
    own_map = top_map(top_inv, top_sub)

    own_map, sums = lax.optimization_barrier((own_map, sums))
    some_maps = lax.all_gather(own_map, "rhi", axis=0, tiled=False)
    arrived, some_maps, all_blocks = lax.optimization_barrier((arrived, some_maps, all_blocks))
    maps = lax.all_gather(some_maps, "rlo", axis=0, tiled=False)

    start = core * (r // 2) + y * own + lax.axis_index("layers") * 8
    rhs_t = lax.dynamic_slice_in_dim(top_rhs[0], start, 8, 1).T
    mine = (jnp.arange(tops) == row)[:, None, None]
    partial = jnp.where(mine, rhs_t[None], 0.0) - arrived.sum(0)

    quarter = lax.all_to_all(partial, "rlo", 0, 0, tiled=True)
    quarter = quarter.reshape((lax.axis_size("rlo"), -1) + quarter.shape[1:]).sum(0)
    quarter = spread(quarter, "rhi").sum(0)
    rhs = spread(quarter, ("rlo", "layers"))
    rhs = rhs.reshape((lax.axis_size("rlo"), -1) + rhs.shape[1:])

    own_tops = top_chain(rhs, maps)
    turned = leaf_backward(row[None], targets, own_tops, all_blocks, own_forward, inv)
    got = lax.all_to_all(turned, COLS, 0, 0, tiled=True)
    return tuple(arrange(got, leaves, r))


def solution(mesh):
    rows = mesh.shape["rows"]
    low = 4
    fine = Mesh(
        mesh.devices.reshape(
            rows // low, low, mesh.shape["cols"] // 2, 2, mesh.shape["layers"]
        ),
        ROWS + COLS + ("layers",),
    )
    held = ROWS + ("layers",)
    in_specs = (
        P(held, None, None),
        P(held, COLS, None),
        P(held, COLS, None, None),
        P(held, COLS),
        P(ROWS, None, None),
        P(ROWS, None, None),
        P(ROWS, None, None),
    )
    out_specs = (P(held, COLS, None), P(ROWS, None, None))
    return jax.shard_map(
        on_device, mesh=fine, in_specs=in_specs, out_specs=out_specs, check_vma=False
    )
```

time: 184 us -> 175 us (0.951)
  blocking collectives: 51 us -> 89.2 us
  starting transfers between devices: 47.2 us -> 16.1 us
  Pallas kernels: 31.6 us -> 23.1 us
  waiting for transfers between devices: 30.2 us -> 26.3 us
  local copies, waits for them, and re-layouts: 4.83 us -> 2.34 us
    all_to_all x2 -> x3, blocking collectives: 30.2 us -> 53.5 us  [the longest x2 40.7 us: spread(): lax.all_to_all(jnp.broadcast_to(x, (n,) + x.shape), axis, 0, 0, tiled=True)]
    ppermute x4 -> x1, starting transfers between devices: 21.8 us -> 2.02 us  [from_core(): return lax.ppermute(x, 'core', [(0, 1), (1, 0)])]
    all_to_all x1, waiting for transfers between devices: 18.2 us -> 0.01 us  [on_device(): arrived = lax.all_to_all(sums, ('y', 'layers'), 0, 0, tiled=True)]
    all_gather x1 -> x2, waiting for transfers between devices: 0.01 us -> 15.2 us  [the longest x1 13.2 us: on_device(): maps = lax.all_gather(some_maps, 'rlo', axis=0, tiled=False)]
    all_gather x1, blocking collectives: 13.5 us -> 26.8 us  [on_device(): some_maps = lax.all_gather(own_map, 'rhi', axis=0, tiled=False)]
    ppermute x3 -> x0, starting transfers between devices: 7.43 us -> none  [from_y(): return lax.ppermute(x, 'y', [(i, (i - step) % n) for i in range(n)])]
    pallas_call x1, Pallas kernels: 10.8 us -> 5.83 us  [leaf_forward(): pl.pallas_call(leaf_forward_kernel, grid_spec=pltpu.PrefetchScalarGridSpe...]
    pallas_call x1, Pallas kernels: 10.9 us -> 6.87 us  [leaf_backward(): pl.pallas_call(leaf_backward_kernel, grid_spec=pltpu.PrefetchScalarGridSp...]
  transfers between devices with their start and end apart: 12 -> 5, of which waited for: 3 -> 3; matrix products, arithmetic and copies ran while one was open for 3% -> 2% of each run, Pallas kernels for 15% -> 4%
where the time goes in v3:
time: 175 us; the launch traced here: 174 us
  blocking collectives  89.2 us (51%)
  waiting for transfers between devices  26.3 us (15%)
  Pallas kernels  23.1 us (13%)
  starting transfers between devices  16.1 us (9%)
  between operations  14.2 us (8%)
  other arithmetic  2.94 us (2%)
  local copies, waits for them, and re-layouts  2.34 us (1%)
    all_to_all x2, blocking collectives, spread(): lax.all_to_all(jnp.broadcast_to(x, (n,) + x.shape), axis, 0, 0, tiled=True)  40.7 us
    all_gather x1, blocking collectives, on_device(): some_maps = lax.all_gather(own_map, 'rhi', axis=0, tiled=False)  26.8 us
    all_gather x1, waiting for transfers between devices, on_device(): maps = lax.all_gather(some_maps, 'rlo', axis=0, tiled=False)  13.2 us
    all_to_all x1, blocking collectives, on_device(): got = lax.all_to_all(turned, COLS, 0, 0, tiled=True)  12.8 us
    all_to_all x1, waiting for transfers between devices, spread(): lax.all_to_all(jnp.broadcast_to(x, (n,) + x.shape), axis, 0, 0, tiled=True)  10.4 us
    all_to_all x1, starting transfers between devices, spread(): lax.all_to_all(jnp.broadcast_to(x, (n,) + x.shape), axis, 0, 0, tiled=True)  10.3 us
    all_to_all x1, blocking collectives, on_device(): quarter = lax.all_to_all(partial, 'rlo', 0, 0, tiled=True)  8.92 us
    pallas_call x1, Pallas kernels, leaf_backward(): pl.pallas_call(leaf_backward_kernel, grid_spec=pltpu.PrefetchScalarGridSp...  6.87 us
  transfers between devices with their start and end apart: 5, of which 3 were waited for; matrix products, arithmetic and copies ran while one was open for 2% of the time, Pallas kernels for 4%

profile of v3, /device:TPU:1, one launch (start us, length us, event | category | flops | bytes accessed | tf_op | source)
XLA Modules:
  0.0 174.2 jit_solution(8410089557049518722)
XLA Ops:
  7.2 0.7 all-gather.6.cloned.1.call-update
  7.9 0.7 convert_bitcast_fusion
  8.6 0.9 select_maximum_fusion
  9.5 1.0 broadcast_in_dim.36
  10.5 10.3 %all-to-all-start = ((f32[8,13,16,128]{3,2,1,0:T(8,128)}), f32[8,13,16,128]{3,2,1,0:T(8,128)S(1)}, u32[]{:S(2)}, u32[]{:S(2)}) async-start(f32[8,13,16,128]{3,2,1,0:T(8,128)} %broadcast_in_dim.36), calls=%async_computation | async-start | bytes 1703936 | tf_op jit(solution)/shard_map/all_to_all | solution.py:240
  20.8 2.0 %collective-permute-start = (f32[12,128,128]{2,1,0:T(8,128)S(1)}, f32[12,128,128]{2,1,0:T(8,128)S(1)}, u32[]{:S(2)}, u32[]{:S(2)}) collective-permute-start(f32[12,128,128]{2,1,0:T(8,128)S(1)} %bitcast.20), channel_id=1, source_target_pairs={{0,4},{4,0},{1,5},{5,1},{2,6},{6,2},{3,7},{7,3},{8,12},{12,8},{9,1... | collective-permute-start | bytes 2359304 | tf_op jit(solution)/shard_map/ppermute | solution.py:244
  22.8 0.6 pad_add_fusion.1.place_ref
  23.4 10.4 %all-to-all-done.inv_ref = f32[8,13,16,128]{3,2,1,0:T(8,128)S(1)} async-done(((f32[8,13,16,128]{3,2,1,0:T(8,128)}), f32[8,13,16,128]{3,2,1,0:T(8,128)S(1)}, u32[]{:S(2)}, u32[]{:S(2)}) %all-to-all-start) | async-done | bytes 852000 | tf_op jit(solution)/shard_map/all_to_all | solution.py:240
  33.9 0.6 pad_add_fusion.targets_ref
  34.5 0.3 copy-done.1
  34.8 0.9 copy-done.3
  35.7 5.8 %leaf_forward.1 = (f32[16,16,8,128]{3,2,1,0:T(8,128)}, f32[12,32,128]{2,1,0:T(8,128)}) custom-call(s32[2]{0:T(128)} %pad_add_fusion.1.place_ref, s32[2,12]{1,0:T(2,128)} %pad_add_fusion.targets_ref, f32[8,13,16,128]{3,2,1,0:T(8,128)} %copy-done.1, f32[12,128,128]{2,1,0:T(8,128)} %bitcast.19, f32[12,128,128]{2,1,0:T(8,128)} %copy-done.3, ...), custom_call_target="tpu_custom_call" | custom-call | tf_op jit(solution)/shard_map/leaf_forward/pallas_call | solution.py:73
  41.5 3.7 %all-to-all-start.1 = ((f32[16,16,8,128]{3,2,1,0:T(8,128)}), f32[16,16,8,128]{3,2,1,0:T(8,128)S(1)}, u32[]{:S(2)}, u32[]{:S(2)}) async-start(f32[16,16,8,128]{3,2,1,0:T(8,128)} %get-tuple-element.20), calls=%async_computation.1 | async-start | bytes 2097152 | tf_op jit(solution)/shard_map/all_to_all | solution.py:267
  45.2 1.7 top_map.1
  47.0 26.8 %all-gather = f32[8,128,128]{2,1,0:T(8,128)} all-gather(f32[2,128,128]{2,1,0:T(8,128)} %top_map.1), channel_id=2, replica_groups=mesh['rhi'=4,'rlo'=4,'y'=4,'core'=2,'layers'=4] {'rhi'}, dimensions={0}, use_global_device_ids=true | all-gather | bytes 655360 | tf_op jit(solution)/shard_map/all_gather | solution.py:271
  73.8 2.0 %all-gather.6.cloned.1.call-done = f32[96,1,128,128]{3,2,1,0:T(8,128)} async-done(((f32[12,1,128,128]{3,2,1,0:T(8,128)}), f32[96,1,128,128]{3,2,1,0:T(8,128)}) %all-gather.6.cloned.1.call-update) | async-done | bytes 6291472 | tf_op jit(solution)/shard_map/all_gather | solution.py:259
  76.1 8.9 %all_to_all.30 = f32[16,8,128]{2,1,0:T(8,128)S(1)} all-to-all(f32[16,8,128]{2,1,0:T(8,128)S(1)} %select_subtract_fusion), channel_id=1, replica_groups=mesh['rhi'=4,'rlo'=4,'y'=4,'core'=2,'layers'=4] {'rlo'}, dimensions={0} | all-to-all | bytes 131072 | tf_op jit(solution)/shard_map/all_to_all | solution.py:280
  85.1 21.8 %all_to_all.31 = f32[4,4,8,128]{3,2,1,0:T(8,128)S(1)} all-to-all(f32[4,4,8,128]{3,2,1,0:T(8,128)S(1)} %broadcast_in_dim.40), channel_id=1, replica_groups=mesh['rhi'=4,'rlo'=4,'y'=4,'core'=2,'layers'=4] {'rhi'}, dimensions={0} | all-to-all | bytes 131072 | tf_op jit(solution)/shard_map/all_to_all | solution.py:240
  106.9 18.9 %all_to_all.32 = f32[16,4,8,128]{3,2,1,0:T(8,128)} all-to-all(f32[16,4,8,128]{3,2,1,0:T(8,128)S(1)} %broadcast_in_dim.41), channel_id=1, replica_groups=mesh['rhi'=4,'rlo'=4,'y'=4,'core'=2,'layers'=4] {'rlo','layers'}, dimensions={0} | all-to-all | bytes 524288 | tf_op jit(solution)/shard_map/all_to_all | solution.py:240
  125.8 13.2 %all-gather.8.cloned.1.call-done = f32[16,2,128,128]{3,2,1,0:T(8,128)} async-done(((f32[4,2,128,128]{3,2,1,0:T(8,128)}), f32[16,2,128,128]{3,2,1,0:T(8,128)}) %all-gather.8.cloned.1.call-update) | async-done | bytes 2097168 | tf_op jit(solution)/shard_map/all_gather | solution.py:273
  138.9 6.8 %top_chain.1.tops_ref = f32[16,32,128]{2,1,0:T(8,128)} custom-call(f32[4,4,4,8,128]{4,3,2,1,0:T(8,128)} %bitcast.23, f32[4,4,2,128,128]{4,3,2,1,0:T(8,128)} %bitcast.21), custom_call_target="tpu_custom_call" | custom-call | tf_op jit(solution)/shard_map/top_chain/pallas_call | solution.py:142
  145.7 6.9 %leaf_backward.1 = f32[8,80,128]{2,1,0:T(8,128)} custom-call(s32[1]{0:T(128)} %bitcast.row_ref, s32[8,12]{1,0:T(8,128)} %bitcast.25, f32[16,32,128]{2,1,0:T(8,128)} %top_chain.1.tops_ref, f32[8,12,128,128]{3,2,1,0:T(8,128)} %bitcast.18, f32[12,32,128]{2,1,0:T(8,128)} %get-tuple-element.25.own_ref, f32[8,13,16,128]{3,2,1,0:T(8,128)} %copy-done.1), custom_call_target="tpu_custom_call" | custom-call | tf_op jit(solution)/shard_map/leaf_backward/pallas_call | solution.py:186
  152.6 12.8 %all_to_all.33.got_ref = f32[8,80,128]{2,1,0:T(8,128)} all-to-all(f32[8,80,128]{2,1,0:T(8,128)} %leaf_backward.1), channel_id=1, replica_groups=mesh['rhi'=4,'rlo'=4,'y'=4,'core'=2,'layers'=4] {'y','core'}, dimensions={0} | all-to-all | bytes 655360 | tf_op jit(solution)/shard_map/all_to_all | solution.py:288
  165.4 1.9 %arrange.1 = (f32[12,16,256]{2,1,0:T(8,128)}, f32[1,128,256]{2,1,0:T(8,128)}) custom-call(f32[8,80,128]{2,1,0:T(8,128)} %all_to_all.33.got_ref), custom_call_target="tpu_custom_call" | custom-call | tf_op jit(solution)/shard_map/arrange/pallas_call | solution.py:228
  (26 shorter events, 0.5 us)
Async XLA Ops:
  7.2 68.6 %copy-start = (f32[1,128,256]{2,1,0:T(8,128)S(1)}, f32[1,128,256]{2,1,0:T(8,128)}, u32[]{:S(2)}) copy-start(f32[1,128,256]{2,1,0:T(8,128)} %param.13) | copy-start | bytes 393220
  7.2 13.6 %copy-start.2 = (f32[12,1,128,128]{3,2,1,0:T(8,128)S(1)}, f32[12,1,128,128]{3,2,1,0:T(8,128)}, u32[]{:S(2)}) copy-start(f32[12,1,128,128]{3,2,1,0:T(8,128)} %param.11) | copy-start | bytes 2359300
  7.2 26.7 %copy-start.5 = (s32[12,1]{0,1:T(1,128)S(1)}, s32[12,1]{0,1:T(1,128)}, u32[]{:S(2)}) copy-start(s32[12,1]{0,1:T(1,128)} %param.12) | copy-start | bytes 148
  7.2 68.6 %all-gather.6.cloned.1.call-start = ((), (), s32[]{:S(2)}) async-start(), calls=%async_computation.6 | async-start | bytes 7077888 | tf_op jit(solution)/shard_map/all_gather | solution.py:259
  10.5 23.3 %all-to-all-start = ((f32[8,13,16,128]{3,2,1,0:T(8,128)}), f32[8,13,16,128]{3,2,1,0:T(8,128)S(1)}, u32[]{:S(2)}, u32[]{:S(2)}) async-start(f32[8,13,16,128]{3,2,1,0:T(8,128)} %broadcast_in_dim.36), calls=%async_computation | async-start | bytes 1703936 | tf_op jit(solution)/shard_map/all_to_all | solution.py:240
  20.8 13.7 %collective-permute-start = (f32[12,128,128]{2,1,0:T(8,128)S(1)}, f32[12,128,128]{2,1,0:T(8,128)S(1)}, u32[]{:S(2)}, u32[]{:S(2)}) collective-permute-start(f32[12,128,128]{2,1,0:T(8,128)S(1)} %bitcast.20), channel_id=1, source_target_pairs={{0,4},{4,0},{1,5},{5,1},{2,6},{6,2},{3,7},{7,3},{8,12},{12,8},{9,1... | collective-permute-start | bytes 2359304 | tf_op jit(solution)/shard_map/ppermute | solution.py:244
  33.8 1.0 copy-start.1
  33.8 7.7 %copy-start.4 = (s32[8,1,1,12]{3,2,1,0:T(1,128)}, s32[8,1,1,12]{3,2,1,0:T(1,128)S(1)}, u32[]{:S(2)}) copy-start(s32[8,1,1,12]{3,2,1,0:T(1,128)S(1)} %slice_convert_fusion) | copy-start | bytes 1156
  34.8 0.9 copy-start.3
  41.5 32.2 %all-to-all-start.1 = ((f32[16,16,8,128]{3,2,1,0:T(8,128)}), f32[16,16,8,128]{3,2,1,0:T(8,128)S(1)}, u32[]{:S(2)}, u32[]{:S(2)}) async-start(f32[16,16,8,128]{3,2,1,0:T(8,128)} %get-tuple-element.20), calls=%async_computation.1 | async-start | bytes 2097152 | tf_op jit(solution)/shard_map/all_to_all | solution.py:267
  45.2 93.8 %all-gather.8.cloned.1.call-start = ((), (), s32[]{:S(2)}) async-start(), calls=%async_computation.7 | async-start | bytes 2621440 | tf_op jit(solution)/shard_map/all_gather | solution.py:273
Sparse Core Ops, SparseCore 0:
  10.2 65.5 all-gather.5
  77.9 61.0 all-gather.7

commit v4 on v3

--- a/solution.py
+++ b/solution.py
@@ -122,7 +122,7 @@
         return rhs_ref[t // high, :, t % high].reshape(layers * n, b)
 
     def maps(t, kind):
-        return maps_ref[t % low, t // low, kind]
+        return maps_ref[t, kind]
 
     solved = []
     current = row_dot(rhs(0), maps(0, 0), 1)
@@ -146,9 +146,11 @@
     )(rhs, maps)
 
 
-def leaf_backward_kernel(row_ref, targets_ref, tops_ref, blocks_ref, own_ref, inv_ref, out_ref, parts):
+def leaf_backward_kernel(row_ref, targets_ref, tops_ref, *refs):
+    *block_refs, own_ref, inv_ref, out_ref, parts = refs
     step = pl.program_id(0)
-    n_cols, count, b, _ = blocks_ref.shape
+    n_cols = len(block_refs)
+    count, b, _ = block_refs[0].shape
     own = own_ref.shape[1]
     slab = b // n_cols
     leaf_rows = out_ref.shape[1] - own
@@ -166,7 +168,7 @@
     for i in range(count):
         leaf = step * count + i
         both = jnp.concatenate([parts[targets_ref[p, leaf]] for p in range(n_cols)], axis=1)
-        high, low = split(blocks_ref[:, i].reshape(n_cols * b, b))
+        high, low = split(jnp.concatenate([ref[i] for ref in block_refs], axis=0))
         r = dot(both, high)
         left = own_ref[i] - ((r[:own] + r[own:]) + dot(both[:own], low))
         results.append(dot3(left, inv_ref[:, i].reshape(b, b)))
@@ -178,7 +180,8 @@
 
 
 def leaf_backward(row, targets, tops, blocks, own, inv):
-    n_cols, leaves, b, _ = blocks.shape
+    n_cols = len(blocks)
+    leaves, b, _ = blocks[0].shape
     mine = own.shape[1]
     slab = b // n_cols
     step = b // mine
@@ -188,9 +191,9 @@
         grid_spec=pltpu.PrefetchScalarGridSpec(
             num_scalar_prefetch=2,
             grid=(leaves // step,),
-            in_specs=[
-                whole(tops.shape),
-                pl.BlockSpec((n_cols, step, b, b), lambda i, *_: (0, i, 0, 0)),
+            in_specs=[whole(tops.shape)]
+            + [pl.BlockSpec((step, b, b), lambda i, *_: (i, 0, 0))] * n_cols
+            + [
                 pl.BlockSpec((step, mine, b), lambda i, *_: (i, 0, 0)),
                 pl.BlockSpec((n_cols, step, slab, b), lambda i, *_: (0, i, 0, 0)),
             ],
@@ -199,7 +202,7 @@
         ),
         out_shape=jax.ShapeDtypeStruct(out, F32),
         name="leaf_backward",
-    )(row, targets, tops, blocks, own, inv)
+    )(row, targets, tops, *blocks, own, inv)
 
 
 def arrange_kernel(got_ref, leaf_ref, top_ref):
@@ -244,6 +247,11 @@
     return lax.ppermute(x, "core", [(0, 1), (1, 0)])
 
 
+def from_y(x, step):
+    n = lax.axis_size("y")
+    return lax.ppermute(x, "y", [(i, (i - step) % n) for i in range(n)])
+
+
 def on_device(known, pivot, leaf_blocks, leaf_target, top_rhs, top_inv, top_sub):
     leaves, b, r = known.shape
     n_y = lax.axis_size("y")
@@ -256,21 +264,19 @@
     slab = pivot.shape[1]
     own = r // n_cols
 
-    all_blocks = lax.all_gather(blocks, COLS, axis=0, tiled=False)
+    named = jnp.zeros((1, slab, b), F32).at[0, 0, :leaves].set(leaf_target[:, 0].astype(F32))
+    packed = jnp.concatenate([pivot, named])
+    inv = spread(packed, COLS)
+    maps = lax.all_gather(top_map(top_inv, top_sub), ROWS, axis=0, tiled=False)
     paired = from_core(blocks)
-    named = jnp.zeros((1, slab, b), F32).at[0, 0, :leaves].set(leaf_target[:, 0].astype(F32))
-    inv = spread(jnp.concatenate([pivot, named]), COLS)
-    targets = inv[:, leaves, 0, :leaves].astype(jnp.int32)
-    two = jnp.stack([leaf_target[:, 0], lax.dynamic_index_in_dim(targets, 2 * y + 1 - core, 0, False)])
-
-    sums, own_forward = leaf_forward(jnp.stack([core, y]), two, inv, blocks, paired, known, tops)
+    far = [from_y(blocks, step) for step in range(1, n_y)]
+
+    targets = inv[:, leaves, 0, :leaves].astype(jnp.int32).reshape(n_y, 2, leaves)
+    targets = jnp.roll(targets, -y, axis=0)
+    targets = jnp.where(core == 0, targets, targets[:, ::-1]).reshape(n_cols, leaves)
+
+    sums, own_forward = leaf_forward(jnp.stack([core, y]), targets, inv, blocks, paired, known, tops)
     arrived = lax.all_to_all(sums, ("y", "layers"), 0, 0, tiled=True)
-    own_map = top_map(top_inv, top_sub)
-
-    own_map, sums = lax.optimization_barrier((own_map, sums))
-    some_maps = lax.all_gather(own_map, "rhi", axis=0, tiled=False)
-    arrived, some_maps, all_blocks = lax.optimization_barrier((arrived, some_maps, all_blocks))
-    maps = lax.all_gather(some_maps, "rlo", axis=0, tiled=False)
 
     start = core * (r // 2) + y * own + lax.axis_index("layers") * 8
     rhs_t = lax.dynamic_slice_in_dim(top_rhs[0], start, 8, 1).T
@@ -280,6 +286,10 @@
     quarter = lax.all_to_all(partial, "rlo", 0, 0, tiled=True)
     quarter = quarter.reshape((lax.axis_size("rlo"), -1) + quarter.shape[1:]).sum(0)
     quarter = spread(quarter, "rhi").sum(0)
+    quarter, far = lax.optimization_barrier((quarter, far))
+    all_blocks = [blocks, paired]
+    for block in far:
+        all_blocks += [block, from_core(block)]
     rhs = spread(quarter, ("rlo", "layers"))
     rhs = rhs.reshape((lax.axis_size("rlo"), -1) + rhs.shape[1:])
 

time: 175 us -> 165 us (0.943)
  blocking collectives: 89.2 us -> 59.6 us
  starting transfers between devices: 16.1 us -> 39.9 us
  waiting for transfers between devices: 26.3 us -> 16.4 us
  local copies, waits for them, and re-layouts: 2.34 us -> 6.04 us
    all_gather x1 -> x0, blocking collectives: 26.8 us -> none  [on_device(): some_maps = lax.all_gather(own_map, 'rhi', axis=0, tiled=False)]
    all_to_all x2 -> x1, blocking collectives: 40.7 us -> 23.3 us  [spread(): lax.all_to_all(jnp.broadcast_to(x, (n,) + x.shape), axis, 0, 0, tiled=True)]
    all_to_all x1, blocking collectives: 12.8 us -> 29 us  [on_device(): got = lax.all_to_all(turned, COLS, 0, 0, tiled=True)]
    all_gather x2 -> x1, waiting for transfers between devices: 15.2 us -> 0.02 us  [on_device(): maps = lax.all_gather(top_map(top_inv, top_sub), ROWS, axis=0, tiled=False)]
    ppermute x1 -> x4, starting transfers between devices: 2.02 us -> 11.8 us  [from_core(): return lax.ppermute(x, 'core', [(0, 1), (1, 0)])]
    ppermute x0 -> x3, starting transfers between devices: none -> 9.38 us  [from_y(): return lax.ppermute(x, 'y', [(i, (i - step) % n) for i in range(n)])]
    all_to_all x1, waiting for transfers between devices: 0.01 us -> 5.18 us  [on_device(): arrived = lax.all_to_all(sums, ('y', 'layers'), 0, 0, tiled=True)]
    all_to_all x1 -> x2, starting transfers between devices: 10.3 us -> 15 us  [spread(): lax.all_to_all(jnp.broadcast_to(x, (n,) + x.shape), axis, 0, 0, tiled=True)]
  transfers between devices with their start and end apart: 5 -> 11, of which waited for: 3 -> 3; matrix products, arithmetic and copies ran while one was open for 2% -> 5% of each run, Pallas kernels for 4% -> 8%
where the time goes in v4:
time: 165 us; the launch traced here: 164 us
  blocking collectives  59.6 us (36%)
  starting transfers between devices  39.9 us (24%)
  Pallas kernels  23.4 us (14%)
  waiting for transfers between devices  16.4 us (10%)
  between operations  14.3 us (9%)
  local copies, waits for them, and re-layouts  6.04 us (4%)
  other arithmetic  4.53 us (3%)
    all_to_all x1, blocking collectives, on_device(): got = lax.all_to_all(turned, COLS, 0, 0, tiled=True)  29 us
    all_to_all x1, blocking collectives, spread(): lax.all_to_all(jnp.broadcast_to(x, (n,) + x.shape), axis, 0, 0, tiled=True)  23.3 us
    all_to_all x2, starting transfers between devices, spread(): lax.all_to_all(jnp.broadcast_to(x, (n,) + x.shape), axis, 0, 0, tiled=True)  15 us
    ppermute x4, starting transfers between devices, from_core(): return lax.ppermute(x, 'core', [(0, 1), (1, 0)])  11.8 us
    all_to_all x2, waiting for transfers between devices, spread(): lax.all_to_all(jnp.broadcast_to(x, (n,) + x.shape), axis, 0, 0, tiled=True)  10.3 us
    ppermute x3, starting transfers between devices, from_y(): return lax.ppermute(x, 'y', [(i, (i - step) % n) for i in range(n)])  9.38 us
    all_to_all x1, blocking collectives, on_device(): quarter = lax.all_to_all(partial, 'rlo', 0, 0, tiled=True)  7.26 us
    pallas_call x1, Pallas kernels, leaf_backward(): pl.pallas_call(leaf_backward_kernel, grid_spec=pltpu.PrefetchScalarGridSp...  6.91 us
  transfers between devices with their start and end apart: 11, of which 3 were waited for; matrix products, arithmetic and copies ran while one was open for 5% of the time, Pallas kernels for 8%

profile of v4, /device:TPU:1, one launch (start us, length us, event | category | flops | bytes accessed | tf_op | source)
XLA Modules:
  0.0 164.1 jit_solution(6453655838612546763)
XLA Ops:
  7.2 1.8 %top_map.1 = f32[2,128,128]{2,1,0:T(8,128)} custom-call(f32[1,128,128]{2,1,0:T(8,128)} %inv_ref.1, f32[1,128,128]{2,1,0:T(8,128)} %sub_ref.1), custom_call_target="tpu_custom_call" | custom-call | tf_op jit(solution)/shard_map/top_map/pallas_call | solution.py:110
  9.7 0.9 select_maximum_fusion
  10.6 1.0 broadcast_in_dim.36
  11.6 10.3 %all-to-all-start = ((f32[8,13,16,128]{3,2,1,0:T(8,128)}), f32[8,13,16,128]{3,2,1,0:T(8,128)S(1)}, u32[]{:S(2)}, u32[]{:S(2)}) async-start(f32[8,13,16,128]{3,2,1,0:T(8,128)} %broadcast_in_dim.36), calls=%async_computation | async-start | bytes 1703936 | tf_op jit(solution)/shard_map/all_to_all | solution.py:243
  21.9 2.0 %collective-permute-start = (f32[12,128,128]{2,1,0:T(8,128)S(1)}, f32[12,128,128]{2,1,0:T(8,128)S(1)}, u32[]{:S(2)}, u32[]{:S(2)}) collective-permute-start(f32[12,128,128]{2,1,0:T(8,128)S(1)} %bitcast.16), channel_id=1, source_target_pairs={{0,4},{4,0},{1,5},{5,1},{2,6},{6,2},{3,7},{7,3},{8,12},{12,8},{9,1... | collective-permute-start | bytes 2359304 | tf_op jit(solution)/shard_map/ppermute | solution.py:247
  24.6 10.3 %all-to-all-done.inv_ref.refs_9_ = f32[8,13,16,128]{3,2,1,0:T(8,128)S(1)} async-done(((f32[8,13,16,128]{3,2,1,0:T(8,128)}), f32[8,13,16,128]{3,2,1,0:T(8,128)S(1)}, u32[]{:S(2)}, u32[]{:S(2)}) %all-to-all-start) | async-done | bytes 852000 | tf_op jit(solution)/shard_map/all_to_all | solution.py:243
  36.6 6.0 %leaf_forward.1 = (f32[16,16,8,128]{3,2,1,0:T(8,128)}, f32[12,32,128]{2,1,0:T(8,128)}) custom-call(s32[2]{0:T(128)} %pad_add_fusion.place_ref, s32[8,12]{1,0:T(8,128)} %bitcast.23, f32[8,13,16,128]{3,2,1,0:T(8,128)} %copy-done.1, f32[12,128,128]{2,1,0:T(8,128)} %bitcast.14, f32[12,128,128]{2,1,0:T(8,128)} %copy-done.4, f32[12,128,256]{2,1,0:T(8,128)} %known_ref.1), custom_call_target="tpu_custom_call" | custom-call | tf_op jit(solution)/shard_map/leaf_forward/pallas_call | solution.py:73
  42.6 3.7 %all-to-all-start.1 = ((f32[16,16,8,128]{3,2,1,0:T(8,128)}), f32[16,16,8,128]{3,2,1,0:T(8,128)S(1)}, u32[]{:S(2)}, u32[]{:S(2)}) async-start(f32[16,16,8,128]{3,2,1,0:T(8,128)} %get-tuple-element.20), calls=%async_computation.1 | async-start | bytes 2097152 | tf_op jit(solution)/shard_map/all_to_all | solution.py:279
  46.3 4.4 %collective-permute-start.1 = (f32[12,128,128]{2,1,0:T(8,128)S(1)}, f32[12,128,128]{2,1,0:T(8,128)S(1)}, u32[]{:S(2)}, u32[]{:S(2)}) collective-permute-start(f32[12,128,128]{2,1,0:T(8,128)S(1)} %bitcast.17), channel_id=1, source_target_pairs={{0,24},{8,0},{16,8},{24,16},{1,25},{9,1},{17,9},{25,17},{2,26},{10... | collective-permute-start | bytes 2359304 | tf_op jit(solution)/shard_map/ppermute | solution.py:252
  50.7 2.4 %collective-permute-start.2 = (f32[12,128,128]{2,1,0:T(8,128)S(1)}, f32[12,128,128]{2,1,0:T(8,128)S(1)}, u32[]{:S(2)}, u32[]{:S(2)}) collective-permute-start(f32[12,128,128]{2,1,0:T(8,128)S(1)} %bitcast.18), channel_id=1, source_target_pairs={{0,16},{8,24},{16,0},{24,8},{1,17},{9,25},{17,1},{25,9},{2,18},{10... | collective-permute-start | bytes 2359304 | tf_op jit(solution)/shard_map/ppermute | solution.py:252
  53.1 2.5 %collective-permute-start.3 = (f32[12,128,128]{2,1,0:T(8,128)S(1)}, f32[12,128,128]{2,1,0:T(8,128)}, u32[]{:S(2)}, u32[]{:S(2)}) collective-permute-start(f32[12,128,128]{2,1,0:T(8,128)S(1)} %bitcast.19), channel_id=1, source_target_pairs={{0,8},{8,16},{16,24},{24,0},{1,9},{9,17},{17,25},{25,1},{2,10},{10... | collective-permute-start | bytes 2359304 | tf_op jit(solution)/shard_map/ppermute | solution.py:252
  56.4 0.9 copy.12
  57.3 5.2 %all-to-all-done.1 = f32[16,16,8,128]{3,2,1,0:T(8,128)S(1)} async-done(((f32[16,16,8,128]{3,2,1,0:T(8,128)}), f32[16,16,8,128]{3,2,1,0:T(8,128)S(1)}, u32[]{:S(2)}, u32[]{:S(2)}) %all-to-all-start.1) | async-done | bytes 1048608 | tf_op jit(solution)/shard_map/all_to_all | solution.py:279
  63.2 0.9 select_subtract_fusion
  64.1 7.3 %all_to_all.30 = f32[16,8,128]{2,1,0:T(8,128)S(1)} all-to-all(f32[16,8,128]{2,1,0:T(8,128)S(1)} %select_subtract_fusion), channel_id=1, replica_groups=mesh['rhi'=4,'rlo'=4,'y'=4,'core'=2,'layers'=4] {'rlo'}, dimensions={0} | all-to-all | bytes 131072 | tf_op jit(solution)/shard_map/all_to_all | solution.py:286
  71.4 23.3 %all_to_all.31 = f32[4,4,8,128]{3,2,1,0:T(8,128)S(1)} all-to-all(f32[4,4,8,128]{3,2,1,0:T(8,128)S(1)} %broadcast_in_dim.40), channel_id=1, replica_groups=mesh['rhi'=4,'rlo'=4,'y'=4,'core'=2,'layers'=4] {'rhi'}, dimensions={0} | all-to-all | bytes 131072 | tf_op jit(solution)/shard_map/all_to_all | solution.py:243
  96.3 4.7 %all-to-all-start.4 = ((f32[16,4,8,128]{3,2,1,0:T(8,128)}), f32[16,4,8,128]{3,2,1,0:T(8,128)S(1)}, u32[]{:S(2)}, u32[]{:S(2)}) async-start(f32[16,4,8,128]{3,2,1,0:T(8,128)} %broadcast_in_dim.41), calls=%async_computation.4 | async-start | bytes 524288 | tf_op jit(solution)/shard_map/all_to_all | solution.py:243
  101.0 5.5 %collective-permute-start.4 = (f32[12,128,128]{2,1,0:T(8,128)S(1)}, f32[12,128,128]{2,1,0:T(8,128)S(1)}, u32[]{:S(2)}, u32[]{:S(2)}) collective-permute-start(f32[12,128,128]{2,1,0:T(8,128)S(1)} %collective-permute-done.1.refs_2_), channel_id=1, source_target_pairs={{0,4},{4,0},{1,5},{5,1},{2,6},{6,2},{3,7},{7,3},{8,12},{12,8},{9,1... | collective-permute-start | bytes 2359304 | tf_op jit(solution)/shard_map/ppermute | solution.py:247
  106.4 1.9 %collective-permute-start.5 = (f32[12,128,128]{2,1,0:T(8,128)S(1)}, f32[12,128,128]{2,1,0:T(8,128)S(1)}, u32[]{:S(2)}, u32[]{:S(2)}) collective-permute-start(f32[12,128,128]{2,1,0:T(8,128)S(1)} %collective-permute-done.2.refs_4_), channel_id=1, source_target_pairs={{0,4},{4,0},{1,5},{5,1},{2,6},{6,2},{3,7},{7,3},{8,12},{12,8},{9,1... | collective-permute-start | bytes 2359304 | tf_op jit(solution)/shard_map/ppermute | solution.py:247
  108.4 2.4 %collective-permute-start.6 = (f32[12,128,128]{2,1,0:T(8,128)}, f32[12,128,128]{2,1,0:T(8,128)}, u32[]{:S(2)}, u32[]{:S(2)}) collective-permute-start(f32[12,128,128]{2,1,0:T(8,128)} %collective-permute-done.3.refs_6_), channel_id=1, source_target_pairs={{0,4},{4,0},{1,5},{5,1},{2,6},{6,2},{3,7},{7,3},{8,12},{12,8},{9,1... | collective-permute-start | bytes 2359304 | tf_op jit(solution)/shard_map/ppermute | solution.py:247
  111.5 6.7 %top_chain.1.tops_ref = f32[16,32,128]{2,1,0:T(8,128)} custom-call(f32[4,4,4,8,128]{4,3,2,1,0:T(8,128)} %bitcast.21, f32[16,2,128,128]{3,2,1,0:T(8,128)} %bitcast.20), custom_call_target="tpu_custom_call" | custom-call | tf_op jit(solution)/shard_map/top_chain/pallas_call | solution.py:142
  119.4 6.9 %leaf_backward.1 = f32[8,80,128]{2,1,0:T(8,128)} custom-call(s32[1]{0:T(128)} %bitcast.row_ref, s32[8,12]{1,0:T(8,128)} %bitcast.24, f32[16,32,128]{2,1,0:T(8,128)} %top_chain.1.tops_ref, f32[12,128,128]{2,1,0:T(8,128)} %bitcast.15, f32[12,128,128]{2,1,0:T(8,128)} %copy-done.4, f32[12,128,128]{2,1,0:T(8,128)} %copy-done.6, f32[12,128,128]{2,1,0:T(8,128)} %copy-done.8, ...), custom_call_target="tpu_custom_call" | custom-call | tf_op jit(solution)/shard_map/leaf_backward/pallas_call | solution.py:189
  126.3 29.0 %all_to_all.32.got_ref = f32[8,80,128]{2,1,0:T(8,128)} all-to-all(f32[8,80,128]{2,1,0:T(8,128)} %leaf_backward.1), channel_id=1, replica_groups=mesh['rhi'=4,'rlo'=4,'y'=4,'core'=2,'layers'=4] {'y','core'}, dimensions={0} | all-to-all | bytes 655360 | tf_op jit(solution)/shard_map/all_to_all | solution.py:298
  155.3 1.9 %arrange.1 = (f32[12,16,256]{2,1,0:T(8,128)}, f32[1,128,256]{2,1,0:T(8,128)}) custom-call(f32[8,80,128]{2,1,0:T(8,128)} %all_to_all.32.got_ref), custom_call_target="tpu_custom_call" | custom-call | tf_op jit(solution)/shard_map/arrange/pallas_call | solution.py:231
  (44 shorter events, 7.8 us)
Async XLA Ops:
  7.2 48.5 %copy-start = (f32[1,128,256]{2,1,0:T(8,128)S(1)}, f32[1,128,256]{2,1,0:T(8,128)}, u32[]{:S(2)}) copy-start(f32[1,128,256]{2,1,0:T(8,128)} %param.13) | copy-start | bytes 393220
  7.2 14.7 %copy-start.2 = (f32[12,1,128,128]{3,2,1,0:T(8,128)S(1)}, f32[12,1,128,128]{3,2,1,0:T(8,128)}, u32[]{:S(2)}) copy-start(f32[12,1,128,128]{3,2,1,0:T(8,128)} %param.11) | copy-start | bytes 2359300
  7.2 103.6 %all-gather.3.cloned.1.call-start = ((), (), s32[]{:S(2)}) async-start(), calls=%async_computation.6 | async-start | bytes 2228224 | tf_op jit(solution)/shard_map/all_gather | solution.py:270
  11.6 23.3 %all-to-all-start = ((f32[8,13,16,128]{3,2,1,0:T(8,128)}), f32[8,13,16,128]{3,2,1,0:T(8,128)S(1)}, u32[]{:S(2)}, u32[]{:S(2)}) async-start(f32[8,13,16,128]{3,2,1,0:T(8,128)} %broadcast_in_dim.36), calls=%async_computation | async-start | bytes 1703936 | tf_op jit(solution)/shard_map/all_to_all | solution.py:243
  21.9 13.8 %collective-permute-start = (f32[12,128,128]{2,1,0:T(8,128)S(1)}, f32[12,128,128]{2,1,0:T(8,128)S(1)}, u32[]{:S(2)}, u32[]{:S(2)}) collective-permute-start(f32[12,128,128]{2,1,0:T(8,128)S(1)} %bitcast.16), channel_id=1, source_target_pairs={{0,4},{4,0},{1,5},{5,1},{2,6},{6,2},{3,7},{7,3},{8,12},{12,8},{9,1... | collective-permute-start | bytes 2359304 | tf_op jit(solution)/shard_map/ppermute | solution.py:247
  34.9 0.9 copy-start.1
  35.7 0.9 copy-start.4
  36.6 9.7 %copy-start.3 = (f32[12,1,128,128]{3,2,1,0:T(8,128)S(1)}, f32[12,1,128,128]{3,2,1,0:T(8,128)}, u32[]{:S(2)}) copy-start(f32[12,1,128,128]{3,2,1,0:T(8,128)} %param.11) | copy-start | bytes 2359300
  42.6 19.9 %all-to-all-start.1 = ((f32[16,16,8,128]{3,2,1,0:T(8,128)}), f32[16,16,8,128]{3,2,1,0:T(8,128)S(1)}, u32[]{:S(2)}, u32[]{:S(2)}) async-start(f32[16,16,8,128]{3,2,1,0:T(8,128)} %get-tuple-element.20), calls=%async_computation.1 | async-start | bytes 2097152 | tf_op jit(solution)/shard_map/all_to_all | solution.py:279
  46.3 48.4 %collective-permute-start.1 = (f32[12,128,128]{2,1,0:T(8,128)S(1)}, f32[12,128,128]{2,1,0:T(8,128)S(1)}, u32[]{:S(2)}, u32[]{:S(2)}) collective-permute-start(f32[12,128,128]{2,1,0:T(8,128)S(1)} %bitcast.17), channel_id=1, source_target_pairs={{0,24},{8,0},{16,8},{24,16},{1,25},{9,1},{17,9},{25,17},{2,26},{10... | collective-permute-start | bytes 2359304 | tf_op jit(solution)/shard_map/ppermute | solution.py:252
  50.7 44.0 %collective-permute-start.2 = (f32[12,128,128]{2,1,0:T(8,128)S(1)}, f32[12,128,128]{2,1,0:T(8,128)S(1)}, u32[]{:S(2)}, u32[]{:S(2)}) collective-permute-start(f32[12,128,128]{2,1,0:T(8,128)S(1)} %bitcast.18), channel_id=1, source_target_pairs={{0,16},{8,24},{16,0},{24,8},{1,17},{9,25},{17,1},{25,9},{2,18},{10... | collective-permute-start | bytes 2359304 | tf_op jit(solution)/shard_map/ppermute | solution.py:252
  53.1 42.4 %collective-permute-start.3 = (f32[12,128,128]{2,1,0:T(8,128)S(1)}, f32[12,128,128]{2,1,0:T(8,128)}, u32[]{:S(2)}, u32[]{:S(2)}) collective-permute-start(f32[12,128,128]{2,1,0:T(8,128)S(1)} %bitcast.19), channel_id=1, source_target_pairs={{0,8},{8,16},{16,24},{24,0},{1,9},{9,17},{17,25},{25,1},{2,10},{10... | collective-permute-start | bytes 2359304 | tf_op jit(solution)/shard_map/ppermute | solution.py:252
  94.7 23.6 %copy-start.6 = (f32[12,128,128]{2,1,0:T(8,128)}, f32[12,128,128]{2,1,0:T(8,128)S(1)}, u32[]{:S(2)}) copy-start(f32[12,128,128]{2,1,0:T(8,128)S(1)} %collective-permute-done.1.refs_2_) | copy-start | bytes 2359300
  94.7 23.6 %copy-start.7 = (f32[12,128,128]{2,1,0:T(8,128)}, f32[12,128,128]{2,1,0:T(8,128)S(1)}, u32[]{:S(2)}) copy-start(f32[12,128,128]{2,1,0:T(8,128)S(1)} %collective-permute-done.2.refs_4_) | copy-start | bytes 2359300
  96.3 14.5 %all-to-all-start.4 = ((f32[16,4,8,128]{3,2,1,0:T(8,128)}), f32[16,4,8,128]{3,2,1,0:T(8,128)S(1)}, u32[]{:S(2)}, u32[]{:S(2)}) async-start(f32[16,4,8,128]{3,2,1,0:T(8,128)} %broadcast_in_dim.41), calls=%async_computation.4 | async-start | bytes 524288 | tf_op jit(solution)/shard_map/all_to_all | solution.py:243
  101.0 17.3 %collective-permute-start.4 = (f32[12,128,128]{2,1,0:T(8,128)S(1)}, f32[12,128,128]{2,1,0:T(8,128)S(1)}, u32[]{:S(2)}, u32[]{:S(2)}) collective-permute-start(f32[12,128,128]{2,1,0:T(8,128)S(1)} %collective-permute-done.1.refs_2_), channel_id=1, source_target_pairs={{0,4},{4,0},{1,5},{5,1},{2,6},{6,2},{3,7},{7,3},{8,12},{12,8},{9,1... | collective-permute-start | bytes 2359304 | tf_op jit(solution)/shard_map/ppermute | solution.py:247
  106.4 11.8 %collective-permute-start.5 = (f32[12,128,128]{2,1,0:T(8,128)S(1)}, f32[12,128,128]{2,1,0:T(8,128)S(1)}, u32[]{:S(2)}, u32[]{:S(2)}) collective-permute-start(f32[12,128,128]{2,1,0:T(8,128)S(1)} %collective-permute-done.2.refs_4_), channel_id=1, source_target_pairs={{0,4},{4,0},{1,5},{5,1},{2,6},{6,2},{3,7},{7,3},{8,12},{12,8},{9,1... | collective-permute-start | bytes 2359304 | tf_op jit(solution)/shard_map/ppermute | solution.py:247
  108.4 9.9 %collective-permute-start.6 = (f32[12,128,128]{2,1,0:T(8,128)}, f32[12,128,128]{2,1,0:T(8,128)}, u32[]{:S(2)}, u32[]{:S(2)}) collective-permute-start(f32[12,128,128]{2,1,0:T(8,128)} %collective-permute-done.3.refs_6_), channel_id=1, source_target_pairs={{0,4},{4,0},{1,5},{5,1},{2,6},{6,2},{3,7},{7,3},{8,12},{12,8},{9,1... | collective-permute-start | bytes 2359304 | tf_op jit(solution)/shard_map/ppermute | solution.py:247
  110.8 0.7 copy-start.5
  118.2 0.9 copy-start.8
  118.2 1.2 copy-start.9
Sparse Core Ops, SparseCore 0:
  10.7 70.6 all-gather.2

commit v5 on v4

--- a/solution.py
+++ b/solution.py
@@ -269,7 +269,7 @@
     inv = spread(packed, COLS)
     maps = lax.all_gather(top_map(top_inv, top_sub), ROWS, axis=0, tiled=False)
     paired = from_core(blocks)
-    far = [from_y(blocks, step) for step in range(1, n_y)]
+    far = [from_y(blocks, 1), None, from_y(blocks, 3)]
 
     targets = inv[:, leaves, 0, :leaves].astype(jnp.int32).reshape(n_y, 2, leaves)
     targets = jnp.roll(targets, -y, axis=0)
@@ -285,8 +285,10 @@
 
     quarter = lax.all_to_all(partial, "rlo", 0, 0, tiled=True)
     quarter = quarter.reshape((lax.axis_size("rlo"), -1) + quarter.shape[1:]).sum(0)
+    held, quarter = lax.optimization_barrier((blocks, quarter))
+    far[1] = from_y(held, 2)
     quarter = spread(quarter, "rhi").sum(0)
-    quarter, far = lax.optimization_barrier((quarter, far))
+    quarter, far[0], far[2] = lax.optimization_barrier((quarter, far[0], far[2]))
     all_blocks = [blocks, paired]
     for block in far:
         all_blocks += [block, from_core(block)]

time: 165 us -> 153 us (0.927)
  blocking collectives: 59.6 us -> 45.9 us
    all_to_all x1, blocking collectives: 29 us -> 15.3 us  [on_device(): got = lax.all_to_all(turned, COLS, 0, 0, tiled=True)]
    all_to_all x1, waiting for transfers between devices: 5.18 us -> 8.03 us  [on_device(): arrived = lax.all_to_all(sums, ('y', 'layers'), 0, 0, tiled=True)]
    all_to_all x2, waiting for transfers between devices: 10.3 us -> 8.49 us  [spread(): lax.all_to_all(jnp.broadcast_to(x, (n,) + x.shape), axis, 0, 0, tiled=True)]
  transfers between devices with their start and end apart: 11 -> 11, of which waited for: 3 -> 2; matrix products, arithmetic and copies ran while one was open for 5% -> 4% of each run, Pallas kernels for 8% -> 10%
where the time goes in v5:
time: 153 us; the launch traced here: 152 us
  blocking collectives  45.9 us (30%)
  starting transfers between devices  41.3 us (27%)
  Pallas kernels  23.3 us (15%)
  waiting for transfers between devices  16.6 us (11%)
  between operations  14.3 us (9%)
  local copies, waits for them, and re-layouts  5.92 us (4%)
  other arithmetic  4.65 us (3%)
    all_to_all x1, blocking collectives, spread(): lax.all_to_all(jnp.broadcast_to(x, (n,) + x.shape), axis, 0, 0, tiled=True)  23.6 us
    all_to_all x2, starting transfers between devices, spread(): lax.all_to_all(jnp.broadcast_to(x, (n,) + x.shape), axis, 0, 0, tiled=True)  15.6 us
    all_to_all x1, blocking collectives, on_device(): got = lax.all_to_all(turned, COLS, 0, 0, tiled=True)  15.3 us
    ppermute x4, starting transfers between devices, from_core(): return lax.ppermute(x, 'core', [(0, 1), (1, 0)])  13 us
    ppermute x3, starting transfers between devices, from_y(): return lax.ppermute(x, 'y', [(i, (i - step) % n) for i in range(n)])  8.98 us
    all_to_all x2, waiting for transfers between devices, spread(): lax.all_to_all(jnp.broadcast_to(x, (n,) + x.shape), axis, 0, 0, tiled=True)  8.49 us
    all_to_all x1, waiting for transfers between devices, on_device(): arrived = lax.all_to_all(sums, ('y', 'layers'), 0, 0, tiled=True)  8.03 us
    all_to_all x1, blocking collectives, on_device(): quarter = lax.all_to_all(partial, 'rlo', 0, 0, tiled=True)  7.03 us
  transfers between devices with their start and end apart: 11, of which 2 were waited for; matrix products, arithmetic and copies ran while one was open for 4% of the time, Pallas kernels for 10%

profile of v5, /device:TPU:1, one launch (start us, length us, event | category | flops | bytes accessed | tf_op | source)
XLA Modules:
  0.0 151.9 jit_solution(4362019084883250083)
XLA Ops:
  7.9 0.9 select_maximum_fusion
  8.8 1.0 broadcast_in_dim.36
  9.8 10.3 %all-to-all-start = ((f32[8,13,16,128]{3,2,1,0:T(8,128)}), f32[8,13,16,128]{3,2,1,0:T(8,128)S(1)}, u32[]{:S(2)}, u32[]{:S(2)}) async-start(f32[8,13,16,128]{3,2,1,0:T(8,128)} %broadcast_in_dim.36), calls=%async_computation | async-start | bytes 1703936 | tf_op jit(solution)/shard_map/all_to_all | solution.py:243
  20.1 1.7 %top_map.1 = f32[2,128,128]{2,1,0:T(8,128)} custom-call(f32[1,128,128]{2,1,0:T(8,128)} %inv_ref.1, f32[1,128,128]{2,1,0:T(8,128)} %sub_ref.1), custom_call_target="tpu_custom_call" | custom-call | tf_op jit(solution)/shard_map/top_map/pallas_call | solution.py:110
  21.9 2.1 %collective-permute-start = (f32[12,128,128]{2,1,0:T(8,128)S(1)}, f32[12,128,128]{2,1,0:T(8,128)S(1)}, u32[]{:S(2)}, u32[]{:S(2)}) collective-permute-start(f32[12,128,128]{2,1,0:T(8,128)S(1)} %bitcast.16), channel_id=1, source_target_pairs={{0,4},{4,0},{1,5},{5,1},{2,6},{6,2},{3,7},{7,3},{8,12},{12,8},{9,1... | collective-permute-start | bytes 2359304 | tf_op jit(solution)/shard_map/ppermute | solution.py:247
  24.6 8.5 %all-to-all-done.inv_ref.refs_9_ = f32[8,13,16,128]{3,2,1,0:T(8,128)S(1)} async-done(((f32[8,13,16,128]{3,2,1,0:T(8,128)}), f32[8,13,16,128]{3,2,1,0:T(8,128)S(1)}, u32[]{:S(2)}, u32[]{:S(2)}) %all-to-all-start) | async-done | bytes 852000 | tf_op jit(solution)/shard_map/all_to_all | solution.py:243
  34.8 6.0 %leaf_forward.1 = (f32[16,16,8,128]{3,2,1,0:T(8,128)}, f32[12,32,128]{2,1,0:T(8,128)}) custom-call(s32[2]{0:T(128)} %pad_add_fusion.place_ref, s32[8,12]{1,0:T(8,128)} %bitcast.23, f32[8,13,16,128]{3,2,1,0:T(8,128)} %copy-done.1, f32[12,128,128]{2,1,0:T(8,128)} %bitcast.14, f32[12,128,128]{2,1,0:T(8,128)} %copy-done.4, f32[12,128,256]{2,1,0:T(8,128)} %known_ref.1), custom_call_target="tpu_custom_call" | custom-call | tf_op jit(solution)/shard_map/leaf_forward/pallas_call | solution.py:73
  40.8 3.7 %all-to-all-start.1 = ((f32[16,16,8,128]{3,2,1,0:T(8,128)}), f32[16,16,8,128]{3,2,1,0:T(8,128)S(1)}, u32[]{:S(2)}, u32[]{:S(2)}) async-start(f32[16,16,8,128]{3,2,1,0:T(8,128)} %get-tuple-element.21), calls=%async_computation.1 | async-start | bytes 2097152 | tf_op jit(solution)/shard_map/all_to_all | solution.py:279
  44.4 4.4 %collective-permute-start.1 = (f32[12,128,128]{2,1,0:T(8,128)S(1)}, f32[12,128,128]{2,1,0:T(8,128)S(1)}, u32[]{:S(2)}, u32[]{:S(2)}) collective-permute-start(f32[12,128,128]{2,1,0:T(8,128)S(1)} %bitcast.17), channel_id=1, source_target_pairs={{0,24},{8,0},{16,8},{24,16},{1,25},{9,1},{17,9},{25,17},{2,26},{10... | collective-permute-start | bytes 2359304 | tf_op jit(solution)/shard_map/ppermute | solution.py:252
  48.9 1.9 %collective-permute-start.2 = (f32[12,128,128]{2,1,0:T(8,128)S(1)}, f32[12,128,128]{2,1,0:T(8,128)S(1)}, u32[]{:S(2)}, u32[]{:S(2)}) collective-permute-start(f32[12,128,128]{2,1,0:T(8,128)S(1)} %bitcast.18), channel_id=1, source_target_pairs={{0,8},{8,16},{16,24},{24,0},{1,9},{9,17},{17,25},{25,1},{2,10},{10... | collective-permute-start | bytes 2359304 | tf_op jit(solution)/shard_map/ppermute | solution.py:252
  51.6 0.9 copy.12
  52.5 8.0 %all-to-all-done.1 = f32[16,16,8,128]{3,2,1,0:T(8,128)S(1)} async-done(((f32[16,16,8,128]{3,2,1,0:T(8,128)}), f32[16,16,8,128]{3,2,1,0:T(8,128)S(1)}, u32[]{:S(2)}, u32[]{:S(2)}) %all-to-all-start.1) | async-done | bytes 1048608 | tf_op jit(solution)/shard_map/all_to_all | solution.py:279
  61.2 0.9 select_subtract_fusion
  62.1 7.0 %all_to_all.30 = f32[16,8,128]{2,1,0:T(8,128)S(1)} all-to-all(f32[16,8,128]{2,1,0:T(8,128)S(1)} %select_subtract_fusion), channel_id=1, replica_groups=mesh['rhi'=4,'rlo'=4,'y'=4,'core'=2,'layers'=4] {'rlo'}, dimensions={0} | all-to-all | bytes 131072 | tf_op jit(solution)/shard_map/all_to_all | solution.py:286
  69.1 2.6 %collective-permute-start.4 = (f32[12,128,128]{2,1,0:T(8,128)S(1)}, f32[12,128,128]{2,1,0:T(8,128)S(1)}, u32[]{:S(2)}, u32[]{:S(2)}) collective-permute-start(f32[12,128,128]{2,1,0:T(8,128)S(1)} %bitcast.19), channel_id=1, source_target_pairs={{0,16},{8,24},{16,0},{24,8},{1,17},{9,25},{17,1},{25,9},{2,18},{10... | collective-permute-start | bytes 2359304 | tf_op jit(solution)/shard_map/ppermute | solution.py:252
  71.8 23.6 %all_to_all.31 = f32[4,4,8,128]{3,2,1,0:T(8,128)S(1)} all-to-all(f32[4,4,8,128]{3,2,1,0:T(8,128)S(1)} %broadcast_in_dim.40), channel_id=1, replica_groups=mesh['rhi'=4,'rlo'=4,'y'=4,'core'=2,'layers'=4] {'rhi'}, dimensions={0} | all-to-all | bytes 131072 | tf_op jit(solution)/shard_map/all_to_all | solution.py:243
  96.2 5.3 %all-to-all-start.4 = ((f32[16,4,8,128]{3,2,1,0:T(8,128)}), f32[16,4,8,128]{3,2,1,0:T(8,128)S(1)}, u32[]{:S(2)}, u32[]{:S(2)}) async-start(f32[16,4,8,128]{3,2,1,0:T(8,128)} %broadcast_in_dim.41), calls=%async_computation.4 | async-start | bytes 524288 | tf_op jit(solution)/shard_map/all_to_all | solution.py:243
  101.5 6.6 %collective-permute-start.3 = (f32[12,128,128]{2,1,0:T(8,128)S(1)}, f32[12,128,128]{2,1,0:T(8,128)}, u32[]{:S(2)}, u32[]{:S(2)}) collective-permute-start(f32[12,128,128]{2,1,0:T(8,128)S(1)} %collective-permute-done.1.refs_2_), channel_id=1, source_target_pairs={{0,4},{4,0},{1,5},{5,1},{2,6},{6,2},{3,7},{7,3},{8,12},{12,8},{9,1... | collective-permute-start | bytes 2359304 | tf_op jit(solution)/shard_map/ppermute | solution.py:247
  108.2 1.9 %collective-permute-start.6 = (f32[12,128,128]{2,1,0:T(8,128)S(1)}, f32[12,128,128]{2,1,0:T(8,128)}, u32[]{:S(2)}, u32[]{:S(2)}) collective-permute-start(f32[12,128,128]{2,1,0:T(8,128)S(1)} %collective-permute-done.2.refs_6_), channel_id=1, source_target_pairs={{0,4},{4,0},{1,5},{5,1},{2,6},{6,2},{3,7},{7,3},{8,12},{12,8},{9,1... | collective-permute-start | bytes 2359304 | tf_op jit(solution)/shard_map/ppermute | solution.py:247
  110.1 2.4 %collective-permute-start.5 = (f32[12,128,128]{2,1,0:T(8,128)S(1)}, f32[12,128,128]{2,1,0:T(8,128)S(1)}, u32[]{:S(2)}, u32[]{:S(2)}) collective-permute-start(f32[12,128,128]{2,1,0:T(8,128)S(1)} %collective-permute-done.4.refs_4_), channel_id=1, source_target_pairs={{0,4},{4,0},{1,5},{5,1},{2,6},{6,2},{3,7},{7,3},{8,12},{12,8},{9,1... | collective-permute-start | bytes 2359304 | tf_op jit(solution)/shard_map/ppermute | solution.py:247
  113.3 6.7 %top_chain.1.tops_ref = f32[16,32,128]{2,1,0:T(8,128)} custom-call(f32[4,4,4,8,128]{4,3,2,1,0:T(8,128)} %bitcast.21, f32[16,2,128,128]{3,2,1,0:T(8,128)} %bitcast.20), custom_call_target="tpu_custom_call" | custom-call | tf_op jit(solution)/shard_map/top_chain/pallas_call | solution.py:142
  120.9 6.9 %leaf_backward.1 = f32[8,80,128]{2,1,0:T(8,128)} custom-call(s32[1]{0:T(128)} %bitcast.row_ref, s32[8,12]{1,0:T(8,128)} %bitcast.24, f32[16,32,128]{2,1,0:T(8,128)} %top_chain.1.tops_ref, f32[12,128,128]{2,1,0:T(8,128)} %bitcast.15, f32[12,128,128]{2,1,0:T(8,128)} %copy-done.4, f32[12,128,128]{2,1,0:T(8,128)} %copy-done.6, ...), custom_call_target="tpu_custom_call" | custom-call | tf_op jit(solution)/shard_map/leaf_backward/pallas_call | solution.py:189
  127.8 15.3 %all_to_all.32.got_ref = f32[8,80,128]{2,1,0:T(8,128)} all-to-all(f32[8,80,128]{2,1,0:T(8,128)} %leaf_backward.1), channel_id=1, replica_groups=mesh['rhi'=4,'rlo'=4,'y'=4,'core'=2,'layers'=4] {'y','core'}, dimensions={0} | all-to-all | bytes 655360 | tf_op jit(solution)/shard_map/all_to_all | solution.py:300
  143.1 1.9 %arrange.1 = (f32[12,16,256]{2,1,0:T(8,128)}, f32[1,128,256]{2,1,0:T(8,128)}) custom-call(f32[8,80,128]{2,1,0:T(8,128)} %all_to_all.32.got_ref), custom_call_target="tpu_custom_call" | custom-call | tf_op jit(solution)/shard_map/arrange/pallas_call | solution.py:231
  (44 shorter events, 7.0 us)
Async XLA Ops:
  7.2 43.7 %copy-start = (f32[1,128,256]{2,1,0:T(8,128)S(1)}, f32[1,128,256]{2,1,0:T(8,128)}, u32[]{:S(2)}) copy-start(f32[1,128,256]{2,1,0:T(8,128)} %param.13) | copy-start | bytes 393220
  7.2 14.7 %copy-start.2 = (f32[12,1,128,128]{3,2,1,0:T(8,128)S(1)}, f32[12,1,128,128]{3,2,1,0:T(8,128)}, u32[]{:S(2)}) copy-start(f32[12,1,128,128]{3,2,1,0:T(8,128)} %param.11) | copy-start | bytes 2359300
  9.8 23.3 %all-to-all-start = ((f32[8,13,16,128]{3,2,1,0:T(8,128)}), f32[8,13,16,128]{3,2,1,0:T(8,128)S(1)}, u32[]{:S(2)}, u32[]{:S(2)}) async-start(f32[8,13,16,128]{3,2,1,0:T(8,128)} %broadcast_in_dim.36), calls=%async_computation | async-start | bytes 1703936 | tf_op jit(solution)/shard_map/all_to_all | solution.py:243
  20.1 92.4 %all-gather.3.cloned.1.call-start = ((), (), s32[]{:S(2)}) async-start(), calls=%async_computation.6 | async-start | bytes 2228224 | tf_op jit(solution)/shard_map/all_gather | solution.py:270
  21.9 12.0 %collective-permute-start = (f32[12,128,128]{2,1,0:T(8,128)S(1)}, f32[12,128,128]{2,1,0:T(8,128)S(1)}, u32[]{:S(2)}, u32[]{:S(2)}) collective-permute-start(f32[12,128,128]{2,1,0:T(8,128)S(1)} %bitcast.16), channel_id=1, source_target_pairs={{0,4},{4,0},{1,5},{5,1},{2,6},{6,2},{3,7},{7,3},{8,12},{12,8},{9,1... | collective-permute-start | bytes 2359304 | tf_op jit(solution)/shard_map/ppermute | solution.py:247
  33.1 0.9 copy-start.1
  33.9 0.9 copy-start.4
  34.8 9.6 %copy-start.3 = (f32[12,1,128,128]{3,2,1,0:T(8,128)S(1)}, f32[12,1,128,128]{3,2,1,0:T(8,128)}, u32[]{:S(2)}) copy-start(f32[12,1,128,128]{3,2,1,0:T(8,128)} %param.11) | copy-start | bytes 2359300
  40.8 19.7 %all-to-all-start.1 = ((f32[16,16,8,128]{3,2,1,0:T(8,128)}), f32[16,16,8,128]{3,2,1,0:T(8,128)S(1)}, u32[]{:S(2)}, u32[]{:S(2)}) async-start(f32[16,16,8,128]{3,2,1,0:T(8,128)} %get-tuple-element.21), calls=%async_computation.1 | async-start | bytes 2097152 | tf_op jit(solution)/shard_map/all_to_all | solution.py:279
  44.4 50.9 %collective-permute-start.1 = (f32[12,128,128]{2,1,0:T(8,128)S(1)}, f32[12,128,128]{2,1,0:T(8,128)S(1)}, u32[]{:S(2)}, u32[]{:S(2)}) collective-permute-start(f32[12,128,128]{2,1,0:T(8,128)S(1)} %bitcast.17), channel_id=1, source_target_pairs={{0,24},{8,0},{16,8},{24,16},{1,25},{9,1},{17,9},{25,17},{2,26},{10... | collective-permute-start | bytes 2359304 | tf_op jit(solution)/shard_map/ppermute | solution.py:252
  48.9 46.5 %collective-permute-start.2 = (f32[12,128,128]{2,1,0:T(8,128)S(1)}, f32[12,128,128]{2,1,0:T(8,128)S(1)}, u32[]{:S(2)}, u32[]{:S(2)}) collective-permute-start(f32[12,128,128]{2,1,0:T(8,128)S(1)} %bitcast.18), channel_id=1, source_target_pairs={{0,8},{8,16},{16,24},{24,0},{1,9},{9,17},{17,25},{25,1},{2,10},{10... | collective-permute-start | bytes 2359304 | tf_op jit(solution)/shard_map/ppermute | solution.py:252
  69.1 41.0 %collective-permute-start.4 = (f32[12,128,128]{2,1,0:T(8,128)S(1)}, f32[12,128,128]{2,1,0:T(8,128)S(1)}, u32[]{:S(2)}, u32[]{:S(2)}) collective-permute-start(f32[12,128,128]{2,1,0:T(8,128)S(1)} %bitcast.19), channel_id=1, source_target_pairs={{0,16},{8,24},{16,0},{24,8},{1,17},{9,25},{17,1},{25,9},{2,18},{10... | collective-permute-start | bytes 2359304 | tf_op jit(solution)/shard_map/ppermute | solution.py:252
  95.4 24.7 %copy-start.6 = (f32[12,128,128]{2,1,0:T(8,128)}, f32[12,128,128]{2,1,0:T(8,128)S(1)}, u32[]{:S(2)}) copy-start(f32[12,128,128]{2,1,0:T(8,128)S(1)} %collective-permute-done.1.refs_2_) | copy-start | bytes 2359300
  95.4 24.7 %copy-start.7 = (f32[12,128,128]{2,1,0:T(8,128)}, f32[12,128,128]{2,1,0:T(8,128)S(1)}, u32[]{:S(2)}) copy-start(f32[12,128,128]{2,1,0:T(8,128)S(1)} %collective-permute-done.2.refs_6_) | copy-start | bytes 2359300
  96.2 16.3 %all-to-all-start.4 = ((f32[16,4,8,128]{3,2,1,0:T(8,128)}), f32[16,4,8,128]{3,2,1,0:T(8,128)S(1)}, u32[]{:S(2)}, u32[]{:S(2)}) async-start(f32[16,4,8,128]{3,2,1,0:T(8,128)} %broadcast_in_dim.41), calls=%async_computation.4 | async-start | bytes 524288 | tf_op jit(solution)/shard_map/all_to_all | solution.py:243
  101.5 18.5 %collective-permute-start.3 = (f32[12,128,128]{2,1,0:T(8,128)S(1)}, f32[12,128,128]{2,1,0:T(8,128)}, u32[]{:S(2)}, u32[]{:S(2)}) collective-permute-start(f32[12,128,128]{2,1,0:T(8,128)S(1)} %collective-permute-done.1.refs_2_), channel_id=1, source_target_pairs={{0,4},{4,0},{1,5},{5,1},{2,6},{6,2},{3,7},{7,3},{8,12},{12,8},{9,1... | collective-permute-start | bytes 2359304 | tf_op jit(solution)/shard_map/ppermute | solution.py:247
  108.2 11.9 %collective-permute-start.6 = (f32[12,128,128]{2,1,0:T(8,128)S(1)}, f32[12,128,128]{2,1,0:T(8,128)}, u32[]{:S(2)}, u32[]{:S(2)}) collective-permute-start(f32[12,128,128]{2,1,0:T(8,128)S(1)} %collective-permute-done.2.refs_6_), channel_id=1, source_target_pairs={{0,4},{4,0},{1,5},{5,1},{2,6},{6,2},{3,7},{7,3},{8,12},{12,8},{9,1... | collective-permute-start | bytes 2359304 | tf_op jit(solution)/shard_map/ppermute | solution.py:247
  110.1 10.0 %copy-start.8 = (f32[12,128,128]{2,1,0:T(8,128)}, f32[12,128,128]{2,1,0:T(8,128)S(1)}, u32[]{:S(2)}) copy-start(f32[12,128,128]{2,1,0:T(8,128)S(1)} %collective-permute-done.4.refs_4_) | copy-start | bytes 2359300
  110.1 9.9 %collective-permute-start.5 = (f32[12,128,128]{2,1,0:T(8,128)S(1)}, f32[12,128,128]{2,1,0:T(8,128)S(1)}, u32[]{:S(2)}, u32[]{:S(2)}) collective-permute-start(f32[12,128,128]{2,1,0:T(8,128)S(1)} %collective-permute-done.4.refs_4_), channel_id=1, source_target_pairs={{0,4},{4,0},{1,5},{5,1},{2,6},{6,2},{3,7},{7,3},{8,12},{12,8},{9,1... | collective-permute-start | bytes 2359304 | tf_op jit(solution)/shard_map/ppermute | solution.py:247
  112.5 0.8 copy-start.5
  120.0 0.9 copy-start.9
Sparse Core Ops, SparseCore 0:
  23.6 64.9 all-gather.2

commit v6 on v5

--- a/solution.py
+++ b/solution.py
@@ -43,7 +43,42 @@
     return pl.BlockSpec(shape, lambda *_: (0,) * len(shape))
 
 
-def leaf_forward_kernel(place_ref, targets_ref, inv_ref, mine_ref, pair_ref, known_ref, sums_ref, own_ref, stage):
+def prepare_kernel(targets_ref, pivot_ref, inv_ref, sub_ref, out_ref, maps_ref):
+    leaves, slab, b = pivot_ref.shape
+    line = lax.broadcasted_iota(jnp.int32, (slab, b), 0)
+    named = jnp.zeros((slab, b), F32)
+    for i in range(leaves):
+        named = jnp.where(line == i, targets_ref[i].astype(F32), named)
+    for c in range(out_ref.shape[0]):
+        out_ref[c, :leaves] = pivot_ref[...]
+        out_ref[c, leaves] = named
+    maps_ref[0] = inv_ref[0]
+    maps_ref[1] = -lax.dot_general(
+        inv_ref[0],
+        sub_ref[0],
+        (((1,), (0,)), ((), ())),
+        precision=lax.Precision.HIGHEST,
+        preferred_element_type=F32,
+    )
+
+
+def prepare(targets, pivot, inv, sub, n_cols):
+    leaves, slab, b = pivot.shape
+    vmem = pl.BlockSpec(memory_space=pltpu.VMEM)
+    return pl.pallas_call(
+        prepare_kernel,
+        in_specs=[pl.BlockSpec(memory_space=pltpu.SMEM), vmem, vmem, vmem],
+        out_specs=[vmem, vmem],
+        out_shape=[
+            jax.ShapeDtypeStruct((n_cols, leaves + 1, slab, b), F32),
+            jax.ShapeDtypeStruct((2,) + inv.shape[1:], F32),
+        ],
+        name="prepare",
+    )(targets, pivot, inv, sub)
+
+
+def leaf_forward_kernel(place_ref, targets_ref, rhs_ref, inv_ref, mine_ref, pair_ref, known_ref, sums_ref, own_ref, stage):
+    core, y, part, row = (place_ref[k] for k in range(4))
     step = pl.program_id(0)
     count, b = mine_ref.shape[:2]
     own = own_ref.shape[1]
@@ -51,20 +86,21 @@
     @pl.when(step == 0)
     def _():
         sums_ref[...] = jnp.zeros_like(sums_ref)
+        sums_ref[part, row] = rhs_ref[...]
 
     for i in range(count):
         inv = inv_ref[:, i].reshape(b, b)
         forward = dot3(known_ref[i].T, inv, 1)
         update = dot3(forward, jnp.concatenate([mine_ref[i], pair_ref[i]], axis=0), 1)
         for k in range(2):
-            t = targets_ref[k, step * count + i]
+            t = targets_ref[2 * y + (core if k == 0 else 1 - core), step * count + i]
             for q in range(sums_ref.shape[0]):
-                sums_ref[q, t] += update[8 * q : 8 * q + 8, k * b : (k + 1) * b]
+                sums_ref[q, t] -= update[8 * q : 8 * q + 8, k * b : (k + 1) * b]
         stage[i] = forward
-        own_ref[i] = stage[i, pl.ds(pl.multiple_of(place_ref[1] * own, own), own), :]
-
-
-def leaf_forward(place, targets, inv, mine, pair, known, tops):
+        own_ref[i] = stage[i, pl.ds(pl.multiple_of(y * own, own), own), :]
+
+
+def leaf_forward(place, targets, rhs, inv, mine, pair, known, tops):
     leaves, b, r = known.shape
     n_cols, _, slab, _ = inv.shape
     half = r // 2
@@ -76,6 +112,7 @@
             num_scalar_prefetch=2,
             grid=(leaves // STEP,),
             in_specs=[
+                whole(rhs.shape),
                 pl.BlockSpec((n_cols, STEP, slab, b), lambda i, *_: (0, i, 0, 0)),
                 block,
                 block,
@@ -92,26 +129,7 @@
             jax.ShapeDtypeStruct((leaves, own, b), F32),
         ],
         name="leaf_forward",
-    )(place, targets, inv, mine, pair, known)
-
-
-def top_map_kernel(inv_ref, sub_ref, out_ref):
-    out_ref[0] = inv_ref[0]
-    out_ref[1] = -lax.dot_general(
-        inv_ref[0],
-        sub_ref[0],
-        (((1,), (0,)), ((), ())),
-        precision=lax.Precision.HIGHEST,
-        preferred_element_type=F32,
-    )
-
-
-def top_map(inv, sub):
-    return pl.pallas_call(
-        top_map_kernel,
-        out_shape=jax.ShapeDtypeStruct((2,) + inv.shape[1:], F32),
-        name="top_map",
-    )(inv, sub)
+    )(place, targets, rhs, inv, mine, pair, known)
 
 
 def top_chain_kernel(rhs_ref, maps_ref, out_ref):
@@ -146,8 +164,9 @@
     )(rhs, maps)
 
 
-def leaf_backward_kernel(row_ref, targets_ref, tops_ref, *refs):
+def leaf_backward_kernel(place_ref, targets_ref, tops_ref, *refs):
     *block_refs, own_ref, inv_ref, out_ref, parts = refs
+    core, y, _, row = (place_ref[k] for k in range(4))
     step = pl.program_id(0)
     n_cols = len(block_refs)
     count, b, _ = block_refs[0].shape
@@ -162,12 +181,18 @@
             parts[t, :own] = high
             parts[t, own:] = low
         for c in range(n_cols):
-            out_ref[c, leaf_rows:] = tops_ref[row_ref[0]]
+            out_ref[c, leaf_rows:] = tops_ref[row]
 
     results = []
     for i in range(count):
         leaf = step * count + i
-        both = jnp.concatenate([parts[targets_ref[p, leaf]] for p in range(n_cols)], axis=1)
+        both = jnp.concatenate(
+            [
+                parts[targets_ref[2 * ((y + k // 2) % (n_cols // 2)) + (core + k) % 2, leaf]]
+                for k in range(n_cols)
+            ],
+            axis=1,
+        )
         high, low = split(jnp.concatenate([ref[i] for ref in block_refs], axis=0))
         r = dot(both, high)
         left = own_ref[i] - ((r[:own] + r[own:]) + dot(both[:own], low))
@@ -179,7 +204,7 @@
         ]
 
 
-def leaf_backward(row, targets, tops, blocks, own, inv):
+def leaf_backward(place, targets, tops, blocks, own, inv):
     n_cols = len(blocks)
     leaves, b, _ = blocks[0].shape
     mine = own.shape[1]
@@ -202,7 +227,7 @@
         ),
         out_shape=jax.ShapeDtypeStruct(out, F32),
         name="leaf_backward",
-    )(row, targets, tops, *blocks, own, inv)
+    )(place, targets, tops, *blocks, own, inv)
 
 
 def arrange_kernel(got_ref, leaf_ref, top_ref):
@@ -264,24 +289,18 @@
     slab = pivot.shape[1]
     own = r // n_cols
 
-    named = jnp.zeros((1, slab, b), F32).at[0, 0, :leaves].set(leaf_target[:, 0].astype(F32))
-    packed = jnp.concatenate([pivot, named])
-    inv = spread(packed, COLS)
-    maps = lax.all_gather(top_map(top_inv, top_sub), ROWS, axis=0, tiled=False)
+    packed, own_maps = prepare(leaf_target[:, 0], pivot, top_inv, top_sub, n_cols)
+    inv = lax.all_to_all(packed, COLS, 0, 0, tiled=True)
+    maps = lax.all_gather(own_maps, ROWS, axis=0, tiled=False)
     paired = from_core(blocks)
     far = [from_y(blocks, 1), None, from_y(blocks, 3)]
-
-    targets = inv[:, leaves, 0, :leaves].astype(jnp.int32).reshape(n_y, 2, leaves)
-    targets = jnp.roll(targets, -y, axis=0)
-    targets = jnp.where(core == 0, targets, targets[:, ::-1]).reshape(n_cols, leaves)
-
-    sums, own_forward = leaf_forward(jnp.stack([core, y]), targets, inv, blocks, paired, known, tops)
-    arrived = lax.all_to_all(sums, ("y", "layers"), 0, 0, tiled=True)
-
-    start = core * (r // 2) + y * own + lax.axis_index("layers") * 8
-    rhs_t = lax.dynamic_slice_in_dim(top_rhs[0], start, 8, 1).T
-    mine = (jnp.arange(tops) == row)[:, None, None]
-    partial = jnp.where(mine, rhs_t[None], 0.0) - arrived.sum(0)
+    targets = inv[:, leaves, :leaves, 0].astype(jnp.int32)
+
+    part = y * lax.axis_size("layers") + lax.axis_index("layers")
+    place = jnp.stack([core, y, part, row])
+    rhs_t = lax.dynamic_slice_in_dim(top_rhs[0], core * (r // 2) + part * 8, 8, 1).T
+    sums, own_forward = leaf_forward(place, targets, rhs_t, inv, blocks, paired, known, tops)
+    partial = lax.all_to_all(sums, ("y", "layers"), 0, 0, tiled=True).sum(0)
 
     quarter = lax.all_to_all(partial, "rlo", 0, 0, tiled=True)
     quarter = quarter.reshape((lax.axis_size("rlo"), -1) + quarter.shape[1:]).sum(0)
@@ -296,7 +315,7 @@
     rhs = rhs.reshape((lax.axis_size("rlo"), -1) + rhs.shape[1:])
 
     own_tops = top_chain(rhs, maps)
-    turned = leaf_backward(row[None], targets, own_tops, all_blocks, own_forward, inv)
+    turned = leaf_backward(place, targets, own_tops, all_blocks, own_forward, inv)
     got = lax.all_to_all(turned, COLS, 0, 0, tiled=True)
     return tuple(arrange(got, leaves, r))
 

time: 153 us -> 151 us (0.987)
  other arithmetic: 4.65 us -> 1.5 us
  waiting for transfers between devices: 16.6 us -> 19.4 us
  local copies, waits for them, and re-layouts: 5.92 us -> 4.09 us
    all_to_all x1 -> x2, waiting for transfers between devices: 8.03 us -> 19.3 us  [the longest x1 9.68 us: on_device(): partial = lax.all_to_all(sums, ('y', 'layers'), 0, 0, tiled=True).sum(0)]
    all_to_all x2 -> x1, starting transfers between devices: 15.6 us -> 4.98 us  [spread(): lax.all_to_all(jnp.broadcast_to(x, (n,) + x.shape), axis, 0, 0, tiled=True)]
    all_to_all x1 -> x2, starting transfers between devices: 3.65 us -> 14 us  [the longest x1 10.3 us: on_device(): inv = lax.all_to_all(packed, COLS, 0, 0, tiled=True)]
    all_to_all x2 -> x1, waiting for transfers between devices: 8.49 us -> 0.01 us  [spread(): lax.all_to_all(jnp.broadcast_to(x, (n,) + x.shape), axis, 0, 0, tiled=True)]
    unnamed x21 -> x16, local copies, waits for them, and re-layouts: 3.37 us -> 2.49 us
  transfers between devices with their start and end apart: 11 -> 11, of which waited for: 2 -> 2; matrix products, arithmetic and copies ran while one was open for 4% -> 2% of each run, Pallas kernels for 10% -> 9%
where the time goes in v6:
time: 151 us; the launch traced here: 150 us
  blocking collectives  46 us (30%)
  starting transfers between devices  41.1 us (27%)
  Pallas kernels  23.7 us (16%)
  waiting for transfers between devices  19.4 us (13%)
  between operations  14.3 us (9%)
  local copies, waits for them, and re-layouts  4.09 us (3%)
    all_to_all x1, blocking collectives, spread(): lax.all_to_all(jnp.broadcast_to(x, (n,) + x.shape), axis, 0, 0, tiled=True)  23.6 us
    all_to_all x1, blocking collectives, on_device(): got = lax.all_to_all(turned, COLS, 0, 0, tiled=True)  15.2 us
    ppermute x4, starting transfers between devices, from_core(): return lax.ppermute(x, 'core', [(0, 1), (1, 0)])  13.1 us
    all_to_all x1, starting transfers between devices, on_device(): inv = lax.all_to_all(packed, COLS, 0, 0, tiled=True)  10.3 us
    all_to_all x1, waiting for transfers between devices, on_device(): partial = lax.all_to_all(sums, ('y', 'layers'), 0, 0, tiled=True).sum(0)  9.68 us
    all_to_all x1, waiting for transfers between devices, on_device(): inv = lax.all_to_all(packed, COLS, 0, 0, tiled=True)  9.66 us
    ppermute x3, starting transfers between devices, from_y(): return lax.ppermute(x, 'y', [(i, (i - step) % n) for i in range(n)])  8.92 us
    all_to_all x1, blocking collectives, on_device(): quarter = lax.all_to_all(partial, 'rlo', 0, 0, tiled=True)  7.13 us
  transfers between devices with their start and end apart: 11, of which 2 were waited for; matrix products, arithmetic and copies ran while one was open for 2% of the time, Pallas kernels for 9%

profile of v6, /device:TPU:1, one launch (start us, length us, event | category | flops | bytes accessed | tf_op | source)
XLA Modules:
  0.0 150.0 jit_solution(9484556637491359456)
XLA Ops:
  7.2 2.0 %prepare.1 = (f32[8,13,16,128]{3,2,1,0:T(8,128)}, f32[2,128,128]{2,1,0:T(8,128)}) custom-call(s32[12]{0:T(128)} %bitcast.22, f32[12,16,128]{2,1,0:T(8,128)} %pivot_ref.1, f32[1,128,128]{2,1,0:T(8,128)} %inv_ref.1, f32[1,128,128]{2,1,0:T(8,128)} %sub_ref.1), custom_call_target="tpu_custom_call" | custom-call | tf_op jit(solution)/shard_map/prepare/pallas_call | solution.py:68
  9.3 10.3 %all-to-all-start = ((f32[8,13,16,128]{3,2,1,0:T(8,128)}), f32[8,13,16,128]{3,2,1,0:T(8,128)S(1)}, u32[]{:S(2)}, u32[]{:S(2)}) async-start(f32[8,13,16,128]{3,2,1,0:T(8,128)} %get-tuple-element.11), calls=%async_computation | async-start | bytes 1703936 | tf_op jit(solution)/shard_map/all_to_all | solution.py:293
  19.6 2.0 %collective-permute-start = (f32[12,128,128]{2,1,0:T(8,128)}, f32[12,128,128]{2,1,0:T(8,128)S(1)}, u32[]{:S(2)}, u32[]{:S(2)}) collective-permute-start(f32[12,128,128]{2,1,0:T(8,128)} %bitcast.12), channel_id=1, source_target_pairs={{0,4},{4,0},{1,5},{5,1},{2,6},{6,2},{3,7},{7,3},{8,12},{12,8},{9,1... | collective-permute-start | bytes 2359304 | tf_op jit(solution)/shard_map/ppermute | solution.py:272
  23.0 9.7 %all-to-all-done.inv_ref.refs_9_ = f32[8,13,16,128]{3,2,1,0:T(8,128)S(1)} async-done(((f32[8,13,16,128]{3,2,1,0:T(8,128)}), f32[8,13,16,128]{3,2,1,0:T(8,128)S(1)}, u32[]{:S(2)}, u32[]{:S(2)}) %all-to-all-start) | async-done | bytes 852000 | tf_op jit(solution)/shard_map/all_to_all | solution.py:293
  32.6 0.9 fusion.targets_ref
  33.5 0.9 copy-done.3
  34.4 6.0 %leaf_forward.1 = (f32[16,16,8,128]{3,2,1,0:T(8,128)}, f32[12,32,128]{2,1,0:T(8,128)}) custom-call(s32[4]{0:T(128)} %pad_add_fusion.place_ref, s32[8,12]{1,0:T(8,128)} %fusion.targets_ref, f32[8,128]{1,0:T(8,128)} %bitcast.21, f32[8,13,16,128]{3,2,1,0:T(8,128)} %copy-done.1, f32[12,128,128]{2,1,0:T(8,128)} %bitcast.13, f32[12,128,128]{2,1,0:T(8,128)} %copy-done.3, ...), custom_call_target="tpu_custom_call" | custom-call | tf_op jit(solution)/shard_map/leaf_forward/pallas_call | solution.py:109
  40.4 3.7 %all-to-all-start.1 = ((f32[16,16,8,128]{3,2,1,0:T(8,128)}), f32[16,16,8,128]{3,2,1,0:T(8,128)S(1)}, u32[]{:S(2)}, u32[]{:S(2)}) async-start(f32[16,16,8,128]{3,2,1,0:T(8,128)} %get-tuple-element.12), calls=%async_computation.1 | async-start | bytes 2097152 | tf_op jit(solution)/shard_map/all_to_all | solution.py:303
  44.0 4.4 %collective-permute-start.1 = (f32[12,128,128]{2,1,0:T(8,128)S(1)}, f32[12,128,128]{2,1,0:T(8,128)S(1)}, u32[]{:S(2)}, u32[]{:S(2)}) collective-permute-start(f32[12,128,128]{2,1,0:T(8,128)S(1)} %bitcast.15), channel_id=1, source_target_pairs={{0,24},{8,0},{16,8},{24,16},{1,25},{9,1},{17,9},{25,17},{2,26},{10... | collective-permute-start | bytes 2359304 | tf_op jit(solution)/shard_map/ppermute | solution.py:277
  48.5 1.9 %collective-permute-start.2 = (f32[12,128,128]{2,1,0:T(8,128)S(1)}, f32[12,128,128]{2,1,0:T(8,128)}, u32[]{:S(2)}, u32[]{:S(2)}) collective-permute-start(f32[12,128,128]{2,1,0:T(8,128)S(1)} %bitcast.16), channel_id=1, source_target_pairs={{0,8},{8,16},{16,24},{24,0},{1,9},{9,17},{17,25},{25,1},{2,10},{10... | collective-permute-start | bytes 2359304 | tf_op jit(solution)/shard_map/ppermute | solution.py:277
  50.4 9.7 %all-to-all-done.1 = f32[16,16,8,128]{3,2,1,0:T(8,128)S(1)} async-done(((f32[16,16,8,128]{3,2,1,0:T(8,128)}), f32[16,16,8,128]{3,2,1,0:T(8,128)S(1)}, u32[]{:S(2)}, u32[]{:S(2)}) %all-to-all-start.1) | async-done | bytes 1048608 | tf_op jit(solution)/shard_map/all_to_all | solution.py:303
  60.2 7.1 %all_to_all.30 = f32[16,8,128]{2,1,0:T(8,128)S(1)} all-to-all(f32[16,8,128]{2,1,0:T(8,128)S(1)} %reduce_sum.27), channel_id=1, replica_groups=mesh['rhi'=4,'rlo'=4,'y'=4,'core'=2,'layers'=4] {'rlo'}, dimensions={0} | all-to-all | bytes 131072 | tf_op jit(solution)/shard_map/all_to_all | solution.py:305
  67.3 2.6 %collective-permute-start.4 = (f32[12,128,128]{2,1,0:T(8,128)S(1)}, f32[12,128,128]{2,1,0:T(8,128)S(1)}, u32[]{:S(2)}, u32[]{:S(2)}) collective-permute-start(f32[12,128,128]{2,1,0:T(8,128)S(1)} %bitcast.17), channel_id=1, source_target_pairs={{0,16},{8,24},{16,0},{24,8},{1,17},{9,25},{17,1},{25,9},{2,18},{10... | collective-permute-start | bytes 2359304 | tf_op jit(solution)/shard_map/ppermute | solution.py:277
  69.9 23.6 %all_to_all.31 = f32[4,4,8,128]{3,2,1,0:T(8,128)S(1)} all-to-all(f32[4,4,8,128]{3,2,1,0:T(8,128)S(1)} %broadcast_in_dim.6), channel_id=1, replica_groups=mesh['rhi'=4,'rlo'=4,'y'=4,'core'=2,'layers'=4] {'rhi'}, dimensions={0} | all-to-all | bytes 131072 | tf_op jit(solution)/shard_map/all_to_all | solution.py:268
  93.5 0.9 broadcast_in_dim.7
  94.4 5.0 %all-to-all-start.4 = ((f32[16,4,8,128]{3,2,1,0:T(8,128)}), f32[16,4,8,128]{3,2,1,0:T(8,128)S(1)}, u32[]{:S(2)}, u32[]{:S(2)}) async-start(f32[16,4,8,128]{3,2,1,0:T(8,128)} %broadcast_in_dim.7), calls=%async_computation.4 | async-start | bytes 524288 | tf_op jit(solution)/shard_map/all_to_all | solution.py:268
  99.4 6.8 %collective-permute-start.3 = (f32[12,128,128]{2,1,0:T(8,128)S(1)}, f32[12,128,128]{2,1,0:T(8,128)}, u32[]{:S(2)}, u32[]{:S(2)}) collective-permute-start(f32[12,128,128]{2,1,0:T(8,128)S(1)} %collective-permute-done.1.refs_2_), channel_id=1, source_target_pairs={{0,4},{4,0},{1,5},{5,1},{2,6},{6,2},{3,7},{7,3},{8,12},{12,8},{9,1... | collective-permute-start | bytes 2359304 | tf_op jit(solution)/shard_map/ppermute | solution.py:272
  106.2 1.9 %collective-permute-start.6 = (f32[12,128,128]{2,1,0:T(8,128)}, f32[12,128,128]{2,1,0:T(8,128)}, u32[]{:S(2)}, u32[]{:S(2)}) collective-permute-start(f32[12,128,128]{2,1,0:T(8,128)} %collective-permute-done.2.refs_6_), channel_id=1, source_target_pairs={{0,4},{4,0},{1,5},{5,1},{2,6},{6,2},{3,7},{7,3},{8,12},{12,8},{9,1... | collective-permute-start | bytes 2359304 | tf_op jit(solution)/shard_map/ppermute | solution.py:272
  108.1 2.4 %collective-permute-start.5 = (f32[12,128,128]{2,1,0:T(8,128)S(1)}, f32[12,128,128]{2,1,0:T(8,128)S(1)}, u32[]{:S(2)}, u32[]{:S(2)}) collective-permute-start(f32[12,128,128]{2,1,0:T(8,128)S(1)} %collective-permute-done.4.refs_4_), channel_id=1, source_target_pairs={{0,4},{4,0},{1,5},{5,1},{2,6},{6,2},{3,7},{7,3},{8,12},{12,8},{9,1... | collective-permute-start | bytes 2359304 | tf_op jit(solution)/shard_map/ppermute | solution.py:272
  111.3 6.8 %top_chain.1.tops_ref = f32[16,32,128]{2,1,0:T(8,128)} custom-call(f32[4,4,4,8,128]{4,3,2,1,0:T(8,128)} %bitcast.19, f32[16,2,128,128]{3,2,1,0:T(8,128)} %bitcast.18), custom_call_target="tpu_custom_call" | custom-call | tf_op jit(solution)/shard_map/top_chain/pallas_call | solution.py:160
  118.1 0.9 copy-done.7
  119.0 7.0 %leaf_backward.1 = f32[8,80,128]{2,1,0:T(8,128)} custom-call(s32[4]{0:T(128)} %pad_add_fusion.place_ref, s32[8,12]{1,0:T(8,128)} %fusion.targets_ref, f32[16,32,128]{2,1,0:T(8,128)} %top_chain.1.tops_ref, f32[12,128,128]{2,1,0:T(8,128)} %bitcast.14, f32[12,128,128]{2,1,0:T(8,128)} %copy-done.3, f32[12,128,128]{2,1,0:T(8,128)} %copy-done.5, ...), custom_call_target="tpu_custom_call" | custom-call | tf_op jit(solution)/shard_map/leaf_backward/pallas_call | solution.py:214
  126.0 15.2 %all_to_all.32.got_ref = f32[8,80,128]{2,1,0:T(8,128)} all-to-all(f32[8,80,128]{2,1,0:T(8,128)} %leaf_backward.1), channel_id=1, replica_groups=mesh['rhi'=4,'rlo'=4,'y'=4,'core'=2,'layers'=4] {'y','core'}, dimensions={0} | all-to-all | bytes 655360 | tf_op jit(solution)/shard_map/all_to_all | solution.py:319
  141.2 1.9 %arrange.1 = (f32[12,16,256]{2,1,0:T(8,128)}, f32[1,128,256]{2,1,0:T(8,128)}) custom-call(f32[8,80,128]{2,1,0:T(8,128)} %all_to_all.32.got_ref), custom_call_target="tpu_custom_call" | custom-call | tf_op jit(solution)/shard_map/arrange/pallas_call | solution.py:256
  (32 shorter events, 2.2 us)
Async XLA Ops:
  7.2 14.5 %copy-start = (f32[1,128,256]{2,1,0:T(8,128)S(1)}, f32[1,128,256]{2,1,0:T(8,128)}, u32[]{:S(2)}) copy-start(f32[1,128,256]{2,1,0:T(8,128)} %param.11) | copy-start | bytes 393220
  7.2 103.4 %all-gather.3.cloned.1.call-start = ((), (), s32[]{:S(2)}) async-start(), calls=%async_computation.6 | async-start | bytes 2228224 | tf_op jit(solution)/shard_map/all_gather | solution.py:294
  9.3 23.4 %all-to-all-start = ((f32[8,13,16,128]{3,2,1,0:T(8,128)}), f32[8,13,16,128]{3,2,1,0:T(8,128)S(1)}, u32[]{:S(2)}, u32[]{:S(2)}) async-start(f32[8,13,16,128]{3,2,1,0:T(8,128)} %get-tuple-element.11), calls=%async_computation | async-start | bytes 1703936 | tf_op jit(solution)/shard_map/all_to_all | solution.py:293
  19.6 13.9 %collective-permute-start = (f32[12,128,128]{2,1,0:T(8,128)}, f32[12,128,128]{2,1,0:T(8,128)S(1)}, u32[]{:S(2)}, u32[]{:S(2)}) collective-permute-start(f32[12,128,128]{2,1,0:T(8,128)} %bitcast.12), channel_id=1, source_target_pairs={{0,4},{4,0},{1,5},{5,1},{2,6},{6,2},{3,7},{7,3},{8,12},{12,8},{9,1... | collective-permute-start | bytes 2359304 | tf_op jit(solution)/shard_map/ppermute | solution.py:272
  32.6 0.9 copy-start.1
  33.5 0.9 copy-start.3
  34.4 9.7 %copy-start.2 = (f32[12,1,128,128]{3,2,1,0:T(8,128)S(1)}, f32[12,1,128,128]{3,2,1,0:T(8,128)}, u32[]{:S(2)}) copy-start(f32[12,1,128,128]{3,2,1,0:T(8,128)} %param.9) | copy-start | bytes 2359300
  40.4 19.7 %all-to-all-start.1 = ((f32[16,16,8,128]{3,2,1,0:T(8,128)}), f32[16,16,8,128]{3,2,1,0:T(8,128)S(1)}, u32[]{:S(2)}, u32[]{:S(2)}) async-start(f32[16,16,8,128]{3,2,1,0:T(8,128)} %get-tuple-element.12), calls=%async_computation.1 | async-start | bytes 2097152 | tf_op jit(solution)/shard_map/all_to_all | solution.py:303
  44.0 49.5 %collective-permute-start.1 = (f32[12,128,128]{2,1,0:T(8,128)S(1)}, f32[12,128,128]{2,1,0:T(8,128)S(1)}, u32[]{:S(2)}, u32[]{:S(2)}) collective-permute-start(f32[12,128,128]{2,1,0:T(8,128)S(1)} %bitcast.15), channel_id=1, source_target_pairs={{0,24},{8,0},{16,8},{24,16},{1,25},{9,1},{17,9},{25,17},{2,26},{10... | collective-permute-start | bytes 2359304 | tf_op jit(solution)/shard_map/ppermute | solution.py:277
  48.5 45.0 %collective-permute-start.2 = (f32[12,128,128]{2,1,0:T(8,128)S(1)}, f32[12,128,128]{2,1,0:T(8,128)}, u32[]{:S(2)}, u32[]{:S(2)}) collective-permute-start(f32[12,128,128]{2,1,0:T(8,128)S(1)} %bitcast.16), channel_id=1, source_target_pairs={{0,8},{8,16},{16,24},{24,0},{1,9},{9,17},{17,25},{25,1},{2,10},{10... | collective-permute-start | bytes 2359304 | tf_op jit(solution)/shard_map/ppermute | solution.py:277
  67.3 40.8 %collective-permute-start.4 = (f32[12,128,128]{2,1,0:T(8,128)S(1)}, f32[12,128,128]{2,1,0:T(8,128)S(1)}, u32[]{:S(2)}, u32[]{:S(2)}) collective-permute-start(f32[12,128,128]{2,1,0:T(8,128)S(1)} %bitcast.17), channel_id=1, source_target_pairs={{0,16},{8,24},{16,0},{24,8},{1,17},{9,25},{17,1},{25,9},{2,18},{10... | collective-permute-start | bytes 2359304 | tf_op jit(solution)/shard_map/ppermute | solution.py:277
  93.5 24.6 %copy-start.5 = (f32[12,128,128]{2,1,0:T(8,128)}, f32[12,128,128]{2,1,0:T(8,128)S(1)}, u32[]{:S(2)}) copy-start(f32[12,128,128]{2,1,0:T(8,128)S(1)} %collective-permute-done.1.refs_2_) | copy-start | bytes 2359300
  94.4 16.1 %all-to-all-start.4 = ((f32[16,4,8,128]{3,2,1,0:T(8,128)}), f32[16,4,8,128]{3,2,1,0:T(8,128)S(1)}, u32[]{:S(2)}, u32[]{:S(2)}) async-start(f32[16,4,8,128]{3,2,1,0:T(8,128)} %broadcast_in_dim.7), calls=%async_computation.4 | async-start | bytes 524288 | tf_op jit(solution)/shard_map/all_to_all | solution.py:268
  99.4 18.7 %collective-permute-start.3 = (f32[12,128,128]{2,1,0:T(8,128)S(1)}, f32[12,128,128]{2,1,0:T(8,128)}, u32[]{:S(2)}, u32[]{:S(2)}) collective-permute-start(f32[12,128,128]{2,1,0:T(8,128)S(1)} %collective-permute-done.1.refs_2_), channel_id=1, source_target_pairs={{0,4},{4,0},{1,5},{5,1},{2,6},{6,2},{3,7},{7,3},{8,12},{12,8},{9,1... | collective-permute-start | bytes 2359304 | tf_op jit(solution)/shard_map/ppermute | solution.py:272
  106.2 11.9 %collective-permute-start.6 = (f32[12,128,128]{2,1,0:T(8,128)}, f32[12,128,128]{2,1,0:T(8,128)}, u32[]{:S(2)}, u32[]{:S(2)}) collective-permute-start(f32[12,128,128]{2,1,0:T(8,128)} %collective-permute-done.2.refs_6_), channel_id=1, source_target_pairs={{0,4},{4,0},{1,5},{5,1},{2,6},{6,2},{3,7},{7,3},{8,12},{12,8},{9,1... | collective-permute-start | bytes 2359304 | tf_op jit(solution)/shard_map/ppermute | solution.py:272
  108.1 10.0 %copy-start.6 = (f32[12,128,128]{2,1,0:T(8,128)}, f32[12,128,128]{2,1,0:T(8,128)S(1)}, u32[]{:S(2)}) copy-start(f32[12,128,128]{2,1,0:T(8,128)S(1)} %collective-permute-done.4.refs_4_) | copy-start | bytes 2359300
  108.1 9.9 %collective-permute-start.5 = (f32[12,128,128]{2,1,0:T(8,128)S(1)}, f32[12,128,128]{2,1,0:T(8,128)S(1)}, u32[]{:S(2)}, u32[]{:S(2)}) collective-permute-start(f32[12,128,128]{2,1,0:T(8,128)S(1)} %collective-permute-done.4.refs_4_), channel_id=1, source_target_pairs={{0,4},{4,0},{1,5},{5,1},{2,6},{6,2},{3,7},{7,3},{8,12},{12,8},{9,1... | collective-permute-start | bytes 2359304 | tf_op jit(solution)/shard_map/ppermute | solution.py:272
  110.5 0.7 copy-start.4
  118.1 0.9 copy-start.7
Sparse Core Ops, SparseCore 0:
  10.7 70.4 all-gather.2

commit v7 on v6

--- a/solution.py
+++ b/solution.py
@@ -9,7 +9,7 @@
 BF16 = jnp.bfloat16
 ROWS = ("rhi", "rlo")
 COLS = ("y", "core")
-STEP = 4
+STEP = 6
 
 
 def dot(a, b, cb=0):
@@ -142,17 +142,26 @@
     def maps(t, kind):
         return maps_ref[t, kind]
 
+    pairs = [None] + [dot3(maps(t + 1, 1), maps(t, 1)) for t in range(2, tops, 2)]
+    local = [row_dot(rhs(t), maps(t, 0), 1) for t in range(tops)]
+    both = [local[t + 1] + row_dot(local[t], maps(t + 1, 1), 1) for t in range(0, tops, 2)]
+    odd = [both[0]]
+    for k in range(1, tops // 2):
+        odd.append(both[k] + row_dot(odd[-1], pairs[k], 1))
     solved = []
-    current = row_dot(rhs(0), maps(0, 0), 1)
-    solved.append(current)
-    for t in range(1, tops):
-        current = row_dot(rhs(t), maps(t, 0), 1) + row_dot(current, maps(t, 1), 1)
-        solved.append(current)
-    rest = solved[tops - 1]
-    out_ref[tops - 1] = row_dot(rest, maps(tops - 1, 0))
-    for t in range(tops - 2, -1, -1):
-        rest = solved[t] + row_dot(rest, maps(t + 1, 1))
-        out_ref[t] = row_dot(rest, maps(t, 0))
+    for k in range(tops // 2):
+        t = 2 * k
+        solved.append(local[t] + row_dot(odd[k - 1], maps(t, 1), 1) if k else local[0])
+        solved.append(odd[k])
+    rest = [None] * tops
+    rest[tops - 1] = solved[tops - 1]
+    for k in range(tops // 2 - 1, 0, -1):
+        ahead = solved[2 * k - 1] + row_dot(solved[2 * k], maps(2 * k, 1))
+        rest[2 * k - 1] = ahead + row_dot(rest[2 * k + 1], pairs[k])
+    for t in range(tops - 2, -1, -2):
+        rest[t] = solved[t] + row_dot(rest[t + 1], maps(t + 1, 1))
+    for t in range(tops):
+        out_ref[t] = row_dot(rest[t], maps(t, 0))
 
 
 def top_chain(rhs, maps):

time: 151 us -> 149 us (0.987)
  Pallas kernels: 23.7 us -> 21.8 us
  transfers between devices with their start and end apart: 11 -> 11, of which waited for: 2 -> 2; matrix products, arithmetic and copies ran while one was open for 2% -> 2% of each run, Pallas kernels for 9% -> 7%
where the time goes in v7:
time: 149 us; the launch traced here: 148 us
  blocking collectives  46.5 us (31%)
  starting transfers between devices  40.4 us (27%)
  Pallas kernels  21.8 us (15%)
  waiting for transfers between devices  19.4 us (13%)
  between operations  14.3 us (10%)
  local copies, waits for them, and re-layouts  4.09 us (3%)
  other arithmetic  1.5 us (1%)
    all_to_all x1, blocking collectives, spread(): lax.all_to_all(jnp.broadcast_to(x, (n,) + x.shape), axis, 0, 0, tiled=True)  24.1 us
    all_to_all x1, blocking collectives, on_device(): got = lax.all_to_all(turned, COLS, 0, 0, tiled=True)  15.2 us
    ppermute x4, starting transfers between devices, from_core(): return lax.ppermute(x, 'core', [(0, 1), (1, 0)])  12.5 us
    all_to_all x1, starting transfers between devices, on_device(): inv = lax.all_to_all(packed, COLS, 0, 0, tiled=True)  10.3 us
    all_to_all x1, waiting for transfers between devices, on_device(): partial = lax.all_to_all(sums, ('y', 'layers'), 0, 0, tiled=True).sum(0)  9.66 us
    all_to_all x1, waiting for transfers between devices, on_device(): inv = lax.all_to_all(packed, COLS, 0, 0, tiled=True)  9.66 us
    ppermute x3, starting transfers between devices, from_y(): return lax.ppermute(x, 'y', [(i, (i - step) % n) for i in range(n)])  8.75 us
    all_to_all x1, blocking collectives, on_device(): quarter = lax.all_to_all(partial, 'rlo', 0, 0, tiled=True)  7.18 us
  transfers between devices with their start and end apart: 11, of which 2 were waited for; matrix products, arithmetic and copies ran while one was open for 2% of the time, Pallas kernels for 7%

profile of v7, /device:TPU:1, one launch (start us, length us, event | category | flops | bytes accessed | tf_op | source)
XLA Modules:
  0.0 147.9 jit_solution(11809841899511839734)
XLA Ops:
  7.2 2.0 %prepare.1 = (f32[8,13,16,128]{3,2,1,0:T(8,128)}, f32[2,128,128]{2,1,0:T(8,128)}) custom-call(s32[12]{0:T(128)} %bitcast.22, f32[12,16,128]{2,1,0:T(8,128)} %pivot_ref.1, f32[1,128,128]{2,1,0:T(8,128)} %inv_ref.1, f32[1,128,128]{2,1,0:T(8,128)} %sub_ref.1), custom_call_target="tpu_custom_call" | custom-call | tf_op jit(solution)/shard_map/prepare/pallas_call | solution.py:68
  9.3 10.3 %all-to-all-start = ((f32[8,13,16,128]{3,2,1,0:T(8,128)}), f32[8,13,16,128]{3,2,1,0:T(8,128)S(1)}, u32[]{:S(2)}, u32[]{:S(2)}) async-start(f32[8,13,16,128]{3,2,1,0:T(8,128)} %get-tuple-element.11), calls=%async_computation | async-start | bytes 1703936 | tf_op jit(solution)/shard_map/all_to_all | solution.py:302
  19.6 2.0 %collective-permute-start = (f32[12,128,128]{2,1,0:T(8,128)}, f32[12,128,128]{2,1,0:T(8,128)S(1)}, u32[]{:S(2)}, u32[]{:S(2)}) collective-permute-start(f32[12,128,128]{2,1,0:T(8,128)} %bitcast.12), channel_id=1, source_target_pairs={{0,4},{4,0},{1,5},{5,1},{2,6},{6,2},{3,7},{7,3},{8,12},{12,8},{9,1... | collective-permute-start | bytes 2359304 | tf_op jit(solution)/shard_map/ppermute | solution.py:281
  23.0 9.7 %all-to-all-done.inv_ref.refs_9_ = f32[8,13,16,128]{3,2,1,0:T(8,128)S(1)} async-done(((f32[8,13,16,128]{3,2,1,0:T(8,128)}), f32[8,13,16,128]{3,2,1,0:T(8,128)S(1)}, u32[]{:S(2)}, u32[]{:S(2)}) %all-to-all-start) | async-done | bytes 852000 | tf_op jit(solution)/shard_map/all_to_all | solution.py:302
  32.6 0.9 fusion.targets_ref
  33.5 0.9 copy-done.3
  34.4 5.6 %leaf_forward.1 = (f32[16,16,8,128]{3,2,1,0:T(8,128)}, f32[12,32,128]{2,1,0:T(8,128)}) custom-call(s32[4]{0:T(128)} %pad_add_fusion.place_ref, s32[8,12]{1,0:T(8,128)} %fusion.targets_ref, f32[8,128]{1,0:T(8,128)} %bitcast.21, f32[8,13,16,128]{3,2,1,0:T(8,128)} %copy-done.1, f32[12,128,128]{2,1,0:T(8,128)} %bitcast.13, f32[12,128,128]{2,1,0:T(8,128)} %copy-done.3, ...), custom_call_target="tpu_custom_call" | custom-call | tf_op jit(solution)/shard_map/leaf_forward/pallas_call | solution.py:109
  39.9 3.7 %all-to-all-start.1 = ((f32[16,16,8,128]{3,2,1,0:T(8,128)}), f32[16,16,8,128]{3,2,1,0:T(8,128)S(1)}, u32[]{:S(2)}, u32[]{:S(2)}) async-start(f32[16,16,8,128]{3,2,1,0:T(8,128)} %get-tuple-element.12), calls=%async_computation.1 | async-start | bytes 2097152 | tf_op jit(solution)/shard_map/all_to_all | solution.py:312
  43.6 4.4 %collective-permute-start.1 = (f32[12,128,128]{2,1,0:T(8,128)S(1)}, f32[12,128,128]{2,1,0:T(8,128)S(1)}, u32[]{:S(2)}, u32[]{:S(2)}) collective-permute-start(f32[12,128,128]{2,1,0:T(8,128)S(1)} %bitcast.15), channel_id=1, source_target_pairs={{0,24},{8,0},{16,8},{24,16},{1,25},{9,1},{17,9},{25,17},{2,26},{10... | collective-permute-start | bytes 2359304 | tf_op jit(solution)/shard_map/ppermute | solution.py:286
  48.1 1.9 %collective-permute-start.2 = (f32[12,128,128]{2,1,0:T(8,128)S(1)}, f32[12,128,128]{2,1,0:T(8,128)}, u32[]{:S(2)}, u32[]{:S(2)}) collective-permute-start(f32[12,128,128]{2,1,0:T(8,128)S(1)} %bitcast.16), channel_id=1, source_target_pairs={{0,8},{8,16},{16,24},{24,0},{1,9},{9,17},{17,25},{25,1},{2,10},{10... | collective-permute-start | bytes 2359304 | tf_op jit(solution)/shard_map/ppermute | solution.py:286
  50.0 9.7 %all-to-all-done.1 = f32[16,16,8,128]{3,2,1,0:T(8,128)S(1)} async-done(((f32[16,16,8,128]{3,2,1,0:T(8,128)}), f32[16,16,8,128]{3,2,1,0:T(8,128)S(1)}, u32[]{:S(2)}, u32[]{:S(2)}) %all-to-all-start.1) | async-done | bytes 1048608 | tf_op jit(solution)/shard_map/all_to_all | solution.py:312
  59.7 7.2 %all_to_all.30 = f32[16,8,128]{2,1,0:T(8,128)S(1)} all-to-all(f32[16,8,128]{2,1,0:T(8,128)S(1)} %reduce_sum.27), channel_id=1, replica_groups=mesh['rhi'=4,'rlo'=4,'y'=4,'core'=2,'layers'=4] {'rlo'}, dimensions={0} | all-to-all | bytes 131072 | tf_op jit(solution)/shard_map/all_to_all | solution.py:314
  66.9 2.4 %collective-permute-start.4 = (f32[12,128,128]{2,1,0:T(8,128)S(1)}, f32[12,128,128]{2,1,0:T(8,128)S(1)}, u32[]{:S(2)}, u32[]{:S(2)}) collective-permute-start(f32[12,128,128]{2,1,0:T(8,128)S(1)} %bitcast.17), channel_id=1, source_target_pairs={{0,16},{8,24},{16,0},{24,8},{1,17},{9,25},{17,1},{25,9},{2,18},{10... | collective-permute-start | bytes 2359304 | tf_op jit(solution)/shard_map/ppermute | solution.py:286
  69.3 24.1 %all_to_all.31 = f32[4,4,8,128]{3,2,1,0:T(8,128)S(1)} all-to-all(f32[4,4,8,128]{3,2,1,0:T(8,128)S(1)} %broadcast_in_dim.6), channel_id=1, replica_groups=mesh['rhi'=4,'rlo'=4,'y'=4,'core'=2,'layers'=4] {'rhi'}, dimensions={0} | all-to-all | bytes 131072 | tf_op jit(solution)/shard_map/all_to_all | solution.py:277
  93.5 0.9 broadcast_in_dim.7
  94.3 5.0 %all-to-all-start.4 = ((f32[16,4,8,128]{3,2,1,0:T(8,128)}), f32[16,4,8,128]{3,2,1,0:T(8,128)S(1)}, u32[]{:S(2)}, u32[]{:S(2)}) async-start(f32[16,4,8,128]{3,2,1,0:T(8,128)} %broadcast_in_dim.7), calls=%async_computation.4 | async-start | bytes 524288 | tf_op jit(solution)/shard_map/all_to_all | solution.py:277
  99.4 6.2 %collective-permute-start.3 = (f32[12,128,128]{2,1,0:T(8,128)S(1)}, f32[12,128,128]{2,1,0:T(8,128)}, u32[]{:S(2)}, u32[]{:S(2)}) collective-permute-start(f32[12,128,128]{2,1,0:T(8,128)S(1)} %collective-permute-done.1.refs_2_), channel_id=1, source_target_pairs={{0,4},{4,0},{1,5},{5,1},{2,6},{6,2},{3,7},{7,3},{8,12},{12,8},{9,1... | collective-permute-start | bytes 2359304 | tf_op jit(solution)/shard_map/ppermute | solution.py:281
  105.6 1.9 %collective-permute-start.6 = (f32[12,128,128]{2,1,0:T(8,128)}, f32[12,128,128]{2,1,0:T(8,128)}, u32[]{:S(2)}, u32[]{:S(2)}) collective-permute-start(f32[12,128,128]{2,1,0:T(8,128)} %collective-permute-done.2.refs_6_), channel_id=1, source_target_pairs={{0,4},{4,0},{1,5},{5,1},{2,6},{6,2},{3,7},{7,3},{8,12},{12,8},{9,1... | collective-permute-start | bytes 2359304 | tf_op jit(solution)/shard_map/ppermute | solution.py:281
  107.5 2.4 %collective-permute-start.5 = (f32[12,128,128]{2,1,0:T(8,128)S(1)}, f32[12,128,128]{2,1,0:T(8,128)S(1)}, u32[]{:S(2)}, u32[]{:S(2)}) collective-permute-start(f32[12,128,128]{2,1,0:T(8,128)S(1)} %collective-permute-done.4.refs_4_), channel_id=1, source_target_pairs={{0,4},{4,0},{1,5},{5,1},{2,6},{6,2},{3,7},{7,3},{8,12},{12,8},{9,1... | collective-permute-start | bytes 2359304 | tf_op jit(solution)/shard_map/ppermute | solution.py:281
  110.7 5.3 %top_chain.1.tops_ref = f32[16,32,128]{2,1,0:T(8,128)} custom-call(f32[4,4,4,8,128]{4,3,2,1,0:T(8,128)} %bitcast.19, f32[16,2,128,128]{3,2,1,0:T(8,128)} %bitcast.18), custom_call_target="tpu_custom_call" | custom-call | tf_op jit(solution)/shard_map/top_chain/pallas_call | solution.py:169
  116.0 0.9 copy-done.7
  116.9 7.0 %leaf_backward.1 = f32[8,80,128]{2,1,0:T(8,128)} custom-call(s32[4]{0:T(128)} %pad_add_fusion.place_ref, s32[8,12]{1,0:T(8,128)} %fusion.targets_ref, f32[16,32,128]{2,1,0:T(8,128)} %top_chain.1.tops_ref, f32[12,128,128]{2,1,0:T(8,128)} %bitcast.14, f32[12,128,128]{2,1,0:T(8,128)} %copy-done.3, f32[12,128,128]{2,1,0:T(8,128)} %copy-done.5, ...), custom_call_target="tpu_custom_call" | custom-call | tf_op jit(solution)/shard_map/leaf_backward/pallas_call | solution.py:223
  123.9 15.2 %all_to_all.32.got_ref = f32[8,80,128]{2,1,0:T(8,128)} all-to-all(f32[8,80,128]{2,1,0:T(8,128)} %leaf_backward.1), channel_id=1, replica_groups=mesh['rhi'=4,'rlo'=4,'y'=4,'core'=2,'layers'=4] {'y','core'}, dimensions={0} | all-to-all | bytes 655360 | tf_op jit(solution)/shard_map/all_to_all | solution.py:328
  139.1 1.9 %arrange.1 = (f32[12,16,256]{2,1,0:T(8,128)}, f32[1,128,256]{2,1,0:T(8,128)}) custom-call(f32[8,80,128]{2,1,0:T(8,128)} %all_to_all.32.got_ref), custom_call_target="tpu_custom_call" | custom-call | tf_op jit(solution)/shard_map/arrange/pallas_call | solution.py:265
  (32 shorter events, 2.2 us)
Async XLA Ops:
  7.2 14.5 %copy-start = (f32[1,128,256]{2,1,0:T(8,128)S(1)}, f32[1,128,256]{2,1,0:T(8,128)}, u32[]{:S(2)}) copy-start(f32[1,128,256]{2,1,0:T(8,128)} %param.11) | copy-start | bytes 393220
  7.2 102.8 %all-gather.3.cloned.1.call-start = ((), (), s32[]{:S(2)}) async-start(), calls=%async_computation.6 | async-start | bytes 2228224 | tf_op jit(solution)/shard_map/all_gather | solution.py:303
  9.3 23.4 %all-to-all-start = ((f32[8,13,16,128]{3,2,1,0:T(8,128)}), f32[8,13,16,128]{3,2,1,0:T(8,128)S(1)}, u32[]{:S(2)}, u32[]{:S(2)}) async-start(f32[8,13,16,128]{3,2,1,0:T(8,128)} %get-tuple-element.11), calls=%async_computation | async-start | bytes 1703936 | tf_op jit(solution)/shard_map/all_to_all | solution.py:302
  19.6 13.9 %collective-permute-start = (f32[12,128,128]{2,1,0:T(8,128)}, f32[12,128,128]{2,1,0:T(8,128)S(1)}, u32[]{:S(2)}, u32[]{:S(2)}) collective-permute-start(f32[12,128,128]{2,1,0:T(8,128)} %bitcast.12), channel_id=1, source_target_pairs={{0,4},{4,0},{1,5},{5,1},{2,6},{6,2},{3,7},{7,3},{8,12},{12,8},{9,1... | collective-permute-start | bytes 2359304 | tf_op jit(solution)/shard_map/ppermute | solution.py:281
  32.6 0.9 copy-start.1
  33.5 0.9 copy-start.3
  34.4 9.2 %copy-start.2 = (f32[12,1,128,128]{3,2,1,0:T(8,128)S(1)}, f32[12,1,128,128]{3,2,1,0:T(8,128)}, u32[]{:S(2)}) copy-start(f32[12,1,128,128]{3,2,1,0:T(8,128)} %param.9) | copy-start | bytes 2359300
  39.9 19.7 %all-to-all-start.1 = ((f32[16,16,8,128]{3,2,1,0:T(8,128)}), f32[16,16,8,128]{3,2,1,0:T(8,128)S(1)}, u32[]{:S(2)}, u32[]{:S(2)}) async-start(f32[16,16,8,128]{3,2,1,0:T(8,128)} %get-tuple-element.12), calls=%async_computation.1 | async-start | bytes 2097152 | tf_op jit(solution)/shard_map/all_to_all | solution.py:312
  43.6 49.8 %collective-permute-start.1 = (f32[12,128,128]{2,1,0:T(8,128)S(1)}, f32[12,128,128]{2,1,0:T(8,128)S(1)}, u32[]{:S(2)}, u32[]{:S(2)}) collective-permute-start(f32[12,128,128]{2,1,0:T(8,128)S(1)} %bitcast.15), channel_id=1, source_target_pairs={{0,24},{8,0},{16,8},{24,16},{1,25},{9,1},{17,9},{25,17},{2,26},{10... | collective-permute-start | bytes 2359304 | tf_op jit(solution)/shard_map/ppermute | solution.py:286
  48.1 45.4 %collective-permute-start.2 = (f32[12,128,128]{2,1,0:T(8,128)S(1)}, f32[12,128,128]{2,1,0:T(8,128)}, u32[]{:S(2)}, u32[]{:S(2)}) collective-permute-start(f32[12,128,128]{2,1,0:T(8,128)S(1)} %bitcast.16), channel_id=1, source_target_pairs={{0,8},{8,16},{16,24},{24,0},{1,9},{9,17},{17,25},{25,1},{2,10},{10... | collective-permute-start | bytes 2359304 | tf_op jit(solution)/shard_map/ppermute | solution.py:286
  66.9 40.6 %collective-permute-start.4 = (f32[12,128,128]{2,1,0:T(8,128)S(1)}, f32[12,128,128]{2,1,0:T(8,128)S(1)}, u32[]{:S(2)}, u32[]{:S(2)}) collective-permute-start(f32[12,128,128]{2,1,0:T(8,128)S(1)} %bitcast.17), channel_id=1, source_target_pairs={{0,16},{8,24},{16,0},{24,8},{1,17},{9,25},{17,1},{25,9},{2,18},{10... | collective-permute-start | bytes 2359304 | tf_op jit(solution)/shard_map/ppermute | solution.py:286
  93.5 22.6 %copy-start.5 = (f32[12,128,128]{2,1,0:T(8,128)}, f32[12,128,128]{2,1,0:T(8,128)S(1)}, u32[]{:S(2)}) copy-start(f32[12,128,128]{2,1,0:T(8,128)S(1)} %collective-permute-done.1.refs_2_) | copy-start | bytes 2359300
  94.3 15.6 %all-to-all-start.4 = ((f32[16,4,8,128]{3,2,1,0:T(8,128)}), f32[16,4,8,128]{3,2,1,0:T(8,128)S(1)}, u32[]{:S(2)}, u32[]{:S(2)}) async-start(f32[16,4,8,128]{3,2,1,0:T(8,128)} %broadcast_in_dim.7), calls=%async_computation.4 | async-start | bytes 524288 | tf_op jit(solution)/shard_map/all_to_all | solution.py:277
  99.4 16.6 %collective-permute-start.3 = (f32[12,128,128]{2,1,0:T(8,128)S(1)}, f32[12,128,128]{2,1,0:T(8,128)}, u32[]{:S(2)}, u32[]{:S(2)}) collective-permute-start(f32[12,128,128]{2,1,0:T(8,128)S(1)} %collective-permute-done.1.refs_2_), channel_id=1, source_target_pairs={{0,4},{4,0},{1,5},{5,1},{2,6},{6,2},{3,7},{7,3},{8,12},{12,8},{9,1... | collective-permute-start | bytes 2359304 | tf_op jit(solution)/shard_map/ppermute | solution.py:281
  105.6 10.4 %collective-permute-start.6 = (f32[12,128,128]{2,1,0:T(8,128)}, f32[12,128,128]{2,1,0:T(8,128)}, u32[]{:S(2)}, u32[]{:S(2)}) collective-permute-start(f32[12,128,128]{2,1,0:T(8,128)} %collective-permute-done.2.refs_6_), channel_id=1, source_target_pairs={{0,4},{4,0},{1,5},{5,1},{2,6},{6,2},{3,7},{7,3},{8,12},{12,8},{9,1... | collective-permute-start | bytes 2359304 | tf_op jit(solution)/shard_map/ppermute | solution.py:281
  107.5 8.5 %copy-start.6 = (f32[12,128,128]{2,1,0:T(8,128)}, f32[12,128,128]{2,1,0:T(8,128)S(1)}, u32[]{:S(2)}) copy-start(f32[12,128,128]{2,1,0:T(8,128)S(1)} %collective-permute-done.4.refs_4_) | copy-start | bytes 2359300
  107.5 8.5 %collective-permute-start.5 = (f32[12,128,128]{2,1,0:T(8,128)S(1)}, f32[12,128,128]{2,1,0:T(8,128)S(1)}, u32[]{:S(2)}, u32[]{:S(2)}) collective-permute-start(f32[12,128,128]{2,1,0:T(8,128)S(1)} %collective-permute-done.4.refs_4_), channel_id=1, source_target_pairs={{0,4},{4,0},{1,5},{5,1},{2,6},{6,2},{3,7},{7,3},{8,12},{12,8},{9,1... | collective-permute-start | bytes 2359304 | tf_op jit(solution)/shard_map/ppermute | solution.py:281
  110.0 0.7 copy-start.4
  116.0 0.9 copy-start.7
Sparse Core Ops, SparseCore 0:
  10.7 70.2 all-gather.2

commit v8 on v7

--- a/solution.py
+++ b/solution.py
@@ -173,11 +173,32 @@
     )(rhs, maps)
 
 
+def halves_kernel(mine_ref, pair_ref, high_ref, low_ref):
+    b = mine_ref.shape[1]
+    for k, ref in enumerate((mine_ref, pair_ref)):
+        for i in range(ref.shape[0]):
+            high_ref[i, k * b : (k + 1) * b], low_ref[i, k * b : (k + 1) * b] = split(ref[i])
+
+
+def halves(mine, pair):
+    leaves, b, _ = mine.shape
+    block = pl.BlockSpec((STEP, b, b), lambda i: (i, 0, 0))
+    out = pl.BlockSpec((STEP, 2 * b, b), lambda i: (i, 0, 0))
+    return pl.pallas_call(
+        halves_kernel,
+        grid=(leaves // STEP,),
+        in_specs=[block] * 2,
+        out_specs=[out] * 2,
+        out_shape=[jax.ShapeDtypeStruct((leaves, 2 * b, b), BF16)] * 2,
+        name="halves",
+    )(mine, pair)
+
+
 def leaf_backward_kernel(place_ref, targets_ref, tops_ref, *refs):
-    *block_refs, own_ref, inv_ref, out_ref, parts = refs
+    high_ref, low_ref, *block_refs, own_ref, inv_ref, out_ref, parts = refs
     core, y, _, row = (place_ref[k] for k in range(4))
     step = pl.program_id(0)
-    n_cols = len(block_refs)
+    n_cols = len(block_refs) + 2
     count, b, _ = block_refs[0].shape
     own = own_ref.shape[1]
     slab = b // n_cols
@@ -203,6 +224,8 @@
             axis=1,
         )
         high, low = split(jnp.concatenate([ref[i] for ref in block_refs], axis=0))
+        high = jnp.concatenate([high_ref[i], high], axis=0)
+        low = jnp.concatenate([low_ref[i], low], axis=0)
         r = dot(both, high)
         left = own_ref[i] - ((r[:own] + r[own:]) + dot(both[:own], low))
         results.append(dot3(left, inv_ref[:, i].reshape(b, b)))
@@ -213,8 +236,8 @@
         ]
 
 
-def leaf_backward(place, targets, tops, blocks, own, inv):
-    n_cols = len(blocks)
+def leaf_backward(place, targets, tops, near, blocks, own, inv):
+    n_cols = len(blocks) + 2
     leaves, b, _ = blocks[0].shape
     mine = own.shape[1]
     slab = b // n_cols
@@ -226,7 +249,8 @@
             num_scalar_prefetch=2,
             grid=(leaves // step,),
             in_specs=[whole(tops.shape)]
-            + [pl.BlockSpec((step, b, b), lambda i, *_: (i, 0, 0))] * n_cols
+            + [pl.BlockSpec((step, 2 * b, b), lambda i, *_: (i, 0, 0))] * 2
+            + [pl.BlockSpec((step, b, b), lambda i, *_: (i, 0, 0))] * len(blocks)
             + [
                 pl.BlockSpec((step, mine, b), lambda i, *_: (i, 0, 0)),
                 pl.BlockSpec((n_cols, step, slab, b), lambda i, *_: (0, i, 0, 0)),
@@ -236,7 +260,7 @@
         ),
         out_shape=jax.ShapeDtypeStruct(out, F32),
         name="leaf_backward",
-    )(place, targets, tops, *blocks, own, inv)
+    )(place, targets, tops, *near, *blocks, own, inv)
 
 
 def arrange_kernel(got_ref, leaf_ref, top_ref):
@@ -309,7 +333,11 @@
     place = jnp.stack([core, y, part, row])
     rhs_t = lax.dynamic_slice_in_dim(top_rhs[0], core * (r // 2) + part * 8, 8, 1).T
     sums, own_forward = leaf_forward(place, targets, rhs_t, inv, blocks, paired, known, tops)
-    partial = lax.all_to_all(sums, ("y", "layers"), 0, 0, tiled=True).sum(0)
+    near, sums = lax.optimization_barrier(((blocks, paired), sums))
+    near = halves(*near)
+    partial = lax.all_to_all(sums, ("y", "layers"), 0, 0, tiled=True)
+    partial, near = lax.optimization_barrier((partial, near))
+    partial = partial.sum(0)
 
     quarter = lax.all_to_all(partial, "rlo", 0, 0, tiled=True)
     quarter = quarter.reshape((lax.axis_size("rlo"), -1) + quarter.shape[1:]).sum(0)
@@ -317,14 +345,14 @@
     far[1] = from_y(held, 2)
     quarter = spread(quarter, "rhi").sum(0)
     quarter, far[0], far[2] = lax.optimization_barrier((quarter, far[0], far[2]))
-    all_blocks = [blocks, paired]
+    all_blocks = []
     for block in far:
         all_blocks += [block, from_core(block)]
     rhs = spread(quarter, ("rlo", "layers"))
     rhs = rhs.reshape((lax.axis_size("rlo"), -1) + rhs.shape[1:])
 
     own_tops = top_chain(rhs, maps)
-    turned = leaf_backward(place, targets, own_tops, all_blocks, own_forward, inv)
+    turned = leaf_backward(place, targets, own_tops, near, all_blocks, own_forward, inv)
     got = lax.all_to_all(turned, COLS, 0, 0, tiled=True)
     return tuple(arrange(got, leaves, r))
 

time: 149 us -> 150 us (level)
  waiting for transfers between devices: 19.4 us -> 16.9 us
  Pallas kernels: 21.8 us -> 24.1 us
    all_to_all x1, waiting for transfers between devices: 9.66 us -> 7.27 us  [on_device(): partial = lax.all_to_all(sums, ('y', 'layers'), 0, 0, tiled=True)]
    pallas_call x0 -> x1, Pallas kernels: none -> 2.39 us  [halves(): pl.pallas_call(halves_kernel, grid=(leaves // STEP,), in_specs=[block] *...]
  transfers between devices with their start and end apart: 11 -> 11, of which waited for: 2 -> 2; matrix products, arithmetic and copies ran while one was open for 2% -> 3% of each run, Pallas kernels for 7% -> 9%
where the time goes in v8:
time: 150 us; the launch traced here: 149 us
  blocking collectives  46.8 us (31%)
  starting transfers between devices  40.7 us (27%)
  Pallas kernels  24.1 us (16%)
  waiting for transfers between devices  16.9 us (11%)
  between operations  14.3 us (10%)
  local copies, waits for them, and re-layouts  4.36 us (3%)
  other arithmetic  2.18 us (1%)
    all_to_all x1, blocking collectives, spread(): lax.all_to_all(jnp.broadcast_to(x, (n,) + x.shape), axis, 0, 0, tiled=True)  23.3 us
    all_to_all x1, blocking collectives, on_device(): got = lax.all_to_all(turned, COLS, 0, 0, tiled=True)  15.2 us
    ppermute x4, starting transfers between devices, from_core(): return lax.ppermute(x, 'core', [(0, 1), (1, 0)])  13 us
    all_to_all x1, starting transfers between devices, on_device(): inv = lax.all_to_all(packed, COLS, 0, 0, tiled=True)  10.3 us
    all_to_all x1, waiting for transfers between devices, on_device(): inv = lax.all_to_all(packed, COLS, 0, 0, tiled=True)  9.6 us
    ppermute x3, starting transfers between devices, from_y(): return lax.ppermute(x, 'y', [(i, (i - step) % n) for i in range(n)])  8.38 us
    all_to_all x1, blocking collectives, on_device(): quarter = lax.all_to_all(partial, 'rlo', 0, 0, tiled=True)  8.35 us
    all_to_all x1, waiting for transfers between devices, on_device(): partial = lax.all_to_all(sums, ('y', 'layers'), 0, 0, tiled=True)  7.27 us
  transfers between devices with their start and end apart: 11, of which 2 were waited for; matrix products, arithmetic and copies ran while one was open for 3% of the time, Pallas kernels for 9%

profile of v8, /device:TPU:1, one launch (start us, length us, event | category | flops | bytes accessed | tf_op | source)
XLA Modules:
  0.0 149.3 jit_solution(13202014481306721351)
XLA Ops:
  7.2 2.0 %prepare.1 = (f32[8,13,16,128]{3,2,1,0:T(8,128)}, f32[2,128,128]{2,1,0:T(8,128)}) custom-call(s32[12]{0:T(128)} %bitcast.22, f32[12,16,128]{2,1,0:T(8,128)} %pivot_ref.1, f32[1,128,128]{2,1,0:T(8,128)} %inv_ref.1, f32[1,128,128]{2,1,0:T(8,128)} %sub_ref.1), custom_call_target="tpu_custom_call" | custom-call | tf_op jit(solution)/shard_map/prepare/pallas_call | solution.py:68
  9.3 10.3 %all-to-all-start = ((f32[8,13,16,128]{3,2,1,0:T(8,128)}), f32[8,13,16,128]{3,2,1,0:T(8,128)S(1)}, u32[]{:S(2)}, u32[]{:S(2)}) async-start(f32[8,13,16,128]{3,2,1,0:T(8,128)} %get-tuple-element.19), calls=%async_computation | async-start | bytes 1703936 | tf_op jit(solution)/shard_map/all_to_all | solution.py:326
  19.6 2.0 %collective-permute-start = (f32[12,128,128]{2,1,0:T(8,128)}, f32[12,128,128]{2,1,0:T(8,128)S(1)}, u32[]{:S(2)}, u32[]{:S(2)}) collective-permute-start(f32[12,128,128]{2,1,0:T(8,128)} %bitcast.12), channel_id=1, source_target_pairs={{0,4},{4,0},{1,5},{5,1},{2,6},{6,2},{3,7},{7,3},{8,12},{12,8},{9,1... | collective-permute-start | bytes 2359304 | tf_op jit(solution)/shard_map/ppermute | solution.py:305
  23.0 9.6 %all-to-all-done.inv_ref.refs_9_ = f32[8,13,16,128]{3,2,1,0:T(8,128)S(1)} async-done(((f32[8,13,16,128]{3,2,1,0:T(8,128)}), f32[8,13,16,128]{3,2,1,0:T(8,128)S(1)}, u32[]{:S(2)}, u32[]{:S(2)}) %all-to-all-start) | async-done | bytes 852000 | tf_op jit(solution)/shard_map/all_to_all | solution.py:326
  32.6 0.9 fusion.targets_ref
  33.5 0.9 copy-done.4
  34.4 5.6 %leaf_forward.1 = (f32[16,16,8,128]{3,2,1,0:T(8,128)}, f32[12,32,128]{2,1,0:T(8,128)}) custom-call(s32[4]{0:T(128)} %pad_add_fusion.place_ref, s32[8,12]{1,0:T(8,128)} %fusion.targets_ref, f32[8,128]{1,0:T(8,128)} %bitcast.21, f32[8,13,16,128]{3,2,1,0:T(8,128)} %copy-done.1, f32[12,128,128]{2,1,0:T(8,128)} %bitcast.13, f32[12,128,128]{2,1,0:T(8,128)} %copy-done.4, ...), custom_call_target="tpu_custom_call" | custom-call | tf_op jit(solution)/shard_map/leaf_forward/pallas_call | solution.py:109
  40.0 3.8 %all-to-all-start.1 = ((f32[16,16,8,128]{3,2,1,0:T(8,128)}), f32[16,16,8,128]{3,2,1,0:T(8,128)S(1)}, u32[]{:S(2)}, u32[]{:S(2)}) async-start(f32[16,16,8,128]{3,2,1,0:T(8,128)} %get-tuple-element.21), calls=%async_computation.1 | async-start | bytes 2097152 | tf_op jit(solution)/shard_map/all_to_all | solution.py:338
  43.8 4.4 %collective-permute-start.1 = (f32[12,128,128]{2,1,0:T(8,128)S(1)}, f32[12,128,128]{2,1,0:T(8,128)S(1)}, u32[]{:S(2)}, u32[]{:S(2)}) collective-permute-start(f32[12,128,128]{2,1,0:T(8,128)S(1)} %bitcast.15), channel_id=1, source_target_pairs={{0,24},{8,0},{16,8},{24,16},{1,25},{9,1},{17,9},{25,17},{2,26},{10... | collective-permute-start | bytes 2359304 | tf_op jit(solution)/shard_map/ppermute | solution.py:310
  48.2 1.9 %collective-permute-start.2 = (f32[12,128,128]{2,1,0:T(8,128)S(1)}, f32[12,128,128]{2,1,0:T(8,128)}, u32[]{:S(2)}, u32[]{:S(2)}) collective-permute-start(f32[12,128,128]{2,1,0:T(8,128)S(1)} %bitcast.16), channel_id=1, source_target_pairs={{0,8},{8,16},{16,24},{24,0},{1,9},{9,17},{17,25},{25,1},{2,10},{10... | collective-permute-start | bytes 2359304 | tf_op jit(solution)/shard_map/ppermute | solution.py:310
  50.2 2.4 %halves.1 = (bf16[12,256,128]{2,1,0:T(8,128)(2,1)}, bf16[12,256,128]{2,1,0:T(8,128)(2,1)}) custom-call(f32[12,128,128]{2,1,0:T(8,128)} %bitcast.14, f32[12,128,128]{2,1,0:T(8,128)} %copy-done.4), custom_call_target="tpu_custom_call" | custom-call | tf_op jit(solution)/shard_map/halves/pallas_call | solution.py:187
  52.6 7.3 %all-to-all-done.1 = f32[16,16,8,128]{3,2,1,0:T(8,128)S(1)} async-done(((f32[16,16,8,128]{3,2,1,0:T(8,128)}), f32[16,16,8,128]{3,2,1,0:T(8,128)S(1)}, u32[]{:S(2)}, u32[]{:S(2)}) %all-to-all-start.1) | async-done | bytes 1048608 | tf_op jit(solution)/shard_map/all_to_all | solution.py:338
  60.5 8.3 %all_to_all.30 = f32[16,8,128]{2,1,0:T(8,128)S(1)} all-to-all(f32[16,8,128]{2,1,0:T(8,128)} %reduce_sum.27), channel_id=1, replica_groups=mesh['rhi'=4,'rlo'=4,'y'=4,'core'=2,'layers'=4] {'rlo'}, dimensions={0} | all-to-all | bytes 131072 | tf_op jit(solution)/shard_map/all_to_all | solution.py:342
  68.9 2.0 %collective-permute-start.4 = (f32[12,128,128]{2,1,0:T(8,128)S(1)}, f32[12,128,128]{2,1,0:T(8,128)S(1)}, u32[]{:S(2)}, u32[]{:S(2)}) collective-permute-start(f32[12,128,128]{2,1,0:T(8,128)S(1)} %bitcast.17), channel_id=1, source_target_pairs={{0,16},{8,24},{16,0},{24,8},{1,17},{9,25},{17,1},{25,9},{2,18},{10... | collective-permute-start | bytes 2359304 | tf_op jit(solution)/shard_map/ppermute | solution.py:310
  70.9 23.3 %all_to_all.31 = f32[4,4,8,128]{3,2,1,0:T(8,128)S(1)} all-to-all(f32[4,4,8,128]{3,2,1,0:T(8,128)S(1)} %broadcast_in_dim.6), channel_id=1, replica_groups=mesh['rhi'=4,'rlo'=4,'y'=4,'core'=2,'layers'=4] {'rhi'}, dimensions={0} | all-to-all | bytes 131072 | tf_op jit(solution)/shard_map/all_to_all | solution.py:301
  95.0 5.1 %all-to-all-start.4 = ((f32[16,4,8,128]{3,2,1,0:T(8,128)}), f32[16,4,8,128]{3,2,1,0:T(8,128)S(1)}, u32[]{:S(2)}, u32[]{:S(2)}) async-start(f32[16,4,8,128]{3,2,1,0:T(8,128)} %broadcast_in_dim.7), calls=%async_computation.4 | async-start | bytes 524288 | tf_op jit(solution)/shard_map/all_to_all | solution.py:301
  100.2 6.6 %collective-permute-start.3 = (f32[12,128,128]{2,1,0:T(8,128)S(1)}, f32[12,128,128]{2,1,0:T(8,128)S(1)}, u32[]{:S(2)}, u32[]{:S(2)}) collective-permute-start(f32[12,128,128]{2,1,0:T(8,128)S(1)} %collective-permute-done.1.refs_2_), channel_id=1, source_target_pairs={{0,4},{4,0},{1,5},{5,1},{2,6},{6,2},{3,7},{7,3},{8,12},{12,8},{9,1... | collective-permute-start | bytes 2359304 | tf_op jit(solution)/shard_map/ppermute | solution.py:305
  106.8 1.9 %collective-permute-start.6 = (f32[12,128,128]{2,1,0:T(8,128)}, f32[12,128,128]{2,1,0:T(8,128)}, u32[]{:S(2)}, u32[]{:S(2)}) collective-permute-start(f32[12,128,128]{2,1,0:T(8,128)} %collective-permute-done.2.refs_6_), channel_id=1, source_target_pairs={{0,4},{4,0},{1,5},{5,1},{2,6},{6,2},{3,7},{7,3},{8,12},{12,8},{9,1... | collective-permute-start | bytes 2359304 | tf_op jit(solution)/shard_map/ppermute | solution.py:305
  108.8 2.4 %collective-permute-start.5 = (f32[12,128,128]{2,1,0:T(8,128)S(1)}, f32[12,128,128]{2,1,0:T(8,128)S(1)}, u32[]{:S(2)}, u32[]{:S(2)}) collective-permute-start(f32[12,128,128]{2,1,0:T(8,128)S(1)} %collective-permute-done.4.refs_4_), channel_id=1, source_target_pairs={{0,4},{4,0},{1,5},{5,1},{2,6},{6,2},{3,7},{7,3},{8,12},{12,8},{9,1... | collective-permute-start | bytes 2359304 | tf_op jit(solution)/shard_map/ppermute | solution.py:305
  111.9 5.3 %top_chain.1.tops_ref = f32[16,32,128]{2,1,0:T(8,128)} custom-call(f32[4,4,4,8,128]{4,3,2,1,0:T(8,128)} %bitcast.19, f32[16,2,128,128]{3,2,1,0:T(8,128)} %bitcast.18), custom_call_target="tpu_custom_call" | custom-call | tf_op jit(solution)/shard_map/top_chain/pallas_call | solution.py:169
  117.3 0.8 copy-done.8
  118.4 6.9 %leaf_backward.1 = f32[8,80,128]{2,1,0:T(8,128)} custom-call(s32[4]{0:T(128)} %pad_add_fusion.place_ref, s32[8,12]{1,0:T(8,128)} %fusion.targets_ref, f32[16,32,128]{2,1,0:T(8,128)} %top_chain.1.tops_ref, bf16[12,256,128]{2,1,0:T(8,128)(2,1)} %get-tuple-element.30.refs_0_, bf16[12,256,128]{2,1,0:T(8,128)(2,1)} %get-tuple-element.31.refs_1_, ...), custom_call_target="tpu_custom_call" | custom-call | tf_op jit(solution)/shard_map/leaf_backward/pallas_call | solution.py:246
  125.3 15.2 %all_to_all.32.got_ref = f32[8,80,128]{2,1,0:T(8,128)} all-to-all(f32[8,80,128]{2,1,0:T(8,128)} %leaf_backward.1), channel_id=1, replica_groups=mesh['rhi'=4,'rlo'=4,'y'=4,'core'=2,'layers'=4] {'y','core'}, dimensions={0} | all-to-all | bytes 655360 | tf_op jit(solution)/shard_map/all_to_all | solution.py:356
  140.5 1.9 %arrange.1 = (f32[12,16,256]{2,1,0:T(8,128)}, f32[1,128,256]{2,1,0:T(8,128)}) custom-call(f32[8,80,128]{2,1,0:T(8,128)} %all_to_all.32.got_ref), custom_call_target="tpu_custom_call" | custom-call | tf_op jit(solution)/shard_map/arrange/pallas_call | solution.py:289
  (37 shorter events, 4.0 us)
Async XLA Ops:
  7.2 14.5 %copy-start = (f32[1,128,256]{2,1,0:T(8,128)S(1)}, f32[1,128,256]{2,1,0:T(8,128)}, u32[]{:S(2)}) copy-start(f32[1,128,256]{2,1,0:T(8,128)} %param.11) | copy-start | bytes 393220
  7.2 104.0 %all-gather.3.cloned.1.call-start = ((), (), s32[]{:S(2)}) async-start(), calls=%async_computation.6 | async-start | bytes 2228224 | tf_op jit(solution)/shard_map/all_gather | solution.py:327
  9.3 23.4 %all-to-all-start = ((f32[8,13,16,128]{3,2,1,0:T(8,128)}), f32[8,13,16,128]{3,2,1,0:T(8,128)S(1)}, u32[]{:S(2)}, u32[]{:S(2)}) async-start(f32[8,13,16,128]{3,2,1,0:T(8,128)} %get-tuple-element.19), calls=%async_computation | async-start | bytes 1703936 | tf_op jit(solution)/shard_map/all_to_all | solution.py:326
  19.6 13.9 %collective-permute-start = (f32[12,128,128]{2,1,0:T(8,128)}, f32[12,128,128]{2,1,0:T(8,128)S(1)}, u32[]{:S(2)}, u32[]{:S(2)}) collective-permute-start(f32[12,128,128]{2,1,0:T(8,128)} %bitcast.12), channel_id=1, source_target_pairs={{0,4},{4,0},{1,5},{5,1},{2,6},{6,2},{3,7},{7,3},{8,12},{12,8},{9,1... | collective-permute-start | bytes 2359304 | tf_op jit(solution)/shard_map/ppermute | solution.py:305
  32.6 0.9 copy-start.1
  33.5 0.9 copy-start.4
  34.4 9.4 %copy-start.2 = (f32[12,1,128,128]{3,2,1,0:T(8,128)S(1)}, f32[12,1,128,128]{3,2,1,0:T(8,128)}, u32[]{:S(2)}) copy-start(f32[12,1,128,128]{3,2,1,0:T(8,128)} %param.9) | copy-start | bytes 2359300
  40.0 28.9 %copy-start.3 = (f32[12,1,128,128]{3,2,1,0:T(8,128)S(1)}, f32[12,1,128,128]{3,2,1,0:T(8,128)}, u32[]{:S(2)}) copy-start(f32[12,1,128,128]{3,2,1,0:T(8,128)} %param.9) | copy-start | bytes 2359300
  40.0 19.8 %all-to-all-start.1 = ((f32[16,16,8,128]{3,2,1,0:T(8,128)}), f32[16,16,8,128]{3,2,1,0:T(8,128)S(1)}, u32[]{:S(2)}, u32[]{:S(2)}) async-start(f32[16,16,8,128]{3,2,1,0:T(8,128)} %get-tuple-element.21), calls=%async_computation.1 | async-start | bytes 2097152 | tf_op jit(solution)/shard_map/all_to_all | solution.py:338
  43.8 50.4 %collective-permute-start.1 = (f32[12,128,128]{2,1,0:T(8,128)S(1)}, f32[12,128,128]{2,1,0:T(8,128)S(1)}, u32[]{:S(2)}, u32[]{:S(2)}) collective-permute-start(f32[12,128,128]{2,1,0:T(8,128)S(1)} %bitcast.15), channel_id=1, source_target_pairs={{0,24},{8,0},{16,8},{24,16},{1,25},{9,1},{17,9},{25,17},{2,26},{10... | collective-permute-start | bytes 2359304 | tf_op jit(solution)/shard_map/ppermute | solution.py:310
  48.2 46.0 %collective-permute-start.2 = (f32[12,128,128]{2,1,0:T(8,128)S(1)}, f32[12,128,128]{2,1,0:T(8,128)}, u32[]{:S(2)}, u32[]{:S(2)}) collective-permute-start(f32[12,128,128]{2,1,0:T(8,128)S(1)} %bitcast.16), channel_id=1, source_target_pairs={{0,8},{8,16},{16,24},{24,0},{1,9},{9,17},{17,25},{25,1},{2,10},{10... | collective-permute-start | bytes 2359304 | tf_op jit(solution)/shard_map/ppermute | solution.py:310
  68.9 39.9 %collective-permute-start.4 = (f32[12,128,128]{2,1,0:T(8,128)S(1)}, f32[12,128,128]{2,1,0:T(8,128)S(1)}, u32[]{:S(2)}, u32[]{:S(2)}) collective-permute-start(f32[12,128,128]{2,1,0:T(8,128)S(1)} %bitcast.17), channel_id=1, source_target_pairs={{0,16},{8,24},{16,0},{24,8},{1,17},{9,25},{17,1},{25,9},{2,18},{10... | collective-permute-start | bytes 2359304 | tf_op jit(solution)/shard_map/ppermute | solution.py:310
  94.2 23.1 %copy-start.6 = (f32[12,128,128]{2,1,0:T(8,128)}, f32[12,128,128]{2,1,0:T(8,128)S(1)}, u32[]{:S(2)}) copy-start(f32[12,128,128]{2,1,0:T(8,128)S(1)} %collective-permute-done.1.refs_2_) | copy-start | bytes 2359300
  95.0 16.1 %all-to-all-start.4 = ((f32[16,4,8,128]{3,2,1,0:T(8,128)}), f32[16,4,8,128]{3,2,1,0:T(8,128)S(1)}, u32[]{:S(2)}, u32[]{:S(2)}) async-start(f32[16,4,8,128]{3,2,1,0:T(8,128)} %broadcast_in_dim.7), calls=%async_computation.4 | async-start | bytes 524288 | tf_op jit(solution)/shard_map/all_to_all | solution.py:301
  100.2 17.0 %collective-permute-start.3 = (f32[12,128,128]{2,1,0:T(8,128)S(1)}, f32[12,128,128]{2,1,0:T(8,128)S(1)}, u32[]{:S(2)}, u32[]{:S(2)}) collective-permute-start(f32[12,128,128]{2,1,0:T(8,128)S(1)} %collective-permute-done.1.refs_2_), channel_id=1, source_target_pairs={{0,4},{4,0},{1,5},{5,1},{2,6},{6,2},{3,7},{7,3},{8,12},{12,8},{9,1... | collective-permute-start | bytes 2359304 | tf_op jit(solution)/shard_map/ppermute | solution.py:305
  106.8 10.4 %collective-permute-start.6 = (f32[12,128,128]{2,1,0:T(8,128)}, f32[12,128,128]{2,1,0:T(8,128)}, u32[]{:S(2)}, u32[]{:S(2)}) collective-permute-start(f32[12,128,128]{2,1,0:T(8,128)} %collective-permute-done.2.refs_6_), channel_id=1, source_target_pairs={{0,4},{4,0},{1,5},{5,1},{2,6},{6,2},{3,7},{7,3},{8,12},{12,8},{9,1... | collective-permute-start | bytes 2359304 | tf_op jit(solution)/shard_map/ppermute | solution.py:305
  108.7 8.5 %copy-start.7 = (f32[12,128,128]{2,1,0:T(8,128)}, f32[12,128,128]{2,1,0:T(8,128)S(1)}, u32[]{:S(2)}) copy-start(f32[12,128,128]{2,1,0:T(8,128)S(1)} %collective-permute-done.4.refs_4_) | copy-start | bytes 2359300
  108.8 8.5 %collective-permute-start.5 = (f32[12,128,128]{2,1,0:T(8,128)S(1)}, f32[12,128,128]{2,1,0:T(8,128)S(1)}, u32[]{:S(2)}, u32[]{:S(2)}) collective-permute-start(f32[12,128,128]{2,1,0:T(8,128)S(1)} %collective-permute-done.4.refs_4_), channel_id=1, source_target_pairs={{0,4},{4,0},{1,5},{5,1},{2,6},{6,2},{3,7},{7,3},{8,12},{12,8},{9,1... | collective-permute-start | bytes 2359304 | tf_op jit(solution)/shard_map/ppermute | solution.py:305
  111.2 0.8 copy-start.5
  117.2 0.9 copy-start.8
  117.2 1.2 copy-start.9
Sparse Core Ops, SparseCore 0:
  10.7 70.0 all-gather.2

commit v9 on v7

--- a/solution.py
+++ b/solution.py
@@ -82,11 +82,13 @@
     step = pl.program_id(0)
     count, b = mine_ref.shape[:2]
     own = own_ref.shape[1]
+    n_y = known_ref.shape[2] // own
+    layers = sums_ref.shape[0] // n_y
 
     @pl.when(step == 0)
     def _():
         sums_ref[...] = jnp.zeros_like(sums_ref)
-        sums_ref[part, row] = rhs_ref[...]
+        sums_ref[part % layers * n_y + part // layers, row] = rhs_ref[...]
 
     for i in range(count):
         inv = inv_ref[:, i].reshape(b, b)
@@ -95,7 +97,7 @@
         for k in range(2):
             t = targets_ref[2 * y + (core if k == 0 else 1 - core), step * count + i]
             for q in range(sums_ref.shape[0]):
-                sums_ref[q, t] -= update[8 * q : 8 * q + 8, k * b : (k + 1) * b]
+                sums_ref[q % layers * n_y + q // layers, t] -= update[8 * q : 8 * q + 8, k * b : (k + 1) * b]
         stage[i] = forward
         own_ref[i] = stage[i, pl.ds(pl.multiple_of(y * own, own), own), :]
 
@@ -309,7 +311,7 @@
     place = jnp.stack([core, y, part, row])
     rhs_t = lax.dynamic_slice_in_dim(top_rhs[0], core * (r // 2) + part * 8, 8, 1).T
     sums, own_forward = leaf_forward(place, targets, rhs_t, inv, blocks, paired, known, tops)
-    partial = lax.all_to_all(sums, ("y", "layers"), 0, 0, tiled=True).sum(0)
+    partial = lax.all_to_all(sums, ("layers", "y"), 0, 0, tiled=True).sum(0)
 
     quarter = lax.all_to_all(partial, "rlo", 0, 0, tiled=True)
     quarter = quarter.reshape((lax.axis_size("rlo"), -1) + quarter.shape[1:]).sum(0)

time: 149 us -> 148 us (level)
  no operation moved by 1% of the time
where the time goes in v9:
time: 148 us
  blocking collectives  46.1 us (31%)
  starting transfers between devices  40.9 us (28%)
  Pallas kernels  21.8 us (15%)
  waiting for transfers between devices  19 us (13%)
  between operations  14.3 us (10%)
  local copies, waits for them, and re-layouts  4.09 us (3%)
  other arithmetic  1.5 us (1%)
    all_to_all x1, blocking collectives, spread(): lax.all_to_all(jnp.broadcast_to(x, (n,) + x.shape), axis, 0, 0, tiled=True)  23.8 us
    all_to_all x1, blocking collectives, on_device(): got = lax.all_to_all(turned, COLS, 0, 0, tiled=True)  15.2 us
    ppermute x4, starting transfers between devices, from_core(): return lax.ppermute(x, 'core', [(0, 1), (1, 0)])  13.2 us
    all_to_all x1, starting transfers between devices, on_device(): inv = lax.all_to_all(packed, COLS, 0, 0, tiled=True)  10.3 us
    all_to_all x1, waiting for transfers between devices, on_device(): inv = lax.all_to_all(packed, COLS, 0, 0, tiled=True)  9.66 us
    ppermute x3, starting transfers between devices, from_y(): return lax.ppermute(x, 'y', [(i, (i - step) % n) for i in range(n)])  9.46 us
    all_to_all x1, waiting for transfers between devices, on_device(): partial = lax.all_to_all(sums, ('layers', 'y'), 0, 0, tiled=True).sum(0)  9.31 us
    all_to_all x1, blocking collectives, on_device(): quarter = lax.all_to_all(partial, 'rlo', 0, 0, tiled=True)  7.07 us
  transfers between devices with their start and end apart: 11, of which 2 were waited for; matrix products, arithmetic and copies ran while one was open for 2% of the time, Pallas kernels for 7%

profile of v9, /device:TPU:1, one launch (start us, length us, event | category | flops | bytes accessed | tf_op | source)
XLA Modules:
  0.0 147.7 jit_solution(5929996391579406627)
XLA Ops:
  7.2 2.0 %prepare.1 = (f32[8,13,16,128]{3,2,1,0:T(8,128)}, f32[2,128,128]{2,1,0:T(8,128)}) custom-call(s32[12]{0:T(128)} %bitcast.22, f32[12,16,128]{2,1,0:T(8,128)} %pivot_ref.1, f32[1,128,128]{2,1,0:T(8,128)} %inv_ref.1, f32[1,128,128]{2,1,0:T(8,128)} %sub_ref.1), custom_call_target="tpu_custom_call" | custom-call | tf_op jit(solution)/shard_map/prepare/pallas_call | solution.py:68
  9.3 10.3 %all-to-all-start = ((f32[8,13,16,128]{3,2,1,0:T(8,128)}), f32[8,13,16,128]{3,2,1,0:T(8,128)S(1)}, u32[]{:S(2)}, u32[]{:S(2)}) async-start(f32[8,13,16,128]{3,2,1,0:T(8,128)} %get-tuple-element.11), calls=%async_computation | async-start | bytes 1703936 | tf_op jit(solution)/shard_map/all_to_all | solution.py:304
  19.6 2.0 %collective-permute-start = (f32[12,128,128]{2,1,0:T(8,128)}, f32[12,128,128]{2,1,0:T(8,128)S(1)}, u32[]{:S(2)}, u32[]{:S(2)}) collective-permute-start(f32[12,128,128]{2,1,0:T(8,128)} %bitcast.12), channel_id=1, source_target_pairs={{0,4},{4,0},{1,5},{5,1},{2,6},{6,2},{3,7},{7,3},{8,12},{12,8},{9,1... | collective-permute-start | bytes 2359304 | tf_op jit(solution)/shard_map/ppermute | solution.py:283
  23.0 9.7 %all-to-all-done.inv_ref.refs_9_ = f32[8,13,16,128]{3,2,1,0:T(8,128)S(1)} async-done(((f32[8,13,16,128]{3,2,1,0:T(8,128)}), f32[8,13,16,128]{3,2,1,0:T(8,128)S(1)}, u32[]{:S(2)}, u32[]{:S(2)}) %all-to-all-start) | async-done | bytes 852000 | tf_op jit(solution)/shard_map/all_to_all | solution.py:304
  32.6 0.9 fusion.targets_ref
  33.5 0.9 copy-done.3
  34.4 5.6 %leaf_forward.1 = (f32[16,16,8,128]{3,2,1,0:T(8,128)}, f32[12,32,128]{2,1,0:T(8,128)}) custom-call(s32[4]{0:T(128)} %pad_add_fusion.place_ref, s32[8,12]{1,0:T(8,128)} %fusion.targets_ref, f32[8,128]{1,0:T(8,128)} %bitcast.21, f32[8,13,16,128]{3,2,1,0:T(8,128)} %copy-done.1, f32[12,128,128]{2,1,0:T(8,128)} %bitcast.13, f32[12,128,128]{2,1,0:T(8,128)} %copy-done.3, ...), custom_call_target="tpu_custom_call" | custom-call | tf_op jit(solution)/shard_map/leaf_forward/pallas_call | solution.py:111
  39.9 3.7 %all-to-all-start.1 = ((f32[16,16,8,128]{3,2,1,0:T(8,128)}), f32[16,16,8,128]{3,2,1,0:T(8,128)S(1)}, u32[]{:S(2)}, u32[]{:S(2)}) async-start(f32[16,16,8,128]{3,2,1,0:T(8,128)} %get-tuple-element.12), calls=%async_computation.1 | async-start | bytes 2097152 | tf_op jit(solution)/shard_map/all_to_all | solution.py:314
  43.6 4.4 %collective-permute-start.1 = (f32[12,128,128]{2,1,0:T(8,128)S(1)}, f32[12,128,128]{2,1,0:T(8,128)S(1)}, u32[]{:S(2)}, u32[]{:S(2)}) collective-permute-start(f32[12,128,128]{2,1,0:T(8,128)S(1)} %bitcast.15), channel_id=1, source_target_pairs={{0,24},{8,0},{16,8},{24,16},{1,25},{9,1},{17,9},{25,17},{2,26},{10... | collective-permute-start | bytes 2359304 | tf_op jit(solution)/shard_map/ppermute | solution.py:288
  48.0 1.9 %collective-permute-start.2 = (f32[12,128,128]{2,1,0:T(8,128)S(1)}, f32[12,128,128]{2,1,0:T(8,128)}, u32[]{:S(2)}, u32[]{:S(2)}) collective-permute-start(f32[12,128,128]{2,1,0:T(8,128)S(1)} %bitcast.16), channel_id=1, source_target_pairs={{0,8},{8,16},{16,24},{24,0},{1,9},{9,17},{17,25},{25,1},{2,10},{10... | collective-permute-start | bytes 2359304 | tf_op jit(solution)/shard_map/ppermute | solution.py:288
  49.9 9.3 %all-to-all-done.1 = f32[16,16,8,128]{3,2,1,0:T(8,128)S(1)} async-done(((f32[16,16,8,128]{3,2,1,0:T(8,128)}), f32[16,16,8,128]{3,2,1,0:T(8,128)S(1)}, u32[]{:S(2)}, u32[]{:S(2)}) %all-to-all-start.1) | async-done | bytes 1048608 | tf_op jit(solution)/shard_map/all_to_all | solution.py:314
  59.3 7.1 %all_to_all.30 = f32[16,8,128]{2,1,0:T(8,128)S(1)} all-to-all(f32[16,8,128]{2,1,0:T(8,128)S(1)} %reduce_sum.27), channel_id=1, replica_groups=mesh['rhi'=4,'rlo'=4,'y'=4,'core'=2,'layers'=4] {'rlo'}, dimensions={0} | all-to-all | bytes 131072 | tf_op jit(solution)/shard_map/all_to_all | solution.py:316
  66.4 3.2 %collective-permute-start.4 = (f32[12,128,128]{2,1,0:T(8,128)S(1)}, f32[12,128,128]{2,1,0:T(8,128)S(1)}, u32[]{:S(2)}, u32[]{:S(2)}) collective-permute-start(f32[12,128,128]{2,1,0:T(8,128)S(1)} %bitcast.17), channel_id=1, source_target_pairs={{0,16},{8,24},{16,0},{24,8},{1,17},{9,25},{17,1},{25,9},{2,18},{10... | collective-permute-start | bytes 2359304 | tf_op jit(solution)/shard_map/ppermute | solution.py:288
  69.6 23.8 %all_to_all.31 = f32[4,4,8,128]{3,2,1,0:T(8,128)S(1)} all-to-all(f32[4,4,8,128]{3,2,1,0:T(8,128)S(1)} %broadcast_in_dim.6), channel_id=1, replica_groups=mesh['rhi'=4,'rlo'=4,'y'=4,'core'=2,'layers'=4] {'rhi'}, dimensions={0} | all-to-all | bytes 131072 | tf_op jit(solution)/shard_map/all_to_all | solution.py:279
  93.4 0.9 broadcast_in_dim.7
  94.3 4.1 %all-to-all-start.4 = ((f32[16,4,8,128]{3,2,1,0:T(8,128)}), f32[16,4,8,128]{3,2,1,0:T(8,128)S(1)}, u32[]{:S(2)}, u32[]{:S(2)}) async-start(f32[16,4,8,128]{3,2,1,0:T(8,128)} %broadcast_in_dim.7), calls=%async_computation.4 | async-start | bytes 524288 | tf_op jit(solution)/shard_map/all_to_all | solution.py:279
  98.4 6.9 %collective-permute-start.3 = (f32[12,128,128]{2,1,0:T(8,128)S(1)}, f32[12,128,128]{2,1,0:T(8,128)}, u32[]{:S(2)}, u32[]{:S(2)}) collective-permute-start(f32[12,128,128]{2,1,0:T(8,128)S(1)} %collective-permute-done.1.refs_2_), channel_id=1, source_target_pairs={{0,4},{4,0},{1,5},{5,1},{2,6},{6,2},{3,7},{7,3},{8,12},{12,8},{9,1... | collective-permute-start | bytes 2359304 | tf_op jit(solution)/shard_map/ppermute | solution.py:283
  105.3 1.9 %collective-permute-start.6 = (f32[12,128,128]{2,1,0:T(8,128)}, f32[12,128,128]{2,1,0:T(8,128)}, u32[]{:S(2)}, u32[]{:S(2)}) collective-permute-start(f32[12,128,128]{2,1,0:T(8,128)} %collective-permute-done.2.refs_6_), channel_id=1, source_target_pairs={{0,4},{4,0},{1,5},{5,1},{2,6},{6,2},{3,7},{7,3},{8,12},{12,8},{9,1... | collective-permute-start | bytes 2359304 | tf_op jit(solution)/shard_map/ppermute | solution.py:283
  107.3 2.4 %collective-permute-start.5 = (f32[12,128,128]{2,1,0:T(8,128)S(1)}, f32[12,128,128]{2,1,0:T(8,128)S(1)}, u32[]{:S(2)}, u32[]{:S(2)}) collective-permute-start(f32[12,128,128]{2,1,0:T(8,128)S(1)} %collective-permute-done.4.refs_4_), channel_id=1, source_target_pairs={{0,4},{4,0},{1,5},{5,1},{2,6},{6,2},{3,7},{7,3},{8,12},{12,8},{9,1... | collective-permute-start | bytes 2359304 | tf_op jit(solution)/shard_map/ppermute | solution.py:283
  110.4 5.3 %top_chain.1.tops_ref = f32[16,32,128]{2,1,0:T(8,128)} custom-call(f32[4,4,4,8,128]{4,3,2,1,0:T(8,128)} %bitcast.19, f32[16,2,128,128]{3,2,1,0:T(8,128)} %bitcast.18), custom_call_target="tpu_custom_call" | custom-call | tf_op jit(solution)/shard_map/top_chain/pallas_call | solution.py:171
  115.8 0.9 copy-done.7
  116.7 7.0 %leaf_backward.1 = f32[8,80,128]{2,1,0:T(8,128)} custom-call(s32[4]{0:T(128)} %pad_add_fusion.place_ref, s32[8,12]{1,0:T(8,128)} %fusion.targets_ref, f32[16,32,128]{2,1,0:T(8,128)} %top_chain.1.tops_ref, f32[12,128,128]{2,1,0:T(8,128)} %bitcast.14, f32[12,128,128]{2,1,0:T(8,128)} %copy-done.3, f32[12,128,128]{2,1,0:T(8,128)} %copy-done.5, ...), custom_call_target="tpu_custom_call" | custom-call | tf_op jit(solution)/shard_map/leaf_backward/pallas_call | solution.py:225
  123.7 15.2 %all_to_all.32.got_ref = f32[8,80,128]{2,1,0:T(8,128)} all-to-all(f32[8,80,128]{2,1,0:T(8,128)} %leaf_backward.1), channel_id=1, replica_groups=mesh['rhi'=4,'rlo'=4,'y'=4,'core'=2,'layers'=4] {'y','core'}, dimensions={0} | all-to-all | bytes 655360 | tf_op jit(solution)/shard_map/all_to_all | solution.py:330
  138.9 1.9 %arrange.1 = (f32[12,16,256]{2,1,0:T(8,128)}, f32[1,128,256]{2,1,0:T(8,128)}) custom-call(f32[8,80,128]{2,1,0:T(8,128)} %all_to_all.32.got_ref), custom_call_target="tpu_custom_call" | custom-call | tf_op jit(solution)/shard_map/arrange/pallas_call | solution.py:267
  (32 shorter events, 2.2 us)
Async XLA Ops:
  7.2 14.5 %copy-start = (f32[1,128,256]{2,1,0:T(8,128)S(1)}, f32[1,128,256]{2,1,0:T(8,128)}, u32[]{:S(2)}) copy-start(f32[1,128,256]{2,1,0:T(8,128)} %param.11) | copy-start | bytes 393220
  7.2 102.6 %all-gather.3.cloned.1.call-start = ((), (), s32[]{:S(2)}) async-start(), calls=%async_computation.6 | async-start | bytes 2228224 | tf_op jit(solution)/shard_map/all_gather | solution.py:305
  9.3 23.4 %all-to-all-start = ((f32[8,13,16,128]{3,2,1,0:T(8,128)}), f32[8,13,16,128]{3,2,1,0:T(8,128)S(1)}, u32[]{:S(2)}, u32[]{:S(2)}) async-start(f32[8,13,16,128]{3,2,1,0:T(8,128)} %get-tuple-element.11), calls=%async_computation | async-start | bytes 1703936 | tf_op jit(solution)/shard_map/all_to_all | solution.py:304
  19.6 13.9 %collective-permute-start = (f32[12,128,128]{2,1,0:T(8,128)}, f32[12,128,128]{2,1,0:T(8,128)S(1)}, u32[]{:S(2)}, u32[]{:S(2)}) collective-permute-start(f32[12,128,128]{2,1,0:T(8,128)} %bitcast.12), channel_id=1, source_target_pairs={{0,4},{4,0},{1,5},{5,1},{2,6},{6,2},{3,7},{7,3},{8,12},{12,8},{9,1... | collective-permute-start | bytes 2359304 | tf_op jit(solution)/shard_map/ppermute | solution.py:283
  32.6 0.9 copy-start.1
  33.5 0.9 copy-start.3
  34.4 9.2 %copy-start.2 = (f32[12,1,128,128]{3,2,1,0:T(8,128)S(1)}, f32[12,1,128,128]{3,2,1,0:T(8,128)}, u32[]{:S(2)}) copy-start(f32[12,1,128,128]{3,2,1,0:T(8,128)} %param.9) | copy-start | bytes 2359300
  39.9 19.3 %all-to-all-start.1 = ((f32[16,16,8,128]{3,2,1,0:T(8,128)}), f32[16,16,8,128]{3,2,1,0:T(8,128)S(1)}, u32[]{:S(2)}, u32[]{:S(2)}) async-start(f32[16,16,8,128]{3,2,1,0:T(8,128)} %get-tuple-element.12), calls=%async_computation.1 | async-start | bytes 2097152 | tf_op jit(solution)/shard_map/all_to_all | solution.py:314
  43.6 49.8 %collective-permute-start.1 = (f32[12,128,128]{2,1,0:T(8,128)S(1)}, f32[12,128,128]{2,1,0:T(8,128)S(1)}, u32[]{:S(2)}, u32[]{:S(2)}) collective-permute-start(f32[12,128,128]{2,1,0:T(8,128)S(1)} %bitcast.15), channel_id=1, source_target_pairs={{0,24},{8,0},{16,8},{24,16},{1,25},{9,1},{17,9},{25,17},{2,26},{10... | collective-permute-start | bytes 2359304 | tf_op jit(solution)/shard_map/ppermute | solution.py:288
  48.0 45.4 %collective-permute-start.2 = (f32[12,128,128]{2,1,0:T(8,128)S(1)}, f32[12,128,128]{2,1,0:T(8,128)}, u32[]{:S(2)}, u32[]{:S(2)}) collective-permute-start(f32[12,128,128]{2,1,0:T(8,128)S(1)} %bitcast.16), channel_id=1, source_target_pairs={{0,8},{8,16},{16,24},{24,0},{1,9},{9,17},{17,25},{25,1},{2,10},{10... | collective-permute-start | bytes 2359304 | tf_op jit(solution)/shard_map/ppermute | solution.py:288
  66.4 40.9 %collective-permute-start.4 = (f32[12,128,128]{2,1,0:T(8,128)S(1)}, f32[12,128,128]{2,1,0:T(8,128)S(1)}, u32[]{:S(2)}, u32[]{:S(2)}) collective-permute-start(f32[12,128,128]{2,1,0:T(8,128)S(1)} %bitcast.17), channel_id=1, source_target_pairs={{0,16},{8,24},{16,0},{24,8},{1,17},{9,25},{17,1},{25,9},{2,18},{10... | collective-permute-start | bytes 2359304 | tf_op jit(solution)/shard_map/ppermute | solution.py:288
  93.4 22.4 %copy-start.5 = (f32[12,128,128]{2,1,0:T(8,128)}, f32[12,128,128]{2,1,0:T(8,128)S(1)}, u32[]{:S(2)}) copy-start(f32[12,128,128]{2,1,0:T(8,128)S(1)} %collective-permute-done.1.refs_2_) | copy-start | bytes 2359300
  94.3 15.4 %all-to-all-start.4 = ((f32[16,4,8,128]{3,2,1,0:T(8,128)}), f32[16,4,8,128]{3,2,1,0:T(8,128)S(1)}, u32[]{:S(2)}, u32[]{:S(2)}) async-start(f32[16,4,8,128]{3,2,1,0:T(8,128)} %broadcast_in_dim.7), calls=%async_computation.4 | async-start | bytes 524288 | tf_op jit(solution)/shard_map/all_to_all | solution.py:279
  98.4 17.3 %collective-permute-start.3 = (f32[12,128,128]{2,1,0:T(8,128)S(1)}, f32[12,128,128]{2,1,0:T(8,128)}, u32[]{:S(2)}, u32[]{:S(2)}) collective-permute-start(f32[12,128,128]{2,1,0:T(8,128)S(1)} %collective-permute-done.1.refs_2_), channel_id=1, source_target_pairs={{0,4},{4,0},{1,5},{5,1},{2,6},{6,2},{3,7},{7,3},{8,12},{12,8},{9,1... | collective-permute-start | bytes 2359304 | tf_op jit(solution)/shard_map/ppermute | solution.py:283
  105.3 10.4 %collective-permute-start.6 = (f32[12,128,128]{2,1,0:T(8,128)}, f32[12,128,128]{2,1,0:T(8,128)}, u32[]{:S(2)}, u32[]{:S(2)}) collective-permute-start(f32[12,128,128]{2,1,0:T(8,128)} %collective-permute-done.2.refs_6_), channel_id=1, source_target_pairs={{0,4},{4,0},{1,5},{5,1},{2,6},{6,2},{3,7},{7,3},{8,12},{12,8},{9,1... | collective-permute-start | bytes 2359304 | tf_op jit(solution)/shard_map/ppermute | solution.py:283
  107.3 8.5 %copy-start.6 = (f32[12,128,128]{2,1,0:T(8,128)}, f32[12,128,128]{2,1,0:T(8,128)S(1)}, u32[]{:S(2)}) copy-start(f32[12,128,128]{2,1,0:T(8,128)S(1)} %collective-permute-done.4.refs_4_) | copy-start | bytes 2359300
  107.3 8.5 %collective-permute-start.5 = (f32[12,128,128]{2,1,0:T(8,128)S(1)}, f32[12,128,128]{2,1,0:T(8,128)S(1)}, u32[]{:S(2)}, u32[]{:S(2)}) collective-permute-start(f32[12,128,128]{2,1,0:T(8,128)S(1)} %collective-permute-done.4.refs_4_), channel_id=1, source_target_pairs={{0,4},{4,0},{1,5},{5,1},{2,6},{6,2},{3,7},{7,3},{8,12},{12,8},{9,1... | collective-permute-start | bytes 2359304 | tf_op jit(solution)/shard_map/ppermute | solution.py:283
  109.7 0.7 copy-start.4
  115.8 0.9 copy-start.7
Sparse Core Ops, SparseCore 0:
  10.7 70.3 all-gather.2
